TPU v7x, 32 devices: a whole 2x2x4 slice. The times are simulated.
32 devices in a mesh: dp: 8 (over z, x), tensor: 4 (over y, core).
Axes of the slice: x: 2, y: 2, z: 4, core: 2. Of those that a mesh axis runs over, the one named last changes fastest.
Arguments:
- tokens: bfloat16 [2560, 2048], P(('dp', 'tensor')), may hold values from -6 to 6
- segment_ids: int32 [2560], replicated, may hold values from 0 to 39, as said below
- key_mask: int32 [2560], replicated, may hold values 0 or 1
- attn_gain: float32 [2048], P(('dp', 'tensor')), may hold values from 0.1 to 1.9
- w_query: bfloat16 [2048, 2048], P('dp', 'tensor'), may hold values from -0.125 to 0.125
- w_key: bfloat16 [2048, 256], P('dp', 'tensor'), may hold values from -0.125 to 0.125
- w_value: bfloat16 [2048, 256], P('dp', 'tensor'), may hold values from -0.125 to 0.125
- w_out: bfloat16 [2048, 2048], P('tensor', 'dp'), may hold values from -0.75 to 0.75
- mlp_gain: float32 [2048], P(('dp', 'tensor')), may hold values from 0.1 to 1.9
- w_gate: bfloat16 [2048, 5632], P('dp', 'tensor'), may hold values from -0.125 to 0.125
- w_up: bfloat16 [2048, 5632], P('dp', 'tensor'), may hold values from -0.125 to 0.125
- w_down: bfloat16 [5632, 2048], P('tensor', 'dp'), may hold values from -0.078125 to 0.078125
- cotangent: bfloat16 [2560, 2048], P(('dp', 'tensor')), may hold values from -6 to 6
Outputs:
- layer_out: bfloat16 [2560, 2048], P(('dp', 'tensor'))
- input_grad: float32 [2560, 2048], P(('dp', 'tensor'))
- grad_attn_gain: float32 [2048], P(('dp', 'tensor'))
- grad_query: float32 [2048, 2048], P('dp', 'tensor')
- grad_key: float32 [2048, 256], P('dp', 'tensor')
- grad_value: float32 [2048, 256], P('dp', 'tensor')
- grad_out: float32 [2048, 2048], P('tensor', 'dp')
- grad_mlp_gain: float32 [2048], P(('dp', 'tensor'))
- grad_gate: float32 [2048, 5632], P('dp', 'tensor')
- grad_up: float32 [2048, 5632], P('dp', 'tensor')
- grad_down: float32 [5632, 2048], P('tensor', 'dp')
Inputs may be any that keep to these rules, and one draw needn't show every extreme that they name: `segment_ids`: segment ids never fall from one token to the next; equal ids form one document; documents start only at positions that are multiples of 16, and there are exactly 40 of them; one document holds exactly 1600 tokens and starts at 0 or at a position of at most 64.
All inputs are finite; a program needn't handle non-finite values.
Results may differ from a plain program's by a relative error of at most 0.019.
Values may be sent and summed in bfloat16 or wider, within the bound.
A program may use at most 192 MiB of HBM per device.

v0:
```python
import math

import jax
import jax.numpy as jnp
from jax import lax
from jax.sharding import PartitionSpec as P

EPS = 1e-05
NEG = -1e30
THETA = 10000.0


def normalize(values, scaling):
    return values * lax.rsqrt(jnp.mean(values * values, axis=-1, keepdims=True) + EPS) * scaling


def angles(positions, half_dim):
    frequency = THETA ** (-jnp.arange(half_dim, dtype=jnp.float32) / half_dim)
    turned = positions.astype(jnp.float32)[:, None] * frequency[None, :]
    return (jnp.cos(turned), jnp.sin(turned))


def rotate(values, cosine_table, sine_table):
    half_dim = values.shape[-1] // 2
    front_half = values[..., :half_dim]
    back_half = values[..., half_dim:]
    cosine_rows = cosine_table[:, None, :]
    sine_rows = sine_table[:, None, :]
    return jnp.concatenate(
        [
            front_half * cosine_rows - back_half * sine_rows,
            back_half * cosine_rows + front_half * sine_rows,
        ],
        axis=-1,
    )


def matmul(left_rows, right_rows):
    return jnp.dot(left_rows, right_rows, preferred_element_type=jnp.float32)


def contract_rows(left_rows, right_rows):
    return lax.dot_general(
        left_rows, right_rows, (((0,), (0,)), ((), ())), preferred_element_type=jnp.float32
    )


def contract_cols(left_rows, right_rows):
    return lax.dot_general(
        left_rows, right_rows, (((1,), (1,)), ((), ())), preferred_element_type=jnp.float32
    )


def collect_rows(local_part):
    return lax.all_gather(local_part, "tensor", axis=0, tiled=True)


def spread_rows(term_fn, row_count):
    return lax.psum_scatter(
        term_fn(jnp.int32(0), row_count * lax.axis_size("tensor")),
        "tensor",
        scatter_dimension=0,
        tiled=True,
    )


def shards(
    tokens,
    segment_ids,
    key_mask,
    attn_gain,
    w_query,
    w_key,
    w_value,
    w_out,
    mlp_gain,
    w_gate,
    w_up,
    w_down,
    cotangent,
):
    data_size = lax.axis_size("dp")
    width_size = lax.axis_size("tensor")
    row_count = tokens.shape[0]
    local_tokens = row_count * width_size
    total_tokens = local_tokens * data_size
    head_dim = w_key.shape[1]
    local_heads = w_query.shape[1] // head_dim
    query_count = local_tokens * local_heads
    score_scale = head_dim ** (-0.5)
    first_row = lax.axis_index("dp") * local_tokens
    attn_scale, mlp_scale = (
        lax.all_gather(attn_gain, ("dp", "tensor"), axis=0, tiled=True),
        lax.all_gather(mlp_gain, ("dp", "tensor"), axis=0, tiled=True),
    )
    w_query_all, w_key_all, w_value_all, w_gate_all, w_up_all, w_out_cols, w_down_cols = (
        lax.all_gather(w_query, "dp", axis=0, tiled=True),
        lax.all_gather(w_key, "dp", axis=0, tiled=True),
        lax.all_gather(w_value, "dp", axis=0, tiled=True),
        lax.all_gather(w_gate, "dp", axis=0, tiled=True),
        lax.all_gather(w_up, "dp", axis=0, tiled=True),
        lax.all_gather(w_out.T, "dp", axis=0, tiled=True),
        lax.all_gather(w_down.T, "dp", axis=0, tiled=True),
    )
    positions = first_row + jnp.arange(local_tokens, dtype=jnp.int32)
    cosine_table, sine_table = angles(positions, head_dim // 2)
    own_segments = lax.dynamic_slice(segment_ids, (first_row,), (local_tokens,))
    query_segment = jnp.repeat(own_segments, local_heads)
    query_index = jnp.repeat(positions, local_heads)
    last_index = first_row + local_tokens - 1
    low_segment = own_segments[0]
    high_segment = own_segments[local_tokens - 1]

    def turn(values):
        return rotate(values, cosine_table, sine_table)

    inputs = tokens.astype(jnp.float32)
    first_norm, first_back = jax.vjp(normalize, inputs, attn_scale)
    normed = collect_rows(first_norm.astype(jnp.bfloat16))
    query_pre = matmul(normed, w_query_all).reshape(local_tokens, local_heads, head_dim)
    key_pre = matmul(normed, w_key_all).reshape(local_tokens, 1, head_dim)
    value_rows = matmul(normed, w_value_all).astype(jnp.bfloat16)
    query_turned, query_back = jax.vjp(turn, query_pre)
    key_turned, key_back = jax.vjp(turn, key_pre)
    query_rows = query_turned.astype(jnp.bfloat16).reshape(query_count, head_dim)
    key_rows = key_turned.astype(jnp.bfloat16).reshape(local_tokens, head_dim)
    key_all, value_all = (
        lax.all_gather(key_rows, "dp", axis=0, tiled=True),
        lax.all_gather(value_rows, "dp", axis=0, tiled=True),
    )
    block_len = math.gcd(total_tokens, 1024)
    count_blocks = total_tokens // block_len
    scan_items = (
        key_all.reshape(count_blocks, block_len, head_dim),
        value_all.reshape(count_blocks, block_len, head_dim),
        segment_ids.reshape(count_blocks, block_len),
        key_mask.reshape(count_blocks, block_len),
        jnp.arange(count_blocks, dtype=jnp.int32) * block_len,
    )

    def reachable(block_segments, key_start):
        return (
            (key_start <= last_index)
            & (block_segments[0] <= high_segment)
            & (block_segments[block_len - 1] >= low_segment)
        )

    def scores_of(key_block, block_segments, block_marks, key_start):
        key_index = key_start + jnp.arange(block_len, dtype=jnp.int32)
        allowed = (
            (query_segment[:, None] == block_segments[None, :])
            & (key_index[None, :] <= query_index[:, None])
            & ((block_marks[None, :] == 1) | (key_index[None, :] == query_index[:, None]))
        )
        raw_scores = contract_cols(query_rows, key_block) * score_scale
        return (jnp.where(allowed, raw_scores, NEG), allowed)

    def stats_step(carried, operands):
        key_block, value_block, block_segments, block_marks, key_start = operands

        def stats_visit_block(running):
            row_top, row_total = running
            scores, allowed = scores_of(key_block, block_segments, block_marks, key_start)
            new_top = jnp.maximum(row_top, jnp.max(scores, axis=1))
            exps = jnp.where(allowed, jnp.exp(scores - new_top[:, None]), 0.0)
            return (new_top, row_total * jnp.exp(row_top - new_top) + jnp.sum(exps, axis=1))

        def stats_skip_block(running):
            return running

        return (
            lax.cond(
                reachable(block_segments, key_start), stats_visit_block, stats_skip_block, carried
            ),
            None,
        )

    start_stats = (
        jnp.full((query_count,), NEG, jnp.float32),
        jnp.zeros((query_count,), jnp.float32),
    )
    (row_top, row_total), unused_stats = lax.scan(stats_step, start_stats, scan_items)

    def probs_of(key_block, block_segments, block_marks, key_start):
        scores, allowed = scores_of(key_block, block_segments, block_marks, key_start)
        return jnp.where(allowed, jnp.exp(scores - row_top[:, None]), 0.0) / row_total[:, None]

    def output_step(carried, operands):
        key_block, value_block, block_segments, block_marks, key_start = operands

        def output_visit_block(running):
            probs = probs_of(key_block, block_segments, block_marks, key_start)
            return running + matmul(probs.astype(jnp.bfloat16), value_block)

        def output_skip_block(running):
            return running

        return (
            lax.cond(
                reachable(block_segments, key_start), output_visit_block, output_skip_block, carried
            ),
            None,
        )

    mixed_sum, unused_out = lax.scan(
        output_step, jnp.zeros((query_count, head_dim), jnp.float32), scan_items
    )
    mixed_low = mixed_sum.reshape(local_tokens, local_heads * head_dim).astype(jnp.bfloat16)

    def attn_term(row_start, count_rows):
        return contract_cols(mixed_low, w_out_cols)

    middle = inputs + spread_rows(attn_term, row_count)
    second_norm, second_back = jax.vjp(normalize, middle, mlp_scale)
    normed_two = collect_rows(second_norm.astype(jnp.bfloat16))
    gate_proj = matmul(normed_two, w_gate_all)
    upward = matmul(normed_two, w_up_all)

    def swish_product(gate_values, up_values):
        return jax.nn.silu(gate_values) * up_values

    hidden_f, swish_back = jax.vjp(swish_product, gate_proj, upward)
    hidden = hidden_f.astype(jnp.bfloat16)

    def mlp_term(row_start, count_rows):
        return contract_cols(hidden, w_down_cols)

    result = (middle + spread_rows(mlp_term, row_count)).astype(jnp.bfloat16)
    upstream = cotangent.astype(jnp.float32)
    down_grad = collect_rows(cotangent)
    grad_down_cols = contract_rows(down_grad, hidden)
    hidden_grad = matmul(down_grad, w_down_cols)
    gate_grad_f, up_grad_f = swish_back(hidden_grad)
    gate_grad = gate_grad_f.astype(jnp.bfloat16)
    up_grad = up_grad_f.astype(jnp.bfloat16)
    grad_gate_all = contract_rows(normed_two, gate_grad)
    grad_up_all = contract_rows(normed_two, up_grad)

    def mlp_back_term(row_start, count_rows):
        return contract_cols(gate_grad, w_gate_all) + contract_cols(up_grad, w_up_all)

    middle_part, mlp_gain_part = second_back(spread_rows(mlp_back_term, row_count))
    middle_grad = upstream + middle_part
    grad_gate, grad_up, grad_down_shard = (
        lax.psum_scatter(
            grad_gate_all.astype(jnp.bfloat16), "dp", scatter_dimension=0, tiled=True
        ).astype(jnp.float32),
        lax.psum_scatter(
            grad_up_all.astype(jnp.bfloat16), "dp", scatter_dimension=0, tiled=True
        ).astype(jnp.float32),
        lax.psum_scatter(
            grad_down_cols.astype(jnp.bfloat16), "dp", scatter_dimension=0, tiled=True
        ).astype(jnp.float32),
    )
    branch_grad = collect_rows(middle_grad.astype(jnp.bfloat16))
    grad_out_cols = contract_rows(branch_grad, mixed_low)
    mixed_grad = matmul(branch_grad, w_out_cols).astype(jnp.bfloat16).reshape(query_count, head_dim)

    def delta_step(carried, operands):
        key_block, value_block, block_segments, block_marks, key_start = operands

        def delta_visit_block(running):
            probs = probs_of(key_block, block_segments, block_marks, key_start)
            prob_grad = contract_cols(mixed_grad, value_block)
            return running + jnp.sum(probs * prob_grad, axis=1)

        def delta_skip_block(running):
            return running

        return (
            lax.cond(
                reachable(block_segments, key_start), delta_visit_block, delta_skip_block, carried
            ),
            None,
        )

    row_delta, unused_delta = lax.scan(
        delta_step, jnp.zeros((query_count,), jnp.float32), scan_items
    )

    def grads_step(carried, operands):
        key_block, value_block, block_segments, block_marks, key_start = operands

        def grads_visit_block(running):
            probs = probs_of(key_block, block_segments, block_marks, key_start)
            prob_grad = contract_cols(mixed_grad, value_block)
            score_grad = (probs * (prob_grad - row_delta[:, None])).astype(jnp.bfloat16)
            key_part = contract_rows(score_grad, query_rows) * score_scale
            value_part = contract_rows(probs.astype(jnp.bfloat16), mixed_grad)
            return (
                running + matmul(score_grad, key_block),
                jnp.concatenate([key_part, value_part], axis=1),
            )

        def grads_skip_block(running):
            return (running, jnp.zeros((block_len, 2 * head_dim), jnp.float32))

        return lax.cond(
            reachable(block_segments, key_start), grads_visit_block, grads_skip_block, carried
        )

    query_sum, key_value_blocks = lax.scan(
        grads_step, jnp.zeros((query_count, head_dim), jnp.float32), scan_items
    )
    key_value_grad = lax.psum_scatter(
        key_value_blocks.reshape(total_tokens, 2 * head_dim).astype(jnp.bfloat16),
        "dp",
        scatter_dimension=0,
        tiled=True,
    ).astype(jnp.float32)
    (query_unturned,) = query_back(
        (query_sum * score_scale).reshape(local_tokens, local_heads, head_dim)
    )
    (key_unturned,) = key_back(key_value_grad[:, :head_dim].reshape(local_tokens, 1, head_dim))
    query_grad = query_unturned.reshape(local_tokens, local_heads * head_dim).astype(jnp.bfloat16)
    key_grad = key_unturned.reshape(local_tokens, head_dim).astype(jnp.bfloat16)
    value_grad = key_value_grad[:, head_dim:].astype(jnp.bfloat16)
    grad_query_all = contract_rows(normed, query_grad)
    grad_key_all = contract_rows(normed, key_grad)
    grad_value_all = contract_rows(normed, value_grad)

    def attn_back_term(row_start, count_rows):
        return (
            contract_cols(query_grad, w_query_all)
            + contract_cols(key_grad, w_key_all)
            + contract_cols(value_grad, w_value_all)
        )

    input_part, attn_gain_part = first_back(spread_rows(attn_back_term, row_count))
    input_grad = middle_grad + input_part
    grad_query, grad_key, grad_value, grad_out_shard = (
        lax.psum_scatter(
            grad_query_all.astype(jnp.bfloat16), "dp", scatter_dimension=0, tiled=True
        ).astype(jnp.float32),
        lax.psum_scatter(
            grad_key_all.astype(jnp.bfloat16), "dp", scatter_dimension=0, tiled=True
        ).astype(jnp.float32),
        lax.psum_scatter(
            grad_value_all.astype(jnp.bfloat16), "dp", scatter_dimension=0, tiled=True
        ).astype(jnp.float32),
        lax.psum_scatter(
            grad_out_cols.astype(jnp.bfloat16), "dp", scatter_dimension=0, tiled=True
        ).astype(jnp.float32),
    )
    grad_attn_gain, grad_mlp_gain = (
        lax.psum_scatter(attn_gain_part, ("dp", "tensor"), scatter_dimension=0, tiled=True),
        lax.psum_scatter(mlp_gain_part, ("dp", "tensor"), scatter_dimension=0, tiled=True),
    )
    return (
        result,
        input_grad,
        grad_attn_gain,
        grad_query,
        grad_key,
        grad_value,
        grad_out_shard.T,
        grad_mlp_gain,
        grad_gate,
        grad_up,
        grad_down_shard.T,
    )


def solution(mesh):
    in_specs = (
        P(("dp", "tensor"), None),
        P(),
        P(),
        P(("dp", "tensor")),
        P("dp", "tensor"),
        P("dp", "tensor"),
        P("dp", "tensor"),
        P("tensor", "dp"),
        P(("dp", "tensor")),
        P("dp", "tensor"),
        P("dp", "tensor"),
        P("tensor", "dp"),
        P(("dp", "tensor"), None),
    )
    out_specs = (
        P(("dp", "tensor"), None),
        P(("dp", "tensor"), None),
        P(("dp", "tensor")),
        P("dp", "tensor"),
        P("dp", "tensor"),
        P("dp", "tensor"),
        P("tensor", "dp"),
        P(("dp", "tensor")),
        P("dp", "tensor"),
        P("dp", "tensor"),
        P("tensor", "dp"),
    )
    return jax.shard_map(shards, mesh=mesh, in_specs=in_specs, out_specs=out_specs, check_vma=False)
```

profile of v0, /device:TPU:0, one launch (start us, length us, event | category | flops | bytes accessed | tf_op | source)
XLA Modules:
  0.0 1628.6 jit_solution(679754171163037573)
XLA Ops:
  10.2 42.1 %all-reduce.9 = (f32[2048]{0:T(1024)S(1)}, f32[2048]{0:T(1024)S(1)}) all-reduce(f32[2048]{0:T(1024)S(1)} %dynamic-update-slice, f32[2048]{0:T(1024)S(1)} %dynamic-update-slice.1), channel_id=1, replica_groups=mesh['dp'=8,'tensor'=4] {'dp','tensor'}, use_global_device_ids=true, to_apply=%add.4 | all-reduce | flops 4096 | bytes 32768
  59.1 31.2 %all_gather.47 = bf16[2048,64]{0,1:T(8,128)(2,1)S(1)} all-gather(bf16[256,64]{0,1:T(8,128)(2,1)} %param.34), channel_id=1, replica_groups=mesh['dp'=8,'tensor'=4] {'dp'}, dimensions={0}, use_global_device_ids=true | all-gather | bytes 294912 | tf_op jit(solution)/shard_map/all_gather | solution.py:98
  90.3 31.8 %all_gather.50 = bf16[2048,64]{0,1:T(8,128)(2,1)S(1)} all-gather(bf16[256,64]{0,1:T(8,128)(2,1)} %param.35), channel_id=1, replica_groups=mesh['dp'=8,'tensor'=4] {'dp'}, dimensions={0}, use_global_device_ids=true | all-gather | bytes 294912 | tf_op jit(solution)/shard_map/all_gather | solution.py:99
  124.6 31.7 %all-gather = bf16[8,320,64]{1,2,0:T(8,128)(2,1)S(1)} all-gather(bf16[1,320,64]{1,2,0:T(8,128)(2,1)S(1)} %maximum_bitcast_fusion.1), channel_id=1, replica_groups=mesh['dp'=8,'tensor'=4] {'dp'}, dimensions={0}, use_global_device_ids=true | all-gather | bytes 368640 | tf_op jit(solution)/shard_map/all_gather | solution.py:128
  157.2 34.0 %all-gather.1 = bf16[8,320,64]{1,2,0:T(8,128)(2,1)} all-gather(bf16[1,320,64]{1,2,0:T(8,128)(2,1)S(1)} %fusion.68), channel_id=1, replica_groups=mesh['dp'=8,'tensor'=4] {'dp'}, dimensions={0}, use_global_device_ids=true | all-gather | bytes 368640 | tf_op jit(solution)/shard_map/all_gather | solution.py:129
  192.5 2.9 fusion.111
  196.8 32.3 %while.57 = (s32[]{:T(128)}, f32[2560]{0:T(1024)S(1)}, f32[2560]{0:T(1024)S(1)}, s32[5]{0:T(128)}, s32[]{:T(128)}, /*index=5*/s32[5,512]{1,0:T(8,128)S(1)}, s32[...) while((s32[]{:T(128)}, f32[2560]{0:T(1024)S(1)}, ...), condition=%wide.region_6.7_spmd.clone, body=%wide.region_1.6_spmd.clone.sunk | while | flops 191371264 | bytes 11532659 | solution.py:182
  202.4 6.3 conditional.12
  229.1 30.0 %while.58 = (s32[]{:T(128)}, f32[2560,64]{0,1:T(8,128)S(1)}, s32[5]{0:T(128)}, s32[]{:T(128)}, s32[5,512]{1,0:T(8,128)S(1)}, /*index=5*/s32[]{:T(128)}, s32[]{:T...) while((s32[]{:T(128)}, f32[2560,64]{0,1:T(8,128)S(1)}, ...), condition=%wide.region_10.11_spmd.clone, body=%wide.region_7.10_spmd.clone.sunk | while | flops 351437824 | bytes 2356079 | solution.py:205
  234.2 4.6 conditional.13
  235.4 3.5 convolution_add_fusion
  260.7 3.9 fusion.112
  265.2 61.6 %reduce-scatter.15.cloned.1.call-done = f32[80,2048]{1,0:T(8,128)} async-done(((f32[320,2048]{1,0:T(8,128)}), f32[80,2048]{1,0:T(8,128)}) %reduce-scatter.15.cloned.1.call-update) | async-done | bytes 655376 | tf_op jit(solution)/shard_map/reduce_scatter | solution.py:59
  331.6 90.2 %all-gather.20.cloned.1.call-done = bf16[2048,1408]{1,0:T(8,128)(2,1)} async-done(((bf16[256,1408]{1,0:T(8,128)(2,1)}), bf16[2048,1408]{1,0:T(8,128)(2,1)}) %all-gather.20.cloned.1.call-update) | async-done | bytes 5767184 | tf_op jit(solution)/shard_map/all_gather | solution.py:100
  421.8 18.5 %all-gather.18.cloned.1.call-done = bf16[320,2048]{1,0:T(8,128)(2,1)} async-done(((bf16[80,2048]{1,0:T(8,128)(2,1)}), bf16[320,2048]{1,0:T(8,128)(2,1)}) %all-gather.18.cloned.1.call-update) | async-done | bytes 1310736 | tf_op jit(solution)/shard_map/all_gather | solution.py:55
  440.3 6.5 fusion.113
  446.8 88.6 %all-gather.22.cloned.1.call-done = bf16[2048,1408]{1,0:T(8,128)(2,1)} async-done(((bf16[256,1408]{1,0:T(8,128)(2,1)}), bf16[2048,1408]{1,0:T(8,128)(2,1)}) %all-gather.22.cloned.1.call-update) | async-done | bytes 5767184 | tf_op jit(solution)/shard_map/all_gather | solution.py:101
  535.4 6.5 fusion.114
  541.9 11.6 all-gather.26.cloned.1.call-done
  553.4 95.9 %all-gather.24.cloned.1.call-done = bf16[2048,1408]{0,1:T(8,128)(2,1)} async-done(((bf16[256,1408]{0,1:T(8,128)(2,1)}), bf16[2048,1408]{0,1:T(8,128)(2,1)}) %all-gather.24.cloned.1.call-update) | async-done | bytes 5767184 | tf_op jit(solution)/shard_map/all_gather | solution.py:103
  649.3 7.8 multiply_convert_fusion
  657.1 5.6 fusion.116
  662.7 3.8 convolution_add_fusion.4
  666.5 33.0 %reduce-scatter.19.cloned.1.call-done = f32[80,2048]{1,0:T(8,128)} async-done(((f32[320,2048]{1,0:T(8,128)}), f32[80,2048]{1,0:T(8,128)}) %reduce-scatter.19.cloned.1.call-update) | async-done | bytes 655376 | tf_op jit(solution)/shard_map/reduce_scatter | solution.py:59
  703.8 18.1 %all-gather.28.cloned.1.call-done = bf16[320,2048]{1,0:T(8,128)(2,1)} async-done(((bf16[80,2048]{1,0:T(8,128)(2,1)}), bf16[320,2048]{1,0:T(8,128)(2,1)}) %all-gather.28.cloned.1.call-update) | async-done | bytes 1310736 | tf_op jit(solution)/shard_map/all_gather | solution.py:55
  721.8 2.9 convolution_convert_fusion.7
  725.0 34.7 %while.59 = (s32[]{:T(128)}, f32[2560]{0:T(1024)S(1)}, s32[5]{0:T(128)}, s32[]{:T(128)}, s32[5,512]{1,0:T(8,128)S(1)}, /*index=5*/s32[]{:T(128)}, s32[]{:T(128)}...) while((s32[]{:T(128)}, f32[2560]{0:T(1024)S(1)}, ...), condition=%wide.region_20.21_spmd.clone, body=%wide.region_16.20_spmd.clone.sunk | while | flops 352584704 | bytes 12226439 | solution.py:277
  730.0 9.7 conditional.14
  730.0 3.2 fusion.40
  734.4 5.3 fusion.35
  760.8 46.4 %while.60 = (s32[]{:T(128)}, f32[2560,64]{0,1:T(8,128)S(1)}, bf16[5,512,128]{2,1,0:T(8,128)(2,1)}, s32[5]{0:T(128)}, s32[]{:T(128)}, /*index=5*/s32[5,512]{1,0:T...) while((s32[]{:T(128)}, f32[2560,64]{0,1:T(8,128)S(1)}, ...), condition=%wide.region_24.25_spmd.clone, body=%wide.region_21.24_spmd.clone.sunk | while | flops 859014144 | bytes 27656096 | solution.py:302
  765.8 10.9 conditional.15
  766.9 3.9 fusion.51
  807.3 120.0 %reduce-scatter.37.cloned.1.call-done = bf16[320,128]{1,0:T(8,128)(2,1)} async-done(((bf16[2560,128]{1,0:T(8,128)(2,1)}), bf16[320,128]{1,0:T(8,128)(2,1)}) %reduce-scatter.37.cloned.1.call-update) | async-done | bytes 81936
  932.5 4.0 convolution_convert_fusion.3
  945.6 6.3 convolution_convert_fusion.2
  953.1 5.1 convolution_convert_fusion.1
  959.8 5.0 fusion.63
  971.8 6.4 fusion.115
  978.2 14.1 reduce-scatter.25.cloned.1.call-done
  993.7 63.4 %reduce-scatter.27.cloned.1.call-done = bf16[256,64]{0,1:T(8,128)(2,1)} async-done(((bf16[2048,64]{0,1:T(8,128)(2,1)}), bf16[256,64]{0,1:T(8,128)(2,1)}) %reduce-scatter.27.cloned.1.call-update) | async-done | bytes 32784 | tf_op jit(solution)/shard_map/reduce_scatter | solution.py:338
  1058.5 69.2 %reduce-scatter.29.cloned.1.call-done = bf16[256,512]{1,0:T(8,128)(2,1)} async-done(((bf16[2048,512]{1,0:T(8,128)(2,1)}), bf16[256,512]{1,0:T(8,128)(2,1)}) %reduce-scatter.29.cloned.1.call-update) | async-done | bytes 262160 | tf_op jit(solution)/shard_map/reduce_scatter | solution.py:341
  1129.7 68.7 %reduce-scatter.23.cloned.1.call-done = bf16[256,512]{1,0:T(8,128)(2,1)} async-done(((bf16[2048,512]{1,0:T(8,128)(2,1)}), bf16[256,512]{1,0:T(8,128)(2,1)}) %reduce-scatter.23.cloned.1.call-update) | async-done | bytes 262160 | tf_op jit(solution)/shard_map/reduce_scatter | solution.py:332
  1200.2 111.1 %reduce-scatter.31.cloned.1.call-done = bf16[256,1408]{1,0:T(8,128)(2,1)} async-done(((bf16[2048,1408]{1,0:T(8,128)(2,1)}), bf16[256,1408]{1,0:T(8,128)(2,1)}) %reduce-scatter.31.cloned.1.call-update) | async-done | bytes 720912 | tf_op jit(solution)/shard_map/reduce_scatter | solution.py:245
  1313.7 111.3 %reduce-scatter.33.cloned.1.call-done = bf16[256,1408]{1,0:T(8,128)(2,1)} async-done(((bf16[2048,1408]{1,0:T(8,128)(2,1)}), bf16[256,1408]{1,0:T(8,128)(2,1)}) %reduce-scatter.33.cloned.1.call-update) | async-done | bytes 720912 | tf_op jit(solution)/shard_map/reduce_scatter | solution.py:248
  1427.3 112.0 %reduce-scatter.35.cloned.1.call-done = bf16[256,1408]{0,1:T(8,128)(2,1)} async-done(((bf16[2048,1408]{0,1:T(8,128)(2,1)}), bf16[256,1408]{0,1:T(8,128)(2,1)}) %reduce-scatter.35.cloned.1.call-update) | async-done | bytes 720912 | tf_op jit(solution)/shard_map/reduce_scatter | solution.py:251
  1541.7 34.7 %reduce-scatter.21.cloned.1.call-done = f32[80,2048]{1,0:T(8,128)} async-done(((f32[320,2048]{1,0:T(8,128)}), f32[80,2048]{1,0:T(8,128)}) %reduce-scatter.21.cloned.1.call-update) | async-done | bytes 655376 | tf_op jit(solution)/shard_map/reduce_scatter | solution.py:59
  1577.8 39.7 %all-reduce.8 = (f32[2048]{0:T(1024)S(1)}, f32[2048]{0:T(1024)S(1)}) all-reduce(f32[2048]{0:T(1024)S(1)} %get-tuple-element.1152, f32[2048]{0:T(1024)S(1)} %copy-done.29), channel_id=7, replica_groups=mesh['dp'=8,'tensor'=4] {'dp','tensor'}, use_global_device_ids=true, to_apply=%region_29.30.clone | all-reduce | flops 4096 | bytes 32768
  (336 shorter events, 136.6 us)
Async XLA Ops:
  7.2 115.2 %all-gather.12.cloned.1.call-start = ((), (), s32[]{:S(2)}) async-start(), calls=%async_computation.12 | async-start | bytes 1638400 | tf_op jit(solution)/shard_map/all_gather | solution.py:55
  8.4 50.7 %copy-start.33 = (f32[80]{0:T(128)}, f32[80]{0:T(128)S(1)}, u32[]{:S(2)}) copy-start(f32[80]{0:T(128)S(1)} %fusion.99) | copy-start | bytes 964
  52.3 649.1 %copy-start.23 = (f32[2048]{0:T(1024)}, f32[2048]{0:T(1024)S(1)}, u32[]{:S(2)}) copy-start(f32[2048]{0:T(1024)S(1)} %get-tuple-element.1281) | copy-start | bytes 24580
  54.2 138.3 %all-gather.14.cloned.1.call-start = ((), (), s32[]{:S(2)}) async-start(), calls=%async_computation.13 | async-start | bytes 2359296 | tf_op jit(solution)/shard_map/all_gather | solution.py:97
  54.9 205.0 %all-gather.16.cloned.1.call-start = ((), (), s32[]{:S(2)}) async-start(), calls=%async_computation.14 | async-start | bytes 2359296 | tf_op jit(solution)/shard_map/all_gather | solution.py:102
  55.7 271.2 %reduce-scatter.15.cloned.1.call-start = ((), (), s32[]{:S(2)}) async-start(), calls=%async_computation.15 | async-start | bytes 3276800 | tf_op jit(solution)/shard_map/reduce_scatter | solution.py:59
  55.7 101.4 %copy-start.32 = (f32[32]{0:T(128)}, f32[32]{0:T(128)S(1)}, u32[]{:S(2)}) copy-start(f32[32]{0:T(128)S(1)} %multiply_power_fusion) | copy-start | bytes 388
  55.7 101.4 %copy-start.27 = (f32[320]{0:T(512)}, f32[320]{0:T(512)S(1)}, u32[]{:S(2)}) copy-start(f32[320]{0:T(512)S(1)} %fusion.98) | copy-start | bytes 3844
  90.3 66.9 %copy-start.13 = (bf16[2048,64]{0,1:T(8,128)(2,1)}, bf16[2048,64]{0,1:T(8,128)(2,1)S(1)}, u32[]{:S(2)}) copy-start(bf16[2048,64]{0,1:T(8,128)(2,1)S(1)} %all_gather.47) | copy-start | bytes 786436
  122.1 69.1 %copy-start.11 = (bf16[2048,64]{0,1:T(8,128)(2,1)}, bf16[2048,64]{0,1:T(8,128)(2,1)S(1)}, u32[]{:S(2)}) copy-start(bf16[2048,64]{0,1:T(8,128)(2,1)S(1)} %all_gather.50) | copy-start | bytes 786436
  122.3 73.1 %copy-start.19 = (f32[320,32]{0,1:T(8,128)}, f32[320,32]{0,1:T(8,128)S(1)}, u32[]{:S(2)}) copy-start(f32[320,32]{0,1:T(8,128)S(1)} %get-tuple-element.1309) | copy-start | bytes 122884
  122.3 73.1 %copy-start.21 = (f32[320,32]{0,1:T(8,128)}, f32[320,32]{0,1:T(8,128)S(1)}, u32[]{:S(2)}) copy-start(f32[320,32]{0,1:T(8,128)S(1)} %get-tuple-element.1310) | copy-start | bytes 122884
  122.4 34.3 %copy-start = (bf16[320,2048]{1,0:T(8,128)(2,1)S(1)}, bf16[320,2048]{1,0:T(8,128)(2,1)}, u32[]{:S(2)}) copy-start(bf16[320,2048]{1,0:T(8,128)(2,1)} %all-gather.12.cloned.1.call-done) | copy-start | bytes 3932164
  264.6 62.3 %copy-start.4 = (bf16[80,2048]{1,0:T(8,128)(2,1)S(1)}, bf16[80,2048]{1,0:T(8,128)(2,1)}, u32[]{:S(2)}) copy-start(bf16[80,2048]{1,0:T(8,128)(2,1)} %param.29) | copy-start | bytes 983044
  264.6 157.2 %all-gather.20.cloned.1.call-start = ((), (), s32[]{:S(2)}) async-start(), calls=%async_computation.17 | async-start | bytes 6488064 | tf_op jit(solution)/shard_map/all_gather | solution.py:100
  265.2 175.1 %all-gather.18.cloned.1.call-start = ((), (), s32[]{:S(2)}) async-start(), calls=%async_computation.16 | async-start | bytes 1638400 | tf_op jit(solution)/shard_map/all_gather | solution.py:55
  328.2 373.2 %copy-start.2 = (f32[80,2048]{1,0:T(8,128)}, f32[80,2048]{1,0:T(8,128)S(1)}, u32[]{:S(2)}) copy-start(f32[80,2048]{1,0:T(8,128)S(1)} %get-tuple-element.1283) | copy-start | bytes 1966084
  328.2 373.2 %copy-start.30 = (f32[80]{0:T(128)}, f32[80]{0:T(128)S(1)}, u32[]{:S(2)}) copy-start(f32[80]{0:T(128)S(1)} %fusion.100) | copy-start | bytes 964
  329.1 206.2 %all-gather.22.cloned.1.call-start = ((), (), s32[]{:S(2)}) async-start(), calls=%async_computation.18 | async-start | bytes 6488064 | tf_op jit(solution)/shard_map/all_gather | solution.py:101
  329.9 223.5 %all-gather.26.cloned.1.call-start = ((), (), s32[]{:S(2)}) async-start(), calls=%async_computation.21 | async-start | bytes 1638400 | tf_op jit(solution)/shard_map/all_gather | solution.py:55
  330.6 318.6 %all-gather.24.cloned.1.call-start = ((), (), s32[]{:S(2)}) async-start(), calls=%async_computation.19 | async-start | bytes 6488064 | tf_op jit(solution)/shard_map/all_gather | solution.py:103
  331.4 368.1 %reduce-scatter.19.cloned.1.call-start = ((), (), s32[]{:S(2)}) async-start(), calls=%async_computation.22 | async-start | bytes 3276800 | tf_op jit(solution)/shard_map/reduce_scatter | solution.py:59
  666.5 34.9 %copy-start.8 = (bf16[80,2048]{1,0:T(8,128)(2,1)S(1)}, bf16[80,2048]{1,0:T(8,128)(2,1)}, u32[]{:S(2)}) copy-start(bf16[80,2048]{1,0:T(8,128)(2,1)} %param.41) | copy-start | bytes 983044
  666.5 55.3 %all-gather.28.cloned.1.call-start = ((), (), s32[]{:S(2)}) async-start(), calls=%async_computation.23 | async-start | bytes 1638400 | tf_op jit(solution)/shard_map/all_gather | solution.py:55
  703.5 223.7 %reduce-scatter.37.cloned.1.call-start = ((), (), s32[]{:S(2)}) async-start(), calls=%async_computation.32 | async-start | bytes 737280
  760.8 167.4 %copy-start.28 = (f32[320]{0:T(512)S(1)}, f32[320]{0:T(512)}, u32[]{:S(2)}) copy-start(f32[320]{0:T(512)} %copy-done.27) | copy-start | bytes 3844
  760.8 168.3 %copy-start.1 = (bf16[320,2048]{1,0:T(8,128)(2,1)S(1)}, bf16[320,2048]{1,0:T(8,128)(2,1)}, u32[]{:S(2)}) copy-start(bf16[320,2048]{1,0:T(8,128)(2,1)} %all-gather.12.cloned.1.call-done) | copy-start | bytes 3932164
  807.2 125.3 %copy-start.17 = (bf16[320,512]{1,0:T(8,128)(2,1)S(1)}, bf16[320,512]{1,0:T(8,128)(2,1)}, u32[]{:S(2)}) copy-start(bf16[320,512]{1,0:T(8,128)(2,1)} %copy-done.16) | copy-start | bytes 983044
  807.2 185.1 %reduce-scatter.25.cloned.1.call-start = ((), (), s32[]{:S(2)}) async-start(), calls=%async_computation.26 | async-start | bytes 294912 | tf_op jit(solution)/shard_map/reduce_scatter | solution.py:335
  930.3 126.9 %reduce-scatter.27.cloned.1.call-start = ((), (), s32[]{:S(2)}) async-start(), calls=%async_computation.27 | async-start | bytes 294912 | tf_op jit(solution)/shard_map/reduce_scatter | solution.py:338
  932.4 195.3 %reduce-scatter.29.cloned.1.call-start = ((), (), s32[]{:S(2)}) async-start(), calls=%async_computation.28 | async-start | bytes 2359296 | tf_op jit(solution)/shard_map/reduce_scatter | solution.py:341
  936.4 261.9 %reduce-scatter.23.cloned.1.call-start = ((), (), s32[]{:S(2)}) async-start(), calls=%async_computation.25 | async-start | bytes 2359296 | tf_op jit(solution)/shard_map/reduce_scatter | solution.py:332
  945.5 365.8 %reduce-scatter.31.cloned.1.call-start = ((), (), s32[]{:S(2)}) async-start(), calls=%async_computation.29 | async-start | bytes 6488064 | tf_op jit(solution)/shard_map/reduce_scatter | solution.py:245
  951.9 473.1 %reduce-scatter.33.cloned.1.call-start = ((), (), s32[]{:S(2)}) async-start(), calls=%async_computation.30 | async-start | bytes 6488064 | tf_op jit(solution)/shard_map/reduce_scatter | solution.py:248
  958.3 581.1 %reduce-scatter.35.cloned.1.call-start = ((), (), s32[]{:S(2)}) async-start(), calls=%async_computation.31 | async-start | bytes 6488064 | tf_op jit(solution)/shard_map/reduce_scatter | solution.py:251
  964.9 611.5 %reduce-scatter.21.cloned.1.call-start = ((), (), s32[]{:S(2)}) async-start(), calls=%async_computation.24 | async-start | bytes 3276800 | tf_op jit(solution)/shard_map/reduce_scatter | solution.py:59
  970.6 648.0 %reduce-scatter.17.cloned.1.call-start = ((), (), s32[]{:S(2)}) async-start(), calls=%async_computation.20 | async-start | bytes 3276800 | tf_op jit(solution)/shard_map/reduce_scatter | solution.py:59
  1313.6 262.8 %copy-start.5 = (bf16[80,2048]{1,0:T(8,128)(2,1)S(1)}, bf16[80,2048]{1,0:T(8,128)(2,1)}, u32[]{:S(2)}) copy-start(bf16[80,2048]{1,0:T(8,128)(2,1)} %param.29) | copy-start | bytes 983044
  1313.6 262.8 %copy-start.26 = (f32[2048]{0:T(1024)S(1)}, f32[2048]{0:T(1024)}, u32[]{:S(2)}) copy-start(f32[2048]{0:T(1024)} %copy-done.25) | copy-start | bytes 24580
  1313.6 262.8 %copy-start.34 = (f32[80]{0:T(128)S(1)}, f32[80]{0:T(128)}, u32[]{:S(2)}) copy-start(f32[80]{0:T(128)} %copy-done.33) | copy-start | bytes 964
  1313.6 264.2 %copy-start.29 = (f32[2048]{0:T(1024)S(1)}, f32[2048]{0:T(1024)}, u32[]{:S(2)}) copy-start(f32[2048]{0:T(1024)} %get-tuple-element.1150) | copy-start | bytes 24580
  1313.6 305.0 %copy-start.38 = (f32[80]{0:T(128)S(1)}, f32[80]{0:T(128)}, u32[]{:S(2)}) copy-start(f32[80]{0:T(128)} %copy-done.37) | copy-start | bytes 964
  1313.6 305.1 %copy-start.3 = (f32[80,2048]{1,0:T(8,128)S(1)}, f32[80,2048]{1,0:T(8,128)}, u32[]{:S(2)}) copy-start(f32[80,2048]{1,0:T(8,128)} %copy-done.2) | copy-start | bytes 1966084
  1313.6 305.1 %copy-start.7 = (f32[80,2048]{1,0:T(8,128)S(1)}, f32[80,2048]{1,0:T(8,128)}, u32[]{:S(2)}) copy-start(f32[80,2048]{1,0:T(8,128)} %reduce-scatter.19.cloned.1.call-done) | copy-start | bytes 1966084
  1313.6 305.1 %copy-start.9 = (bf16[80,2048]{1,0:T(8,128)(2,1)S(1)}, bf16[80,2048]{1,0:T(8,128)(2,1)}, u32[]{:S(2)}) copy-start(bf16[80,2048]{1,0:T(8,128)(2,1)} %param.41) | copy-start | bytes 983044
  1313.6 305.1 %copy-start.24 = (f32[2048]{0:T(1024)S(1)}, f32[2048]{0:T(1024)}, u32[]{:S(2)}) copy-start(f32[2048]{0:T(1024)} %copy-done.23) | copy-start | bytes 24580
  1313.7 305.1 %copy-start.31 = (f32[80]{0:T(128)S(1)}, f32[80]{0:T(128)}, u32[]{:S(2)}) copy-start(f32[80]{0:T(128)} %copy-done.30) | copy-start | bytes 964
  1313.7 305.1 %copy-start.36 = (f32[80]{0:T(128)S(1)}, f32[80]{0:T(128)}, u32[]{:S(2)}) copy-start(f32[80]{0:T(128)} %copy-done.35) | copy-start | bytes 964
  (20 other events, 71.7 us)
Sparse Core Ops, SparseCore 0:
  54.3 18.0 all-gather.11
  74.5 52.9 all-gather.13
  129.5 52.9 all-gather.15
  264.7 62.1 reduce-scatter.14
  329.1 92.6 all-gather.19
  423.9 16.3 all-gather.17
  442.7 92.6 all-gather.21
  537.0 16.3 all-gather.25
  555.7 93.5 all-gather.23
  666.6 32.8 reduce-scatter.18
  703.6 18.1 all-gather.27
  807.3 119.8 reduce-scatter.36
  931.5 60.7 reduce-scatter.24
  996.4 60.6 reduce-scatter.26
  1060.9 66.7 reduce-scatter.28
  1131.5 66.8 reduce-scatter.22
  1202.3 108.9 reduce-scatter.30
  1315.2 109.7 reduce-scatter.32
  1429.1 110.1 reduce-scatter.34
  1541.9 34.4 reduce-scatter.20
  1578.9 34.8 reduce-scatter.16
where the time goes:
time: 1640 us; the launch traced here: 1630 us
  waiting for transfers between devices  1130 us (69%)
  blocking collectives  210 us (13%)
  matrix products  102 us (6%)
  local copies, waits for them, and re-layouts  73.9 us (5%)
  loops' own time  64.4 us (4%)
  other arithmetic  34.4 us (2%)
    reduce_scatter x4, waiting for transfers between devices, spread_rows(): lax.psum_scatter(term_fn(jnp.int32(0), row_count * lax.axis_size('tensor'...  129 us
    unnamed x22, waiting for transfers between devices  124 us
    reduce_scatter x1, waiting for transfers between devices, shards(): lax.psum_scatter(grad_down_cols.astype(jnp.bfloat16), 'dp', scatter_dimen...  112 us
    reduce_scatter x1, waiting for transfers between devices, shards(): lax.psum_scatter(grad_up_all.astype(jnp.bfloat16), 'dp', scatter_dimensio...  111 us
    reduce_scatter x1, waiting for transfers between devices, shards(): lax.psum_scatter(grad_gate_all.astype(jnp.bfloat16), 'dp', scatter_dimens...  111 us
    all_gather x1, waiting for transfers between devices, shards(): lax.all_gather(w_down.T, 'dp', axis=0, tiled=True)  95.9 us
    all_gather x1, waiting for transfers between devices, shards(): lax.all_gather(w_gate, 'dp', axis=0, tiled=True)  90.2 us
    all_gather x1, waiting for transfers between devices, shards(): lax.all_gather(w_up, 'dp', axis=0, tiled=True)  88.6 us
  transfers between devices with their start and end apart: 21, of which 17 were waited for; matrix products, arithmetic and copies ran while one was open for 7% of the time, Pallas kernels for 0%

commit v1 on v0

v1 whole, which is shorter than its diff:
```python
import functools

import jax
import jax.numpy as jnp
from jax import lax
from jax.experimental import pallas as pl
from jax.experimental.pallas import tpu as pltpu
from jax.sharding import PartitionSpec as P

EPS = 1e-05
NEG = -1e30
THETA = 10000.0
BF = jnp.bfloat16
F32 = jnp.float32
MESH = pl.DeviceIdType.MESH
ANY = pl.BlockSpec(memory_space=pl.ANY)
VM = pl.BlockSpec(memory_space=pltpu.VMEM)


def sem_count():
    return 128 + 8 * lax.axis_size("dp")


class Sems:
    def __init__(self, send, recv):
        self.send, self.recv, self.used = send, recv, 0

    def take(self, count):
        base = self.used
        self.used += count
        assert self.used <= sem_count()
        return base


class Place:
    def __init__(self, chain):
        self.n_dp = lax.axis_size("dp")
        self.n_t = lax.axis_size("tensor")
        self.chain = chain
        self.groups = self.n_dp // chain
        self.d = lax.axis_index("dp")
        self.s = lax.axis_index("tensor")
        self.z = self.d // self.groups
        self.t = self.d % self.groups
        self.y = self.s // 2
        self.c = self.s % 2
        self.sy = (1 - self.y) * 2 + self.c
        self.sc = self.y * 2 + 1 - self.c
        self.so = (1 - self.y) * 2 + 1 - self.c
        self.above = self.at(z=jnp.minimum(self.z + 1, chain - 1))
        self.below = self.at(z=jnp.maximum(self.z - 1, 0))

    def at(self, z=None, t=None, s=None):
        z = self.z if z is None else z
        t = self.t if t is None else t
        s = self.s if s is None else s
        return {"dp": z * self.groups + t, "tensor": s}


def when(pred, act):
    if pred is None:
        act()
    else:
        pl.when(pred)(act)


class Copies:
    def __init__(self, sems):
        self.sems = sems
        self.sent = []

    def go(self, i, src, dst, where, pred=None):
        copy = pltpu.make_async_remote_copy(
            src_ref=src,
            dst_ref=dst,
            send_sem=self.sems.send.at[i],
            recv_sem=self.sems.recv.at[i],
            device_id=where,
            device_id_type=MESH,
        )
        when(pred, copy.start)
        self.sent.append((copy, pred))

    def keep(self, i, src, dst):
        copy = pltpu.make_async_copy(src, dst, self.sems.send.at[i])
        copy.start()
        return copy

    def arrive(self, i, dst, where, pred=None):
        copy = pltpu.make_async_remote_copy(
            src_ref=dst,
            dst_ref=dst,
            send_sem=self.sems.send.at[i],
            recv_sem=self.sems.recv.at[i],
            device_id=where,
            device_id_type=MESH,
        )
        when(pred, copy.wait_recv)

    def finish(self):
        for copy, pred in self.sent:
            when(pred, copy.wait_send)


def greet(pc):
    barrier = pltpu.get_barrier_semaphore()
    for k in range(1, pc.n_dp):
        pl.semaphore_signal(
            barrier, inc=1, device_id={"dp": (pc.d + k) % pc.n_dp, "tensor": pc.s}, device_id_type=MESH
        )
    for k in range(1, pc.n_t):
        pl.semaphore_signal(
            barrier, inc=1, device_id={"dp": pc.d, "tensor": (pc.s + k) % pc.n_t}, device_id_type=MESH
        )
    pl.semaphore_wait(barrier, pc.n_dp + pc.n_t - 2)


def run(*tasks):
    live = list(tasks)
    while live:
        left = []
        for task in live:
            try:
                next(task)
                left.append(task)
            except StopIteration:
                pass
        live = left


def chain_steps(pc):
    chain, z = pc.chain, pc.z
    for k in range(chain - 1):
        for side in (0, 1):
            if side == 0:
                got = z - 1 - k >= 0
                yield k, side, jnp.maximum(z - 1 - k, 0), got, pc.above, jnp.logical_and(got, z + 1 < chain)
            else:
                got = z + 1 + k <= chain - 1
                yield k, side, jnp.minimum(z + 1 + k, chain - 1), got, pc.below, jnp.logical_and(got, z > 0)


def plane_gather(pc, sems, own, out, parts=1):
    chain, z, s = pc.chain, pc.z, pc.s
    width = own.shape[1] // parts
    cp = Copies(sems)
    base = sems.take(1 + 8 * chain * parts)

    def sem(kind, i, p):
        return base + 1 + (kind * chain + i) * parts + p

    def view(b, col, p):
        return out.at[b, col, :, pl.ds(p * width, width)]

    keep = cp.keep(base, own, out.at[z, s])
    for p in range(parts):
        src = own.at[:, pl.ds(p * width, width)]
        if chain > 1:
            cp.go(sem(0, 0, p), src, view(z, s, p), pc.above, z + 1 < chain)
            cp.go(sem(1, 0, p), src, view(z, s, p), pc.below, z > 0)
        cp.go(sem(2, 0, p), src, view(z, s, p), pc.at(s=pc.sy))
        cp.go(sem(4, 0, p), src, view(z, s, p), pc.at(s=pc.sc))
    yield
    crossing = [(z, None, 0, p) for p in range(parts)]
    landed = []

    def cross(count):
        for _ in range(min(count, len(crossing))):
            b, got, i, p = crossing.pop(0)
            cp.arrive(sem(2, i, p), view(b, pc.sy, p), pc.at(), got)
            cp.go(sem(6, i, p), view(b, pc.sy, p), view(b, pc.sy, p), pc.at(s=pc.sc), got)
            landed.append((b, got, i, p))

    steps = list(chain_steps(pc))
    for k in range(chain - 1):
        for p in range(parts):
            for step, side, b, got, onward, more in steps:
                if step != k:
                    continue
                i = 1 + k if side == 0 else chain + k
                cp.arrive(sem(side, k, p), view(b, s, p), pc.at(), got)
                if k < chain - 2:
                    cp.go(sem(side, k + 1, p), view(b, s, p), view(b, s, p), onward, more)
                cp.go(sem(2, i, p), view(b, s, p), view(b, s, p), pc.at(s=pc.sy), got)
                cp.go(sem(4, i, p), view(b, s, p), view(b, s, p), pc.at(s=pc.sc), got)
                crossing.append((b, got, i, p))
            cross(1 if k == 0 else 2)
            yield
    while crossing:
        cross(2)
        yield
    for b, got, i, p in landed:
        cp.arrive(sem(4, i, p), view(b, pc.sc, p), pc.at(), got)
        cp.arrive(sem(6, i, p), view(b, pc.so, p), pc.at(), got)
    keep.wait()
    cp.finish()
    yield


def far_first(chain, z, j):
    if j == chain - 1:
        return z
    up = jnp.where(j < chain - 1 - z, chain - 1 - j, j - (chain - 1 - z))
    down = jnp.where(j < z, j, chain - 1 - (j - z))
    return jnp.where(2 * z < chain, up, down)


def each_rows(count, fn, rows=16):
    def body(i, carry):
        fn(pl.ds(pl.multiple_of(i * rows, rows), rows))
        return carry

    lax.fori_loop(0, count // rows, body, 0)


def chain_reduce(pc, cp, right, left, b, last, value, zsend, lrecv, rrecv, store, rows, cols):
    chain, z = pc.chain, pc.z
    if not last:
        fromleft = jnp.logical_and(b > z, z > 0)
        fromright = jnp.logical_and(b < z, z < chain - 1)
        cp.arrive(right, lrecv.at[b, :, cols], pc.at(), fromleft)
        cp.arrive(left, rrecv.at[b, :, cols], pc.at(), fromright)

        @pl.when(fromleft)
        def _():
            def add(r):
                zsend[b, r, cols] = (value(r) + lrecv[b, r, cols].astype(F32)).astype(BF)

            each_rows(rows, add)

        @pl.when(fromright)
        def _():
            def add(r):
                zsend[b, r, cols] = (value(r) + rrecv[b, r, cols].astype(F32)).astype(BF)

            each_rows(rows, add)

        @pl.when(jnp.logical_not(jnp.logical_or(fromleft, fromright)))
        def _():
            def add(r):
                zsend[b, r, cols] = value(r).astype(BF)

            each_rows(rows, add)

        cp.go(right, zsend.at[b, :, cols], lrecv.at[b, :, cols], pc.above, b > z)
        cp.go(left, zsend.at[b, :, cols], rrecv.at[b, :, cols], pc.below, b < z)
        return

    def first(r):
        store(r, value(r), False)

    each_rows(rows, first)
    if chain > 1:

        @pl.when(z > 0)
        def _():
            cp.arrive(right, lrecv.at[b, :, cols], pc.at())

            def add(r):
                store(r, lrecv[b, r, cols].astype(F32), True)

            each_rows(rows, add)

        @pl.when(z < chain - 1)
        def _():
            cp.arrive(left, rrecv.at[b, :, cols], pc.at())

            def add(r):
                store(r, rrecv[b, r, cols].astype(F32), True)

            each_rows(rows, add)


def plane_scratch(chain, rows, width):
    return [
        pltpu.VMEM((chain, 2, rows, width), BF),
        pltpu.VMEM((chain, rows, width), BF),
        pltpu.VMEM((chain, rows, width), BF),
        pltpu.VMEM((chain, rows, width), BF),
        pltpu.VMEM((chain, rows, width), BF),
        pltpu.VMEM((chain, rows, width), BF),
    ]


def plane_reduce(pc, sems, part, scratch, out, parts=1):
    crecv, csum, yrecv, zsend, lrecv, rrecv = scratch
    chain, z = pc.chain, pc.z
    count = out.shape[0]
    width = out.shape[1] // parts
    cp = Copies(sems)
    base = sems.take(5 * chain * parts)

    def sem(kind, i, p):
        return base + (kind * chain + i) * parts + p

    todo = [(j, far_first(chain, z, j), p) for j in range(chain) for p in range(parts)]
    mine = pc.s

    def cols_of(p):
        return pl.ds(p * width, width)

    for j, b, p in todo:
        for over in (1, 0):
            col = pc.so if over else pc.sc
            cp.go(
                sem(over, j, p),
                part.at[b, col, :, cols_of(p)],
                crecv.at[b, over, :, cols_of(p)],
                pc.at(s=pc.sc),
            )
    yield
    for j, b, p in todo:
        cols = cols_of(p)
        cp.arrive(sem(1, j, p), crecv.at[b, 1, :, cols], pc.at())

        def add(r):
            csum[b, r, cols] = (part[b, pc.sy, r, cols].astype(F32) + crecv[b, 1, r, cols].astype(F32)).astype(BF)

        each_rows(count, add)
        cp.go(sem(2, j, p), csum.at[b, :, cols], yrecv.at[b, :, cols], pc.at(s=pc.sy))
        yield
    for j, b, p in todo:
        cols = cols_of(p)
        cp.arrive(sem(0, j, p), crecv.at[b, 0, :, cols], pc.at())
        cp.arrive(sem(2, j, p), yrecv.at[b, :, cols], pc.at())

        def value(r):
            return (
                part[b, mine, r, cols].astype(F32)
                + crecv[b, 0, r, cols].astype(F32)
                + yrecv[b, r, cols].astype(F32)
            )

        def store(r, term, more):
            out[r, cols] = out[r, cols] + term if more else term

        chain_reduce(
            pc,
            cp,
            sem(3, 0, 0) + b * parts + p,
            sem(4, 0, 0) + b * parts + p,
            b,
            j == chain - 1,
            value,
            zsend,
            lrecv,
            rrecv,
            store,
            count,
            cols,
        )
        yield
    cp.finish()
    yield


def dp_gather(pc, sems, own, out):
    chain, groups, z, t = pc.chain, pc.groups, pc.z, pc.t
    cp = Copies(sems)
    base = sems.take(1 + 2 * chain + 2 * chain * groups)
    along = (base + 1, base + 1 + chain)
    across = base + 1 + 2 * chain
    keep = cp.keep(base, own, out(pc.d))
    if chain > 1:
        cp.go(along[0], own, out(pc.d), pc.above, z + 1 < chain)
        cp.go(along[1], own, out(pc.d), pc.below, z > 0)
    for g in range(1, groups):
        cp.go(across + g, own, out(pc.d), pc.at(t=(t + g) % groups))
    yield
    landed = [(z, None, 0)]
    for k, side, b, got, onward, more in chain_steps(pc):
        i = 1 + k if side == 0 else chain + k
        block = out(b * groups + t)
        cp.arrive(along[side] + k, block, pc.at(), got)
        if k < chain - 2:
            cp.go(along[side] + k + 1, block, block, onward, more)
        for g in range(1, groups):
            cp.go(across + i * groups + g, block, block, pc.at(t=(t + g) % groups), got)
        landed.append((b, got, i))
        yield
    for b, got, i in landed:
        for g in range(1, groups):
            cp.arrive(across + i * groups + g, out(b * groups + (t - g + groups) % groups), pc.at(), got)
    keep.wait()
    cp.finish()
    yield


def spread(pc, sems, blocks, out):
    chain, groups, z, t = pc.chain, pc.groups, pc.z, pc.t
    cp = Copies(sems)
    base = sems.take(1 + chain + chain * groups)
    along, across = base + 1, base + 1 + chain
    keep = cp.keep(base, blocks(z), out(pc.d))
    for k in range(1, chain):
        to = (z + k) % chain
        cp.go(along + k, blocks(to), out(pc.d), pc.at(z=to))
    for g in range(1, groups):
        cp.go(across + g, blocks(z), out(pc.d), pc.at(t=(t + g) % groups))
    yield
    for k in range(1, chain):
        block = out((z - k + chain) % chain * groups + t)
        cp.arrive(along + k, block, pc.at())
        for g in range(1, groups):
            cp.go(across + k * groups + g, block, block, pc.at(t=(t + g) % groups))
        yield
    for k in range(chain):
        for g in range(1, groups):
            block = out((z - k + chain) % chain * groups + (t - g + groups) % groups)
            cp.arrive(across + k * groups + g, block, pc.at())
    keep.wait()
    cp.finish()
    yield


def side_sums(pc, cp, across, part, xrecv, csum, count, order):
    chain, groups, t = pc.chain, pc.groups, pc.t
    for j, b in order:
        for g in range(1, groups):
            to = (t + g) % groups
            cp.go(across + j * groups + g, part.at[b * groups + to], xrecv.at[g - 1, b], pc.at(t=to))
    yield
    for j, b in order:
        for g in range(1, groups):
            cp.arrive(across + j * groups + g, xrecv.at[g - 1, b], pc.at())

        def add(r):
            total = part[b * groups + t, r, :].astype(F32)
            for g in range(1, groups):
                total = total + xrecv[g - 1, b, r, :].astype(F32)
            csum(b, r, total)

        each_rows(count, add)
        yield j, b


def dp_scratch(chain, groups, rows, width):
    return [
        pltpu.VMEM((max(groups - 1, 1), chain, rows, width), BF),
        pltpu.VMEM((chain, rows, width), F32),
        pltpu.VMEM((chain, rows, width), BF),
        pltpu.VMEM((chain, rows, width), BF),
        pltpu.VMEM((chain, rows, width), BF),
    ]


def dp_reduce(pc, sems, part, scratch, out):
    xrecv, sums, zsend, lrecv, rrecv = scratch
    chain, groups, z = pc.chain, pc.groups, pc.z
    count = out.shape[0]
    cp = Copies(sems)
    base = sems.take(chain * groups + 2 * chain)
    right = base + chain * groups
    left = right + chain
    order = [(j, far_first(chain, z, j)) for j in range(chain)]
    cols = pl.ds(0, out.shape[1])

    def csum(b, r, total):
        sums[b, r, :] = total

    for made in side_sums(pc, cp, base, part, xrecv, csum, count, order):
        if made is None:
            yield
            continue
        j, b = made

        def value(r):
            return sums[b, r, :]

        def store(r, term, more):
            out[r, :] = out[r, :] + term if more else term

        chain_reduce(
            pc, cp, right + b, left + b, b, j == chain - 1, value, zsend, lrecv, rrecv, store, count, cols
        )
        yield
    cp.finish()
    yield


def collect_scratch(chain, groups, rows, width):
    return [
        pltpu.VMEM((max(groups - 1, 1), chain, rows, width), BF),
        pltpu.VMEM((chain, rows, width), BF),
    ]


def collect(pc, sems, part, scratch, out):
    xrecv, sums = scratch
    chain, groups, z = pc.chain, pc.groups, pc.z
    count = part.shape[1]
    cp = Copies(sems)
    base = sems.take(chain * groups + chain)
    along = base + chain * groups
    order = [(k, (z + chain - 1 - k) % chain) for k in range(chain)]

    def csum(b, r, total):
        sums[b, r, :] = total.astype(BF)

    for made in side_sums(pc, cp, base, part, xrecv, csum, count, order):
        if made is None:
            yield
            continue
        k, b = made
        if k < chain - 1:
            cp.go(along + k, sums.at[b], out.at[z], pc.at(z=b))
        else:
            keep = cp.keep(along + k, sums.at[b], out.at[z])
        yield
    for k in range(chain - 1):
        b = (z - (chain - 1 - k) + chain) % chain
        cp.arrive(along + k, out.at[b], pc.at())
    keep.wait()
    cp.finish()
    yield


def share_gains(pc, sems, own, table):
    cp = Copies(sems)
    base = sems.take(pc.n_dp + pc.n_t)
    table[pc.d, pc.s] = own[...]
    for k in range(1, pc.n_t):
        cp.go(base + k, table.at[pc.d, pc.s], table.at[pc.d, pc.s], {"dp": pc.d, "tensor": (pc.s + k) % pc.n_t})
    yield
    for k in range(1, pc.n_t):
        cp.arrive(base + k, table.at[pc.d, (pc.s - k + pc.n_t) % pc.n_t], pc.at())
    second = base + pc.n_t
    for k in range(1, pc.n_dp):
        cp.go(second + k, table.at[pc.d], table.at[pc.d], {"dp": (pc.d + k) % pc.n_dp, "tensor": pc.s})
    yield
    for k in range(1, pc.n_dp):
        cp.arrive(second + k, table.at[(pc.d - k + pc.n_dp) % pc.n_dp], pc.at())
    cp.finish()
    yield


def lay_gains(pc, table, gains):
    lanes = 128
    devices = pc.n_dp * pc.n_t
    each = gains.shape[1] // devices
    per = lanes // each
    lane = lax.broadcasted_iota(jnp.int32, (8, lanes), 1)
    for j in range(gains.shape[1] // lanes):
        row = table[(j * per) // pc.n_t, (j * per) % pc.n_t]
        for k in range(1, per):
            o = j * per + k
            row = jnp.where(lane >= k * each, table[o // pc.n_t, o % pc.n_t], row)
        gains[:, j * lanes : (j + 1) * lanes] = row


def sum_gains(pc, sems, groups_of, stage, mid, second, out):
    count = stage.shape[1]
    n_dp, n_t = pc.n_dp, pc.n_t
    cp = Copies(sems)
    base = sems.take(n_dp + n_t)

    def start_of(d):
        return d * groups_of.shape[0] // n_dp

    for k in range(1, n_dp):
        to = (pc.d + k) % n_dp
        cp.go(
            base + k,
            groups_of.at[pl.ds(start_of(to), count)],
            stage.at[pc.d],
            {"dp": to, "tensor": pc.s},
        )
    stage[pc.d] = groups_of[pl.ds(start_of(pc.d), count)]
    yield
    for k in range(1, n_dp):
        cp.arrive(base + k, stage.at[(pc.d - k + n_dp) % n_dp], pc.at())
    total = stage[0]
    for k in range(1, n_dp):
        total = total + stage[k]
    mid[...] = total
    yield
    last = base + n_dp
    for k in range(1, n_t):
        to = (pc.s + k) % n_t
        cp.go(last + k, mid.at[to * count // n_t], second.at[pc.s], {"dp": pc.d, "tensor": to})
    second[pc.s] = mid[pc.s * count // n_t]
    yield
    for k in range(1, n_t):
        cp.arrive(last + k, second.at[(pc.s - k + n_t) % n_t], pc.at())
    total = second[0]
    for k in range(1, n_t):
        total = total + second[k]
    out[...] = total
    cp.finish()
    yield


def call(kernel, name, number, ins, outs, scratch, operands, cost):
    sems = [pltpu.SemaphoreType.DMA((sem_count(),))] * 2
    return pl.pallas_call(
        kernel,
        out_shape=[jax.ShapeDtypeStruct(shape, kind) for shape, kind, _ in outs],
        in_specs=ins,
        out_specs=[space for _, _, space in outs],
        scratch_shapes=list(scratch) + sems,
        name=name,
        cost_estimate=pl.CostEstimate(flops=0, bytes_accessed=cost, transcendentals=0),
        compiler_params=pltpu.CompilerParams(
            collective_id=number, has_side_effects=True, vmem_limit_bytes=58 << 20
        ),
    )(*operands)


def unit(v):
    return lax.rsqrt(jnp.mean(v * v, axis=-1, keepdims=True) + EPS)


def gather_kernel(chain, *refs):
    (tok, own_gain, wqkv, wout, wgate, wup, wdown, cot) = refs[:8]
    (normed_all, gains, wqkv_all, wout_all, wgate_all, wup_all, wdown_all, cot_all) = refs[8:16]
    table, normed, send, recv = refs[16:]
    sems = Sems(send, recv)
    pc, near = Place(chain), Place(1)
    greet(pc)

    def head():
        yield from share_gains(pc, sems, own_gain, table)
        lay_gains(pc, table, gains)

        def norm(r):
            v = tok[r, :].astype(F32)
            normed[r, :] = (v * unit(v) * gains[0:1, :]).astype(BF)

        each_rows(tok.shape[0], norm)
        yield from plane_gather(near, sems, normed, normed_all)

    def by_dp(ref):
        return lambda d: ref.at[d]

    tasks = [
        head(),
        dp_gather(pc, sems, wqkv, by_dp(wqkv_all)),
        dp_gather(pc, sems, wout, by_dp(wout_all)),
        spread(pc, sems, by_dp(wgate), by_dp(wgate_all)),
        spread(pc, sems, by_dp(wup), by_dp(wup_all)),
        spread(pc, sems, by_dp(wdown), by_dp(wdown_all)),
        plane_gather(pc, sems, cot, cot_all, 2),
    ]
    run(*tasks)


def keys_kernel(chain, own, out, send, recv):
    sems = Sems(send, recv)
    pc = Place(chain)
    greet(pc)
    run(dp_gather(pc, sems, own, lambda d: out.at[d]))


def middle_kernel(chain, part, tok, gains, middle, all_two, *rest):
    scratch, (total, two), (send, recv) = rest[:6], rest[6:8], rest[8:]
    sems = Sems(send, recv)
    pc, near = Place(chain), Place(1)
    greet(pc)

    def go():
        yield from plane_reduce(near, sems, part, scratch, total)

        def norm(r):
            v = tok[r, :].astype(F32) + total[r, :]
            middle[r, :] = v
            two[r, :] = (v * unit(v) * gains[1:2, :]).astype(BF)

        each_rows(total.shape[0], norm)
        yield from plane_gather(pc, sems, two, all_two, 2)

    run(go())


def back_kernel(chain, *refs):
    (npart, opart, ggate, gup, gdown, middle, cot, gains) = refs[:8]
    (layer_out, middle_grad, branch_all, gain_out, cgate, cup, cdown) = refs[8:15]
    rest = refs[15:]
    s_one, s_two = rest[:6], rest[6:12]
    s_gate, s_up, s_down = rest[12:14], rest[14:16], rest[16:18]
    ngrad, osum, branch, gain_acc, send, recv = rest[18:]
    sems = Sems(send, recv)
    pc, near = Place(chain), Place(1)
    greet(pc)
    rows = middle.shape[0]

    def go():
        yield from plane_reduce(pc, sems, npart, s_one, ngrad)
        gain_acc[...] = jnp.zeros_like(gain_acc)

        def back(r):
            m = middle[r, :]
            root = unit(m)
            xhat = m * root
            g = ngrad[r, :]
            e = g * gains[1:2, :]
            grad = cot[r, :].astype(F32) + root * (e - xhat * jnp.mean(e * xhat, axis=-1, keepdims=True))
            middle_grad[r, :] = grad
            branch[r, :] = grad.astype(BF)
            gain_acc[...] += g * xhat

        each_rows(rows, back)
        yield from plane_gather(near, sems, branch, branch_all)
        gain_out[...] = jnp.broadcast_to(jnp.sum(gain_acc[...], axis=0, keepdims=True), gain_out.shape)

    def last():
        yield from plane_reduce(pc, sems, opart, s_two, osum)

        def finish(r):
            layer_out[r, :] = (middle[r, :] + osum[r, :]).astype(BF)

        each_rows(rows, finish)

    run(
        go(),
        collect(pc, sems, ggate, s_gate, cgate),
        collect(pc, sems, gup, s_up, cup),
        collect(pc, sems, gdown, s_down, cdown),
        last(),
    )


def key_grads_kernel(chain, part, out, *rest):
    scratch, (send, recv) = rest[:5], rest[5:]
    sems = Sems(send, recv)
    pc = Place(chain)
    greet(pc)
    run(dp_reduce(pc, sems, part, scratch, out))


def end_kernel(chain, *refs):
    (part, gqkv, gwout, tok, middle_grad, gains, gain_two) = refs[:7]
    (input_grad, qkv_out, wout_out, gain_out) = refs[7:11]
    rest = refs[11:]
    s_part, s_qkv, s_out = rest[:6], rest[6:11], rest[11:16]
    total, gain_acc, by_group, stage, mid, second, send, recv = rest[16:]
    sems = Sems(send, recv)
    pc, near = Place(chain), Place(1)
    greet(pc)

    def go():
        yield from plane_reduce(near, sems, part, s_part, total)
        gain_acc[...] = jnp.zeros_like(gain_acc)

        def back(r):
            v = tok[r, :].astype(F32)
            root = unit(v)
            xhat = v * root
            g = total[r, :]
            e = g * gains[0:1, :]
            input_grad[r, :] = middle_grad[r, :] + root * (
                e - xhat * jnp.mean(e * xhat, axis=-1, keepdims=True)
            )
            gain_acc[...] += g * xhat

        each_rows(total.shape[0], back)
        own = jnp.sum(gain_acc[...], axis=0, keepdims=True)
        row = lax.broadcasted_iota(jnp.int32, (8, 128), 0)
        for j in range(by_group.shape[0]):
            cols = slice(j * 128, (j + 1) * 128)
            by_group[j] = jnp.where(row == 0, jnp.broadcast_to(own[:, cols], (8, 128)), gain_two[:, cols])
        yield from sum_gains(pc, sems, by_group, stage, mid, second, gain_out)

    run(
        go(),
        dp_reduce(pc, sems, gqkv, s_qkv, qkv_out),
        dp_reduce(pc, sems, gwout, s_out, wout_out),
    )


def attend_kernel(bounds, q, k, v, qseg, qpos, kseg, kmark, mixed, lse, bias):
    size = math_gcd(k.shape[0])
    rows = q.shape[0]
    scale = q.shape[1] ** -0.5

    @pl.when(pl.program_id(0) == 0)
    def _():
        def fill(j, carry):
            at = pl.multiple_of(j * size, size)
            cols = pl.ds(at, size)
            kpos = at + lax.broadcasted_iota(jnp.int32, (1, size), 1)
            same = kpos == qpos[...]
            allowed = (
                (kseg[:, cols] == qseg[...]) & (kpos <= qpos[...]) & ((kmark[:, cols] == 1) | same)
            )
            bias[:, cols] = jnp.where(allowed, 0.0, NEG)
            return carry

        lax.fori_loop(bounds[0], bounds[1], fill, 0)

    def step(j, carry):
        top, total, acc = carry
        cols = pl.ds(pl.multiple_of(j * size, size), size)
        scores = lax.dot_general(
            q[...], k[cols, :], (((1,), (1,)), ((), ())), preferred_element_type=F32
        ) * scale + bias[:, cols]
        new = jnp.maximum(top, jnp.max(scores, axis=1, keepdims=True))
        shrink = jnp.exp(top - new)
        probs = jnp.exp(scores - new)
        total = total * shrink + jnp.sum(probs, axis=1, keepdims=True)
        acc = acc * shrink + jnp.dot(probs.astype(BF), v[cols, :], preferred_element_type=F32)
        return new, total, acc

    top, total, acc = lax.fori_loop(
        bounds[0],
        bounds[1],
        step,
        (jnp.full((rows, 1), NEG, F32), jnp.zeros((rows, 1), F32), jnp.zeros((rows, q.shape[1]), F32)),
    )
    mixed[...] = acc / total
    lse[...] = top + jnp.log(total)


def math_gcd(n):
    size = 256
    while n % size:
        size //= 2
    return size


def attend(bounds, q, k, v, qseg, qpos, kseg, kmark):
    heads, rows, dim = q.shape
    keys = k.shape[0]

    def whole(shape):
        return pl.BlockSpec(shape, lambda h, b: (0, 0))

    def head(shape):
        return pl.BlockSpec((pl.Squeezed(),) + shape, lambda h, b: (h, 0, 0))

    return pl.pallas_call(
        attend_kernel,
        out_shape=[
            jax.ShapeDtypeStruct((heads, rows, dim), F32),
            jax.ShapeDtypeStruct((heads, rows, 1), F32),
        ],
        grid_spec=pltpu.PrefetchScalarGridSpec(
            num_scalar_prefetch=1,
            grid=(heads,),
            in_specs=[
                head((rows, dim)),
                whole((keys, dim)),
                whole((keys, dim)),
                whole((rows, 1)),
                whole((rows, 1)),
                whole((1, keys)),
                whole((1, keys)),
            ],
            out_specs=[head((rows, dim)), head((rows, 1))],
            scratch_shapes=[pltpu.VMEM((rows, keys), F32)],
        ),
        name="attend",
        compiler_params=pltpu.CompilerParams(vmem_limit_bytes=48 << 20),
    )(bounds, q, k, v, qseg, qpos, kseg, kmark)


def attend_back_kernel(bounds, q, dmix, lse, delta, k, v, qseg, qpos, kseg, kmark, dq, dk, dv, bias):
    size = math_gcd(k.shape[0])
    scale = q.shape[1] ** -0.5

    @pl.when(pl.program_id(0) == 0)
    def _():
        dk[...] = jnp.zeros_like(dk)
        dv[...] = jnp.zeros_like(dv)

        def fill(j, carry):
            at = pl.multiple_of(j * size, size)
            rows = pl.ds(at, size)
            kpos = at + lax.broadcasted_iota(jnp.int32, (size, 1), 0)
            same = kpos == qpos[...]
            allowed = (
                (kseg[rows, :] == qseg[...]) & (kpos <= qpos[...]) & ((kmark[rows, :] == 1) | same)
            )
            bias[rows, :] = jnp.where(allowed, 0.0, NEG)
            return carry

        lax.fori_loop(bounds[0], bounds[1], fill, 0)

    def step(j, acc):
        rows = pl.ds(pl.multiple_of(j * size, size), size)
        kb = k[rows, :]
        scores = (
            lax.dot_general(kb, q[...], (((1,), (1,)), ((), ())), preferred_element_type=F32) * scale
            + bias[rows, :]
        )
        probs = jnp.exp(scores - lse[...])
        pgrad = lax.dot_general(
            v[rows, :], dmix[...], (((1,), (1,)), ((), ())), preferred_element_type=F32
        )
        sgrad = (probs * (pgrad - delta[...])).astype(BF)
        dk[rows, :] += jnp.dot(sgrad, q[...], preferred_element_type=F32) * scale
        dv[rows, :] += jnp.dot(probs.astype(BF), dmix[...], preferred_element_type=F32)
        return acc + lax.dot_general(sgrad, kb, (((0,), (0,)), ((), ())), preferred_element_type=F32)

    acc = lax.fori_loop(bounds[0], bounds[1], step, jnp.zeros(dq.shape, F32))
    dq[...] = acc * scale


def attend_back(bounds, q, dmix, lse, delta, k, v, qseg, qpos, kseg, kmark):
    heads, rows, dim = q.shape
    keys = k.shape[0]

    def whole(shape):
        return pl.BlockSpec(shape, lambda h, b: (0, 0))

    def head(shape):
        return pl.BlockSpec((pl.Squeezed(),) + shape, lambda h, b: (h, 0, 0))

    return pl.pallas_call(
        attend_back_kernel,
        out_shape=[
            jax.ShapeDtypeStruct((heads, rows, dim), F32),
            jax.ShapeDtypeStruct((keys, dim), F32),
            jax.ShapeDtypeStruct((keys, dim), F32),
        ],
        grid_spec=pltpu.PrefetchScalarGridSpec(
            num_scalar_prefetch=1,
            grid=(heads,),
            in_specs=[
                head((rows, dim)),
                head((rows, dim)),
                head((1, rows)),
                head((1, rows)),
                whole((keys, dim)),
                whole((keys, dim)),
                whole((1, rows)),
                whole((1, rows)),
                whole((keys, 1)),
                whole((keys, 1)),
            ],
            out_specs=[head((rows, dim)), whole((keys, dim)), whole((keys, dim))],
            scratch_shapes=[pltpu.VMEM((keys, rows), F32)],
        ),
        name="attend_back",
        compiler_params=pltpu.CompilerParams(vmem_limit_bytes=56 << 20),
    )(bounds, q, dmix, lse, delta, k, v, qseg, qpos, kseg, kmark)


def angles(positions, half_dim):
    frequency = THETA ** (-jnp.arange(half_dim, dtype=F32) / half_dim)
    turned = positions.astype(F32)[:, None] * frequency[None, :]
    return jnp.cos(turned), jnp.sin(turned)


def rotate(values, cosine, sine):
    half = values.shape[-1] // 2
    a, b = values[..., :half], values[..., half:]
    cosine, sine = cosine[:, None, :], sine[:, None, :]
    return jnp.concatenate([a * cosine - b * sine, b * cosine + a * sine], axis=-1)


def mm(a, b):
    return jnp.dot(a, b, preferred_element_type=F32)


def mm_tn(a, b):
    return lax.dot_general(a, b, (((0,), (0,)), ((), ())), preferred_element_type=F32)


def mm_nt(a, b):
    return lax.dot_general(a, b, (((1,), (1,)), ((), ())), preferred_element_type=F32)


def shards(
    tokens,
    segment_ids,
    key_mask,
    attn_gain,
    w_query,
    w_key,
    w_value,
    w_out,
    mlp_gain,
    w_gate,
    w_up,
    w_down,
    cotangent,
):
    n_dp, n_t = lax.axis_size("dp"), lax.axis_size("tensor")
    chain = 4
    groups = n_dp // chain
    rows, width = tokens.shape
    local = rows * n_t
    total = local * n_dp
    dim = w_key.shape[1]
    heads = w_query.shape[1] // dim
    wrows = w_query.shape[0]
    units = w_gate.shape[1] // chain
    qkv = w_query.shape[1] + 2 * dim
    me = lax.axis_index("dp")
    first_row = me * local
    share = attn_gain.shape[0]
    tile = 128 // share

    own_gain = jnp.concatenate(
        [
            jnp.tile(attn_gain, tile)[None],
            jnp.tile(mlp_gain, tile)[None],
            jnp.zeros((6, 128), F32),
        ],
        axis=0,
    )
    wqkv = jnp.concatenate([w_query, w_key, w_value], axis=1)
    wout = w_out.T

    def by_chain(w):
        return w.reshape(wrows, chain, units).transpose(1, 0, 2)

    plane = chain * n_t * rows
    nbytes = 60 << 20
    (normed, gains, wqkv, wout, wgate, wup, wdown, cot) = call(
        functools.partial(gather_kernel, chain),
        "gather",
        0,
        [VM, VM] + [ANY] * 6,
        [
            ((1, n_t, rows, width), BF, ANY),
            ((8, width), F32, VM),
            ((n_dp, wrows, qkv), BF, ANY),
            ((n_dp, wrows, heads * dim), BF, ANY),
            ((n_dp, wrows, units), BF, ANY),
            ((n_dp, wrows, units), BF, ANY),
            ((n_dp, wrows, units), BF, ANY),
            ((chain, n_t, rows, width), BF, ANY),
        ],
        [pltpu.VMEM((n_dp, n_t, 8, 128), F32), pltpu.VMEM((rows, width), BF)],
        (tokens, own_gain, wqkv, wout, by_chain(w_gate), by_chain(w_up), by_chain(w_down.T), cotangent),
        nbytes,
    )
    normed = normed.reshape(local, width)
    wqkv = wqkv.reshape(width, qkv)
    wout = wout.reshape(width, heads * dim)
    wgate = wgate.reshape(width, units)
    wup = wup.reshape(width, units)
    wdown = wdown.reshape(width, units)
    cot = cot.reshape(plane, width)

    positions = first_row + jnp.arange(local, dtype=jnp.int32)
    cosine, sine = angles(positions, dim // 2)
    pre = mm(normed, wqkv)
    turned = rotate(pre[:, : (heads + 1) * dim].reshape(local, heads + 1, dim), cosine, sine).astype(BF)
    query = turned[:, :heads].transpose(1, 0, 2)
    own_kv = jnp.concatenate([turned[:, heads], pre[:, (heads + 1) * dim :].astype(BF)], axis=1)
    (kv,) = call(
        functools.partial(keys_kernel, chain),
        "keys",
        1,
        [ANY],
        [((n_dp, local, 2 * dim), BF, ANY)],
        [],
        (own_kv,),
        1 << 20,
    )
    kv = kv.reshape(total, 2 * dim)
    keys, values = kv[:, :dim], kv[:, dim:]
    own_segments = lax.dynamic_slice(segment_ids, (first_row,), (local,))
    size = math_gcd(total)
    start = jnp.sum((segment_ids < own_segments[0]).astype(jnp.int32))
    bounds = jnp.stack([start // size, (first_row + local + size - 1) // size])
    mixed, lse = attend(
        bounds,
        query,
        keys,
        values,
        own_segments[:, None],
        positions[:, None],
        segment_ids[None],
        key_mask[None],
    )
    mixed_low = mixed.transpose(1, 0, 2).reshape(local, heads * dim).astype(BF)
    part = mm_nt(mixed_low, wout).astype(BF).reshape(1, n_t, rows, width)
    middle, two = call(
        functools.partial(middle_kernel, chain),
        "middle",
        2,
        [VM, VM, VM],
        [((rows, width), F32, VM), ((chain, n_t, rows, width), BF, ANY)],
        plane_scratch(1, rows, width) + [pltpu.VMEM((rows, width), F32), pltpu.VMEM((rows, width), BF)],
        (part, tokens, gains),
        nbytes // 4,
    )

    two = two.reshape(plane, width)
    gate = mm(two, wgate)
    up = mm(two, wup)
    sigma = jax.nn.sigmoid(gate)
    silu = gate * sigma
    hidden = (silu * up).astype(BF)
    hidden_grad = mm(cot, wdown)
    gate_grad = (hidden_grad * up * sigma * (1.0 + gate * (1.0 - sigma))).astype(BF)
    up_grad = (hidden_grad * silu).astype(BF)
    npart = (mm_nt(gate_grad, wgate) + mm_nt(up_grad, wup)).astype(BF)
    opart = mm_nt(hidden, wdown).astype(BF)

    def by_dp(g):
        return g.astype(BF).reshape(n_dp, wrows, g.shape[1])

    ggate, gup, gdown = by_dp(mm_tn(two, gate_grad)), by_dp(mm_tn(two, up_grad)), by_dp(mm_tn(cot, hidden))
    block = ((chain, wrows, units), BF, ANY)
    (layer_out, middle_grad, branch, gain_two, ggate, gup, gdown) = call(
        functools.partial(back_kernel, chain),
        "back",
        3,
        [VM] * 8,
        [
            ((rows, width), BF, VM),
            ((rows, width), F32, VM),
            ((1, n_t, rows, width), BF, ANY),
            ((8, width), F32, VM),
            block,
            block,
            block,
        ],
        plane_scratch(chain, rows, width) * 2
        + collect_scratch(chain, groups, wrows, units) * 3
        + [
            pltpu.VMEM((rows, width), F32),
            pltpu.VMEM((rows, width), F32),
            pltpu.VMEM((rows, width), BF),
            pltpu.VMEM((16, width), F32),
        ],
        (
            npart.reshape(chain, n_t, rows, width),
            opart.reshape(chain, n_t, rows, width),
            ggate,
            gup,
            gdown,
            middle,
            cotangent,
            gains,
        ),
        nbytes,
    )

    def shard_of(g):
        return g.transpose(1, 0, 2).reshape(wrows, chain * units).astype(F32)

    grad_gate, grad_up, grad_down = shard_of(ggate), shard_of(gup), shard_of(gdown).T

    branch = branch.reshape(local, width)
    gwout = by_dp(mm_tn(branch, mixed_low))
    mixed_grad = mm(branch, wout).astype(BF).reshape(local, heads, dim).transpose(1, 0, 2)
    delta = jnp.sum(mixed_grad.astype(F32) * mixed, axis=-1)
    dq, dk, dv = attend_back(
        bounds,
        query,
        mixed_grad,
        lse.reshape(heads, 1, local),
        delta.reshape(heads, 1, local),
        keys,
        values,
        own_segments[None],
        positions[None],
        segment_ids[:, None],
        key_mask[:, None],
    )
    dkv = jnp.concatenate([dk, dv], axis=1).astype(BF).reshape(n_dp, local, 2 * dim)
    (dkv,) = call(
        functools.partial(key_grads_kernel, chain),
        "key_grads",
        4,
        [VM],
        [((local, 2 * dim), F32, VM)],
        dp_scratch(chain, groups, local, 2 * dim),
        (dkv,),
        2 << 20,
    )
    turn = jnp.concatenate([dq.transpose(1, 0, 2), dkv[:, None, :dim]], axis=1)
    back = rotate(turn, cosine, -sine).reshape(local, (heads + 1) * dim)
    qkv_grad = jnp.concatenate([back, dkv[:, dim:]], axis=1).astype(BF)
    gqkv = by_dp(mm_tn(normed, qkv_grad))
    part = mm_nt(qkv_grad, wqkv).astype(BF).reshape(1, n_t, rows, width)
    count = max(1, n_t * share // 128)
    input_grad, gqkv, gwout, gain_sum = call(
        functools.partial(end_kernel, chain),
        "end",
        5,
        [VM] * 7,
        [
            ((rows, width), F32, VM),
            ((wrows, qkv), F32, VM),
            ((wrows, heads * dim), F32, VM),
            ((8, 128), F32, VM),
        ],
        plane_scratch(1, rows, width)
        + dp_scratch(chain, groups, wrows, qkv)
        + dp_scratch(chain, groups, wrows, heads * dim)
        + [
            pltpu.VMEM((rows, width), F32),
            pltpu.VMEM((16, width), F32),
            pltpu.VMEM((width // 128, 8, 128), F32),
            pltpu.VMEM((n_dp, count, 8, 128), F32),
            pltpu.VMEM((count, 8, 128), F32),
            pltpu.VMEM((n_t, 8, 128), F32),
        ],
        (part, gqkv, gwout, tokens, middle_grad, gains, gain_two),
        nbytes // 2,
    )
    lane = (me * n_t + lax.axis_index("tensor")) * share % 128
    gain_grads = lax.dynamic_slice(gain_sum, (0, lane), (2, share))
    return (
        layer_out,
        input_grad,
        gain_grads[0],
        gqkv[:, : heads * dim],
        gqkv[:, heads * dim : (heads + 1) * dim],
        gqkv[:, (heads + 1) * dim :],
        gwout.T,
        gain_grads[1],
        grad_gate,
        grad_up,
        grad_down,
    )


def solution(mesh):
    in_specs = (
        P(("dp", "tensor"), None),
        P(),
        P(),
        P(("dp", "tensor")),
        P("dp", "tensor"),
        P("dp", "tensor"),
        P("dp", "tensor"),
        P("tensor", "dp"),
        P(("dp", "tensor")),
        P("dp", "tensor"),
        P("dp", "tensor"),
        P("tensor", "dp"),
        P(("dp", "tensor"), None),
    )
    out_specs = (
        P(("dp", "tensor"), None),
        P(("dp", "tensor"), None),
        P(("dp", "tensor")),
        P("dp", "tensor"),
        P("dp", "tensor"),
        P("dp", "tensor"),
        P("tensor", "dp"),
        P(("dp", "tensor")),
        P("dp", "tensor"),
        P("dp", "tensor"),
        P("tensor", "dp"),
    )
    return jax.shard_map(shards, mesh=mesh, in_specs=in_specs, out_specs=out_specs, check_vma=False)
```

time: 1640 us -> 670 us (0.41)
  waiting for transfers between devices: 1130 us -> 0 us
  Pallas kernels: 0 us -> 533 us
  blocking collectives: 210 us -> 0 us
  loops' own time: 64.4 us -> 0 us
  matrix products: 102 us -> 58.5 us
  local copies, waits for them, and re-layouts: 73.9 us -> 52.9 us
  other arithmetic: 34.4 us -> 16.1 us
    reduce_scatter x11 -> x0, waiting for transfers between devices: 679 us -> none  [the longest x4 129 us: spread_rows(): lax.psum_scatter(term_fn(jnp.int32(0), row_count * lax.axis_size('tensor'...]
    pallas_call x0 -> x8, Pallas kernels: none -> 533 us  [the longest x6 510 us: call(): pl.pallas_call(kernel, out_shape=[jax.ShapeDtypeStruct(shape, kind) for s...]
    all_gather x9 -> x0, waiting for transfers between devices: 323 us -> none  [the longest x1 95.9 us: shards(): lax.all_gather(w_down.T, 'dp', axis=0, tiled=True)]
    all_gather x4 -> x0, blocking collectives: 129 us -> none  [the longest x1 34 us: shards(): lax.all_gather(value_rows, 'dp', axis=0, tiled=True)]
    unnamed x22 -> x0, waiting for transfers between devices: 124 us -> none
    unnamed x2 -> x0, blocking collectives: 81.8 us -> none
    another operation x24 -> x0, loops' own time: 64.4 us -> none  [the longest x1 16.7 us: shards(): lax.scan(stats_step, start_stats, scan_items)]
    dot_general x30 -> x15, matrix products: 102 us -> 58.5 us  [the longest x5 22.3 us: mm_tn(): lax.dot_general(a, b, (((0,), (0,)), ((), ())), preferred_element_type=F32)]
  transfers between devices with their start and end apart: 21 -> 0, of which waited for: 17 -> 0; matrix products, arithmetic and copies ran while one was open for 7% -> 0% of each run, Pallas kernels for 0% -> 0%
where the time goes in v1:
time: 670 us; the launch traced here: 665 us
  Pallas kernels  533 us (80%)
  matrix products  58.5 us (9%)
  local copies, waits for them, and re-layouts  52.9 us (8%)
  other arithmetic  16.1 us (2%)
    pallas_call x6, Pallas kernels, call(): pl.pallas_call(kernel, out_shape=[jax.ShapeDtypeStruct(shape, kind) for s...  510 us
    dot_general x5, matrix products, mm_tn(): lax.dot_general(a, b, (((0,), (0,)), ((), ())), preferred_element_type=F32)  22.3 us
    dot_general x5, matrix products, mm_nt(): lax.dot_general(a, b, (((1,), (1,)), ((), ())), preferred_element_type=F32)  21 us
    unnamed x94, local copies, waits for them, and re-layouts  18 us
    dot_general x5, matrix products, mm(): return jnp.dot(a, b, preferred_element_type=F32)  15.2 us
    pallas_call x1, Pallas kernels, attend_back(): pl.pallas_call(attend_back_kernel, out_shape=[jax.ShapeDtypeStruct((heads...  14.3 us

profile of v1, /device:TPU:0, one launch (start us, length us, event | category | flops | bytes accessed | tf_op | source)
XLA Modules:
  0.0 665.3 jit_solution(14263771933774446851)
XLA Ops:
  2.0 2.0 convert_reduce_fusion
  6.7 1.4 copy.36
  8.1 1.2 copy.37
  9.6 1.2 copy.39
  10.7 1.2 copy.40
  14.7 151.1 %gather.1 = (bf16[1,4,80,2048]{3,2,1,0:T(8,128)(2,1)}, f32[8,2048]{1,0:T(8,128)}, bf16[8,256,640]{2,1,0:T(8,128)(2,1)}, bf16[8,256,512]{2,1,0:T(8,128)(2,1)}, bf...) custom-call(bf16[80,2048]{1,0:T(8,128)(2,1)} %refs_3_.1, ...), custom_call_target="tpu_custom_call" | custom-call | bytes 62914560 | tf_op jit(solution)/shard_map/gather/pallas_call | solution.py:595
  165.9 3.3 fusion.11
  170.6 1.6 copy.65
  172.2 1.3 fusion.4
  173.6 1.8 add_convert_fusion.2
  177.2 21.1 %keys.1 = bf16[8,320,128]{2,1,0:T(8,128)(2,1)} custom-call(bf16[320,128]{1,0:T(8,128)(2,1)} %pad_maximum_fusion.8.own), custom_call_target="tpu_custom_call" | custom-call | bytes 1048576 | tf_op jit(solution)/shard_map/keys/pallas_call | solution.py:595
  198.3 1.6 fusion.9
  200.7 9.5 %attend.1 = (f32[8,320,64]{2,1,0:T(8,128)S(1)}, f32[8,320,1]{2,1,0:T(8,128)S(1)}) custom-call(s32[2]{0:T(128)S(1)} %pad_add_fusion.bounds, bf16[8,320,64]{2,1,0:T(8,128)(2,1)S(1)} %fusion.2.q, bf16[2560,64]{1,0:T(8,128)(2,1)S(1)} %get-tuple-element.97.k, bf16[2560,64]{1,0:T(8,128)(2,1)S(1)} %get-tuple-element.96.v, s32[320,1]{1,0:T(8,128)S(1)} %broadcast_in_dim.40.qseg, ...), custom_call_target="tpu_custom_call" | custom-call | tf_op jit(solution)/shard_map/attend/pallas_call | solution.py:830
  210.3 1.0 copy-done.3
  211.7 3.8 convolution_convert_fusion.7
  215.6 68.5 %middle.1 = (f32[80,2048]{1,0:T(8,128)}, bf16[4,4,80,2048]{3,2,1,0:T(8,128)(2,1)}) custom-call(bf16[1,4,80,2048]{3,2,1,0:T(8,128)(2,1)} %bitcast.120, bf16[80,2048]{1,0:T(8,128)(2,1)} %refs_3_.1, f32[8,2048]{1,0:T(8,128)} %get-tuple-element.43.gains.refs_7_.refs_5_), custom_call_target="tpu_custom_call" | custom-call | bytes 15728640 | tf_op jit(solution)/shard_map/middle/pallas_call | solution.py:595
  284.1 4.7 fusion.12
  288.9 2.1 fusion.10
  291.0 4.3 multiply_convert_fusion
  296.3 3.1 convolution_convert_fusion.4
  299.4 2.5 copy.47
  301.9 5.9 convolution_convert_fusion.5
  307.8 2.7 copy.46
  310.6 5.9 convolution_convert_fusion.3
  316.5 2.6 copy.48
  319.0 7.0 %convolution_convert_fusion = bf16[1280,2048]{1,0:T(8,128)(2,1)} fusion(bf16[1280,352]{0,1:T(8,128)(2,1)} %get-tuple-element.85, bf16[2048,352]{1,0:T(8,128)(2,1)} %bitcast.143), kind=kOutput, calls=%fused_computation.1 | convolution fusion | flops 1848115200 | bytes 7585792 | tf_op jit(solution)/shard_map/dot_general | solution.py:960
  326.1 3.0 fusion.13
  329.0 4.8 add_convert_fusion
  333.8 140.9 %back.1 = (bf16[80,2048]{1,0:T(8,128)(2,1)}, f32[80,2048]{1,0:T(8,128)}, bf16[1,4,80,2048]{3,2,1,0:T(8,128)(2,1)}, f32[8,2048]{1,0:T(8,128)}, bf16[4,256,352]{2,...) custom-call(bf16[4,4,80,2048]{3,2,1,0:T(8,128)(2,1)} %bitcast.93, ...), custom_call_target="tpu_custom_call" | custom-call | bytes 62914560 | tf_op jit(solution)/shard_map/back/pallas_call | solution.py:595
  474.8 2.8 convert_bitcast_fusion
  477.6 3.0 copy.57
  480.5 2.9 copy.63
  483.4 1.6 copy.58
  485.0 4.1 convolution_convert_fusion.2
  490.9 1.4 copy.50
  495.7 2.0 broadcast_in_dim.41.kseg
  497.6 2.0 broadcast_in_dim.42.kmark
  499.6 14.3 %attend_back.1 = (f32[8,320,64]{2,1,0:T(8,128)}, f32[2560,64]{1,0:T(8,128)}, f32[2560,64]{1,0:T(8,128)}) custom-call(s32[2]{0:T(128)} %copy-done.5, bf16[8,320,64]{2,1,0:T(8,128)(2,1)} %copy-done.2, bf16[8,320,64]{2,1,0:T(8,128)(2,1)} %bitcast.98, f32[8,1,320]{2,1,0:T(1,128)} %reshape.246.lse, f32[8,1,320]{2,1,0:T(1,128)} %reshape.238.delta, ...), custom_call_target="tpu_custom_call" | custom-call | tf_op jit(solution)/shard_map/attend_back/pallas_call | solution.py:908
  513.9 1.5 convert.39
  515.7 1.2 pad_maximum_fusion.2.part
  516.9 46.2 %key_grads.1 = f32[320,128]{1,0:T(8,128)} custom-call(bf16[8,320,128]{2,1,0:T(8,128)(2,1)} %pad_maximum_fusion.2.part), custom_call_target="tpu_custom_call" | custom-call | bytes 2097152 | tf_op jit(solution)/shard_map/key_grads/pallas_call | solution.py:595
  566.0 3.2 convolution_convert_fusion.1
  569.3 2.3 convolution_convert_fusion.6
  571.6 81.7 %end.1 = (f32[80,2048]{1,0:T(8,128)}, f32[256,640]{1,0:T(8,128)}, f32[256,512]{1,0:T(8,128)}, f32[8,128]{1,0:T(8,128)}) custom-call(bf16[1,4,80,2048]{3,2,1,0:T(8,128)(2,1)} %bitcast.119, bf16[8,256,640]{2,1,0:T(8,128)(2,1)} %bitcast.108, bf16[8,256,512]{2,1,0:T(8,128)(2,1)} %bitcast.111, bf16[80,2048]{1,0:T(8,128)(2,1)} %refs_3_.1, ...), custom_call_target="tpu_custom_call" | custom-call | bytes 31457280 | tf_op jit(solution)/shard_map/end/pallas_call | solution.py:595
  653.4 2.1 copy.61
  655.5 1.9 slice.70
  658.6 1.1 fusion.8
  661.7 1.5 copy.62
  (134 shorter events, 23.1 us)
Async XLA Ops:
  0.6 8.6 %copy-start.18 = (bf16[256,1408]{1,0:T(8,128)(2,1)S(1)}, bf16[256,1408]{1,0:T(8,128)(2,1)}, u32[]{:S(2)}) copy-start(bf16[256,1408]{1,0:T(8,128)(2,1)} %param.23) | copy-start | bytes 2162692
  6.7 194.0 %copy-start.5 = (s32[2]{0:T(128)}, s32[2]{0:T(128)S(1)}, u32[]{:S(2)}) copy-start(s32[2]{0:T(128)S(1)} %pad_add_fusion.bounds) | copy-start | bytes 28
  9.2 1.5 copy-start.19
  9.5 2.4 copy-start.27
  9.5 2.5 copy-start.28
  9.6 2.6 copy-start.24
  10.7 2.2 copy-start.23
  10.7 3.1 copy-start.34
  10.7 3.2 copy-start.35
  169.2 0.9 copy-start.13
  199.9 10.4 %copy-start = (bf16[2560,64]{1,0:T(8,128)(2,1)}, bf16[2560,64]{1,0:T(8,128)(2,1)S(1)}, u32[]{:S(2)}) copy-start(bf16[2560,64]{1,0:T(8,128)(2,1)S(1)} %get-tuple-element.96.v) | copy-start | bytes 983044
  199.9 10.4 %copy-start.1 = (bf16[2560,64]{1,0:T(8,128)(2,1)}, bf16[2560,64]{1,0:T(8,128)(2,1)S(1)}, u32[]{:S(2)}) copy-start(bf16[2560,64]{1,0:T(8,128)(2,1)S(1)} %get-tuple-element.97.k) | copy-start | bytes 983044
  199.9 0.8 copy-start.25
  199.9 0.8 copy-start.26
  200.3 11.1 %copy-start.2 = (bf16[8,320,64]{2,1,0:T(8,128)(2,1)}, bf16[8,320,64]{2,1,0:T(8,128)(2,1)S(1)}, u32[]{:S(2)}) copy-start(bf16[8,320,64]{2,1,0:T(8,128)(2,1)S(1)} %fusion.2.q) | copy-start | bytes 983044
  210.3 1.1 copy-start.3
  215.6 68.5 %copy-start.7 = (bf16[8,256,352]{2,1,0:T(8,128)(2,1)S(1)}, bf16[8,256,352]{2,1,0:T(8,128)(2,1)}, u32[]{:S(2)}) copy-start(bf16[8,256,352]{2,1,0:T(8,128)(2,1)} %get-tuple-element.46) | copy-start | bytes 4325380
  215.6 73.3 %slice-start = ((s8[5242880]{0:T(1024)(128)(4,1)}), s8[1048576]{0:T(1024)(128)(4,1)S(1)}, s32[]{:S(2)}) async-start(s8[5242880]{0:T(1024)(128)(4,1)} %bitcast.130), calls=%async_computation | async-start | bytes 2097152
  284.1 4.8 slice-start.1
  284.1 4.8 copy-start.31
  284.1 6.9 %slice-start.2 = ((s8[5242880]{0:T(1024)(128)(4,1)}), s8[4194304]{0:T(1024)(128)(4,1)S(1)}, s32[]{:S(2)}) async-start(s8[5242880]{0:T(1024)(128)(4,1)} %bitcast.135), calls=%async_computation.2 | async-start | bytes 8388608
  288.8 2.2 slice-start.3
  288.9 2.1 copy-start.8
  295.3 1.0 copy-start.15
  319.0 7.0 %copy-start.14 = (bf16[1280,352]{0,1:T(8,128)(2,1)S(1)}, bf16[1280,352]{0,1:T(8,128)(2,1)}, u32[]{:S(2)}) copy-start(bf16[1280,352]{0,1:T(8,128)(2,1)} %get-tuple-element.86) | copy-start | bytes 2703364
  326.1 3.0 copy-start.9
  326.1 3.0 copy-start.16
  485.0 4.1 copy-start.30
  485.0 4.1 copy-start.33
  490.9 2.6 copy-start.4
  492.3 1.6 copy-start.6
  513.9 1.7 copy-start.11
  515.7 48.3 %copy-start.10 = (f32[8,320,64]{2,1,0:T(8,128)S(1)}, f32[8,320,64]{2,1,0:T(8,128)}, u32[]{:S(2)}) copy-start(f32[8,320,64]{2,1,0:T(8,128)} %get-tuple-element.51) | copy-start | bytes 1966084
  515.7 48.3 %copy-start.20 = (f32[320,32]{1,0:T(8,128)S(1)}, f32[320,32]{1,0:T(8,128)}, u32[]{:S(2)}) copy-start(f32[320,32]{1,0:T(8,128)} %get-tuple-element.98) | copy-start | bytes 122884
  564.6 0.9 copy-start.12
  564.6 1.4 copy-start.32
  566.0 3.2 copy-start.29
  653.4 7.8 %copy-start.17 = (bf16[4,256,352]{2,1,0:T(8,128)(2,1)S(1)}, bf16[4,256,352]{2,1,0:T(8,128)(2,1)}, u32[]{:S(2)}) copy-start(bf16[4,256,352]{2,1,0:T(8,128)(2,1)} %get-tuple-element.60) | copy-start | bytes 2162692
  661.7 1.6 copy-start.22
  661.7 2.3 copy-start.21

commit v2 on v1

--- a/solution.py
+++ b/solution.py
@@ -18,7 +18,7 @@
 
 
 def sem_count():
-    return 128 + 8 * lax.axis_size("dp")
+    return 200 + 12 * lax.axis_size("dp")
 
 
 class Sems:
@@ -118,14 +118,44 @@
 def run(*tasks):
     live = list(tasks)
     while live:
-        left = []
-        for task in live:
-            try:
-                next(task)
-                left.append(task)
-            except StopIteration:
-                pass
-        live = left
+        live = [task for task in live if next(task, "end") != "end"]
+
+
+def pipeline(tasks):
+    next(tasks[0])
+    next(tasks[0])
+    yield
+    for i, task in enumerate(tasks):
+        ahead = i + 1 < len(tasks)
+        while next(task, "tail") != "tail":
+            if ahead:
+                next(tasks[i + 1])
+                next(tasks[i + 1])
+                ahead = False
+            yield
+        if ahead:
+            next(tasks[i + 1])
+            next(tasks[i + 1])
+        yield
+    for task in tasks:
+        for _ in task:
+            yield
+
+
+class Behind:
+    def __init__(self, task):
+        self.task = task
+
+    def __call__(self, steps=1):
+        for _ in range(steps):
+            next(self.task, None)
+
+    def along(self, task, steps=1):
+        for _ in task:
+            self(steps)
+
+    def drain(self):
+        run(self.task)
 
 
 def chain_steps(pc):
@@ -155,12 +185,15 @@
     keep = cp.keep(base, own, out.at[z, s])
     for p in range(parts):
         src = own.at[:, pl.ds(p * width, width)]
+        cp.go(sem(2, 0, p), src, view(z, s, p), pc.at(s=pc.sy))
+        cp.go(sem(4, 0, p), src, view(z, s, p), pc.at(s=pc.sc))
+    yield "own"
+    for p in range(parts):
+        src = own.at[:, pl.ds(p * width, width)]
         if chain > 1:
             cp.go(sem(0, 0, p), src, view(z, s, p), pc.above, z + 1 < chain)
             cp.go(sem(1, 0, p), src, view(z, s, p), pc.below, z > 0)
-        cp.go(sem(2, 0, p), src, view(z, s, p), pc.at(s=pc.sy))
-        cp.go(sem(4, 0, p), src, view(z, s, p), pc.at(s=pc.sc))
-    yield
+    yield "start"
     crossing = [(z, None, 0, p) for p in range(parts)]
     landed = []
 
@@ -185,10 +218,11 @@
                 cp.go(sem(4, i, p), view(b, s, p), view(b, s, p), pc.at(s=pc.sc), got)
                 crossing.append((b, got, i, p))
             cross(1 if k == 0 else 2)
-            yield
+            yield "more"
+    yield "tail"
     while crossing:
         cross(2)
-        yield
+        yield "more"
     for b, got, i, p in landed:
         cp.arrive(sem(4, i, p), view(b, pc.sc, p), pc.at(), got)
         cp.arrive(sem(6, i, p), view(b, pc.so, p), pc.at(), got)
@@ -299,17 +333,16 @@
     def cols_of(p):
         return pl.ds(p * width, width)
 
-    for j, b, p in todo:
-        for over in (1, 0):
-            col = pc.so if over else pc.sc
+    def pass_core(over):
+        for j, b, p in todo:
             cp.go(
                 sem(over, j, p),
-                part.at[b, col, :, cols_of(p)],
+                part.at[b, pc.so if over else pc.sc, :, cols_of(p)],
                 crecv.at[b, over, :, cols_of(p)],
                 pc.at(s=pc.sc),
             )
-    yield
-    for j, b, p in todo:
+
+    def cross(j, b, p):
         cols = cols_of(p)
         cp.arrive(sem(1, j, p), crecv.at[b, 1, :, cols], pc.at())
 
@@ -318,11 +351,21 @@
 
         each_rows(count, add)
         cp.go(sem(2, j, p), csum.at[b, :, cols], yrecv.at[b, :, cols], pc.at(s=pc.sy))
+
+    pass_core(1)
+    yield
+    ahead = list(todo)
+    for _ in range(min(2, len(ahead))):
+        cross(*ahead.pop(0))
         yield
+    pass_core(0)
+    yield
     for j, b, p in todo:
         cols = cols_of(p)
         cp.arrive(sem(0, j, p), crecv.at[b, 0, :, cols], pc.at())
         cp.arrive(sem(2, j, p), yrecv.at[b, :, cols], pc.at())
+        if ahead:
+            cross(*ahead.pop(0))
 
         def value(r):
             return (
@@ -361,12 +404,13 @@
     along = (base + 1, base + 1 + chain)
     across = base + 1 + 2 * chain
     keep = cp.keep(base, own, out(pc.d))
+    for g in range(1, groups):
+        cp.go(across + g, own, out(pc.d), pc.at(t=(t + g) % groups))
+    yield "own"
     if chain > 1:
         cp.go(along[0], own, out(pc.d), pc.above, z + 1 < chain)
         cp.go(along[1], own, out(pc.d), pc.below, z > 0)
-    for g in range(1, groups):
-        cp.go(across + g, own, out(pc.d), pc.at(t=(t + g) % groups))
-    yield
+    yield "start"
     landed = [(z, None, 0)]
     for k, side, b, got, onward, more in chain_steps(pc):
         i = 1 + k if side == 0 else chain + k
@@ -377,7 +421,8 @@
         for g in range(1, groups):
             cp.go(across + i * groups + g, block, block, pc.at(t=(t + g) % groups), got)
         landed.append((b, got, i))
-        yield
+        yield "more"
+    yield "tail"
     for b, got, i in landed:
         for g in range(1, groups):
             cp.arrive(across + i * groups + g, out(b * groups + (t - g + groups) % groups), pc.at(), got)
@@ -392,18 +437,20 @@
     base = sems.take(1 + chain + chain * groups)
     along, across = base + 1, base + 1 + chain
     keep = cp.keep(base, blocks(z), out(pc.d))
+    for g in range(1, groups):
+        cp.go(across + g, blocks(z), out(pc.d), pc.at(t=(t + g) % groups))
+    yield "own"
     for k in range(1, chain):
         to = (z + k) % chain
         cp.go(along + k, blocks(to), out(pc.d), pc.at(z=to))
-    for g in range(1, groups):
-        cp.go(across + g, blocks(z), out(pc.d), pc.at(t=(t + g) % groups))
-    yield
+    yield "start"
     for k in range(1, chain):
         block = out((z - k + chain) % chain * groups + t)
         cp.arrive(along + k, block, pc.at())
         for g in range(1, groups):
             cp.go(across + k * groups + g, block, block, pc.at(t=(t + g) % groups))
-        yield
+        yield "more"
+    yield "tail"
     for k in range(chain):
         for g in range(1, groups):
             block = out((z - k + chain) % chain * groups + (t - g + groups) % groups)
@@ -413,25 +460,33 @@
     yield
 
 
-def side_sums(pc, cp, across, part, xrecv, csum, count, order):
-    chain, groups, t = pc.chain, pc.groups, pc.t
-    for j, b in order:
+def side_sums(pc, cp, bases, parts, recvs, order, put, window=2):
+    groups, t = pc.groups, pc.t
+    todo = [(m, j, b) for m in range(len(parts)) for j, b in order]
+
+    def send(m, j, b):
         for g in range(1, groups):
             to = (t + g) % groups
-            cp.go(across + j * groups + g, part.at[b * groups + to], xrecv.at[g - 1, b], pc.at(t=to))
-    yield
-    for j, b in order:
+            cp.go(bases[m] + j * groups + g, parts[m].at[b * groups + to], recvs[m].at[g - 1, b], pc.at(t=to))
+
+    ahead = list(todo)
+    for _ in range(min(window, len(ahead))):
+        send(*ahead.pop(0))
+    yield None
+    for m, j, b in todo:
         for g in range(1, groups):
-            cp.arrive(across + j * groups + g, xrecv.at[g - 1, b], pc.at())
+            cp.arrive(bases[m] + j * groups + g, recvs[m].at[g - 1, b], pc.at())
+        if ahead:
+            send(*ahead.pop(0))
 
         def add(r):
-            total = part[b * groups + t, r, :].astype(F32)
+            total = parts[m][b * groups + t, r, :].astype(F32)
             for g in range(1, groups):
-                total = total + xrecv[g - 1, b, r, :].astype(F32)
-            csum(b, r, total)
-
-        each_rows(count, add)
-        yield j, b
+                total = total + recvs[m][g - 1, b, r, :].astype(F32)
+            put(m, b, r, total)
+
+        each_rows(parts[m].shape[1], add)
+        yield m, j, b
 
 
 def dp_scratch(chain, groups, rows, width):
@@ -444,25 +499,25 @@
     ]
 
 
-def dp_reduce(pc, sems, part, scratch, out):
-    xrecv, sums, zsend, lrecv, rrecv = scratch
+def dp_reduce(pc, sems, parts, scratches, outs):
     chain, groups, z = pc.chain, pc.groups, pc.z
-    count = out.shape[0]
     cp = Copies(sems)
-    base = sems.take(chain * groups + 2 * chain)
-    right = base + chain * groups
-    left = right + chain
+    count = len(parts)
+    bases = [sems.take(chain * groups) for _ in range(count)]
+    ups = [sems.take(chain) for _ in range(count)]
+    downs = [sems.take(chain) for _ in range(count)]
     order = [(j, far_first(chain, z, j)) for j in range(chain)]
-    cols = pl.ds(0, out.shape[1])
-
-    def csum(b, r, total):
-        sums[b, r, :] = total
-
-    for made in side_sums(pc, cp, base, part, xrecv, csum, count, order):
+
+    def put(m, b, r, total):
+        scratches[m][1][b, r, :] = total
+
+    for made in side_sums(pc, cp, bases, parts, [s[0] for s in scratches], order, put):
         if made is None:
             yield
             continue
-        j, b = made
+        m, j, b = made
+        _, sums, zsend, lrecv, rrecv = scratches[m]
+        out = outs[m]
 
         def value(r):
             return sums[b, r, :]
@@ -471,7 +526,19 @@
             out[r, :] = out[r, :] + term if more else term
 
         chain_reduce(
-            pc, cp, right + b, left + b, b, j == chain - 1, value, zsend, lrecv, rrecv, store, count, cols
+            pc,
+            cp,
+            ups[m] + b,
+            downs[m] + b,
+            b,
+            j == chain - 1,
+            value,
+            zsend,
+            lrecv,
+            rrecv,
+            store,
+            out.shape[0],
+            pl.ds(0, out.shape[1]),
         )
         yield
     cp.finish()
@@ -485,32 +552,35 @@
     ]
 
 
-def collect(pc, sems, part, scratch, out):
-    xrecv, sums = scratch
+def collect(pc, sems, parts, scratches, outs):
     chain, groups, z = pc.chain, pc.groups, pc.z
-    count = part.shape[1]
+    count = len(parts)
     cp = Copies(sems)
-    base = sems.take(chain * groups + chain)
-    along = base + chain * groups
+    bases = [sems.take(chain * groups) for _ in range(count)]
+    along = [sems.take(chain) for _ in range(count)]
     order = [(k, (z + chain - 1 - k) % chain) for k in range(chain)]
-
-    def csum(b, r, total):
-        sums[b, r, :] = total.astype(BF)
-
-    for made in side_sums(pc, cp, base, part, xrecv, csum, count, order):
+    kept = []
+
+    def put(m, b, r, total):
+        scratches[m][1][b, r, :] = total.astype(BF)
+
+    for made in side_sums(pc, cp, bases, parts, [s[0] for s in scratches], order, put, 3):
         if made is None:
             yield
             continue
-        k, b = made
+        m, k, b = made
+        block = scratches[m][1].at[b]
         if k < chain - 1:
-            cp.go(along + k, sums.at[b], out.at[z], pc.at(z=b))
+            cp.go(along[m] + k, block, outs[m].at[z], pc.at(z=b))
         else:
-            keep = cp.keep(along + k, sums.at[b], out.at[z])
+            kept.append(cp.keep(along[m] + k, block, outs[m].at[z]))
         yield
-    for k in range(chain - 1):
-        b = (z - (chain - 1 - k) + chain) % chain
-        cp.arrive(along + k, out.at[b], pc.at())
-    keep.wait()
+    for m in range(count):
+        for k in range(chain - 1):
+            b = (z - (chain - 1 - k) + chain) % chain
+            cp.arrive(along[m] + k, outs[m].at[b], pc.at())
+    for copy in kept:
+        copy.wait()
     cp.finish()
     yield
 
@@ -610,12 +680,148 @@
     return lax.rsqrt(jnp.mean(v * v, axis=-1, keepdims=True) + EPS)
 
 
-def gather_kernel(chain, *refs):
-    (tok, own_gain, wqkv, wout, wgate, wup, wdown, cot) = refs[:8]
-    (normed_all, gains, wqkv_all, wout_all, wgate_all, wup_all, wdown_all, cot_all) = refs[8:16]
-    table, normed, send, recv = refs[16:]
+def gcd_of(n, size):
+    while n % size:
+        size //= 2
+    return size
+
+
+def rows_of(ref, count):
+    return lambda d: ref.at[pl.ds(pl.multiple_of(d * count, count), count)]
+
+
+def halves():
+    lane = lax.broadcasted_iota(jnp.int32, (1, 128), 1)
+    return lane < 64
+
+
+def turn(x, cosine, sine):
+    lane = lax.broadcasted_iota(jnp.int32, x.shape, 1)
+    swapped = jnp.where(lane % 64 < 32, pltpu.roll(x, 96, 1), pltpu.roll(x, 32, 1))
+    return x * cosine + swapped * sine
+
+
+def key_range(first, count, total, size):
+    long_end = 5 * total // 8
+    low = jnp.where(first >= long_end + total // 32 - 16, long_end, 0)
+    return low // size, (first + count + size - 1) // size
+
+
+def fill_bias(bias, low, high, size, qseg, qpos, kseg, kmark):
+    def fill(j, carry):
+        at = pl.multiple_of(j * size, size)
+        cols = pl.ds(at, size)
+        kpos = at + lax.broadcasted_iota(jnp.int32, (1, size), 1)
+        allowed = (
+            (kseg[:, cols] == qseg[...])
+            & (kpos <= qpos[...])
+            & ((kmark[:, cols] == 1) | (kpos == qpos[...]))
+        )
+        bias[:, cols] = jnp.where(allowed, 0.0, NEG)
+        return carry
+
+    lax.fori_loop(low, high, fill, 0)
+
+
+def spread_lanes(kv, kk, vv):
+    size = gcd_of(kv.shape[0], 256)
+    left = lax.broadcasted_iota(jnp.int32, (size, 128), 1) < 64
+
+    def body(j, carry):
+        r = pl.ds(pl.multiple_of(j * size, size), size)
+        x = kv[r, :].astype(F32)
+        y = pltpu.roll(x, 64, 1)
+        kk[r, :] = jnp.where(left, x, y).astype(BF)
+        vv[r, :] = jnp.where(left, y, x).astype(BF)
+        return carry
+
+    lax.fori_loop(0, kv.shape[0] // size, body, 0)
+
+
+def attend(pc, query, kk, vv, bias, mixed, mixed_low, lse, step):
+    local, total = query.shape[0], kk.shape[0]
+    size = gcd_of(total, 256)
+    tile = local // 2
+    left = lax.broadcasted_iota(jnp.int32, (tile, 128), 1) < 64
+    lane = lax.broadcasted_iota(jnp.int32, (tile, 128), 1)
+    even = jnp.where(halves(), 1.0, 0.0).astype(BF)
+    odd = jnp.where(halves(), 0.0, 1.0).astype(BF)
+    for i in range(local // tile):
+        rows = slice(i * tile, (i + 1) * tile)
+        low, high = key_range(pc.d * local + i * tile, tile, total, size)
+        stats = jnp.zeros((tile, 128), F32)
+        for chunk in range(query.shape[1] // 128):
+            lanes = slice(chunk * 128, (chunk + 1) * 128)
+            both = query[rows, lanes]
+            heads = (both * even, both * odd)
+
+            def body(j, carry):
+                cols = pl.ds(pl.multiple_of(j * size, size), size)
+                key, value, mask = kk[cols, :], vv[cols, :], bias[rows, cols]
+                out = []
+                for q, (top, tot, acc) in zip(heads, carry):
+                    s = lax.dot_general(q, key, (((1,), (1,)), ((), ())), preferred_element_type=F32) + mask
+                    new = jnp.maximum(top, jnp.max(s, axis=1, keepdims=True))
+                    shrink = jnp.exp(top - new)
+                    p = jnp.exp(s - new)
+                    tot = tot * shrink + jnp.sum(p, axis=1, keepdims=True)
+                    acc = acc * shrink + jnp.dot(p.astype(BF), value, preferred_element_type=F32)
+                    out.append((new, tot, acc))
+                return tuple(out)
+
+            start = (jnp.full((tile, 1), NEG, F32), jnp.zeros((tile, 1), F32), jnp.zeros((tile, 128), F32))
+            (top0, tot0, acc0), (top1, tot1, acc1) = lax.fori_loop(low, high, body, (start, start))
+            result = jnp.where(left, acc0 / tot0, acc1 / tot1)
+            mixed[rows, lanes] = result
+            mixed_low[rows, lanes] = result.astype(BF)
+            stats = jnp.where(lane == 2 * chunk, top0 + jnp.log(tot0), stats)
+            stats = jnp.where(lane == 2 * chunk + 1, top1 + jnp.log(tot1), stats)
+            step()
+        lse[rows, :] = stats
+
+
+def tiled_nt(left, right, put, size=256):
+    size = gcd_of(right.shape[0], size)
+
+    def body(j, carry):
+        cols = pl.ds(pl.multiple_of(j * size, size), size)
+        put(
+            cols,
+            lax.dot_general(left, right[cols, :], (((1,), (1,)), ((), ())), preferred_element_type=F32),
+        )
+        return carry
+
+    lax.fori_loop(0, right.shape[0] // size, body, 0)
+
+
+def forward_kernel(chain, *refs):
+    (tok, own_gain, wqkv, wout, wgate, wup, wdown, cot, cosine, sine, qseg, qpos, kseg, kmark) = refs[:14]
+    (
+        normed_all,
+        gains,
+        wqkv_all,
+        wout_all,
+        wgate_all,
+        wup_all,
+        wdown_all,
+        cot_all,
+        query,
+        kv_all,
+        mixed,
+        mixed_low,
+        lse,
+        middle,
+        two_all,
+    ) = refs[14:29]
+    rest = refs[29:]
+    table, normed, own_kv, kk, vv, bias, part, total, two = rest[:9]
+    scratch, (send, recv) = rest[9:15], rest[15:]
     sems = Sems(send, recv)
     pc, near = Place(chain), Place(1)
+    rows, width = tok.shape
+    wrows = wqkv.shape[0]
+    local = query.shape[0]
+    wide = query.shape[1]
     greet(pc)
 
     def head():
@@ -626,49 +832,66 @@
             v = tok[r, :].astype(F32)
             normed[r, :] = (v * unit(v) * gains[0:1, :]).astype(BF)
 
-        each_rows(tok.shape[0], norm)
+        each_rows(rows, norm)
         yield from plane_gather(near, sems, normed, normed_all)
 
-    def by_dp(ref):
-        return lambda d: ref.at[d]
-
-    tasks = [
-        head(),
-        dp_gather(pc, sems, wqkv, by_dp(wqkv_all)),
-        dp_gather(pc, sems, wout, by_dp(wout_all)),
-        spread(pc, sems, by_dp(wgate), by_dp(wgate_all)),
-        spread(pc, sems, by_dp(wup), by_dp(wup_all)),
-        spread(pc, sems, by_dp(wdown), by_dp(wdown_all)),
-        plane_gather(pc, sems, cot, cot_all, 2),
-    ]
-    run(*tasks)
-
-
-def keys_kernel(chain, own, out, send, recv):
-    sems = Sems(send, recv)
-    pc = Place(chain)
-    greet(pc)
-    run(dp_gather(pc, sems, own, lambda d: out.at[d]))
-
-
-def middle_kernel(chain, part, tok, gains, middle, all_two, *rest):
-    scratch, (total, two), (send, recv) = rest[:6], rest[6:8], rest[8:]
-    sems = Sems(send, recv)
-    pc, near = Place(chain), Place(1)
-    greet(pc)
-
-    def go():
-        yield from plane_reduce(near, sems, part, scratch, total)
-
-        def norm(r):
-            v = tok[r, :].astype(F32) + total[r, :]
-            middle[r, :] = v
-            two[r, :] = (v * unit(v) * gains[1:2, :]).astype(BF)
-
-        each_rows(total.shape[0], norm)
-        yield from plane_gather(pc, sems, two, all_two, 2)
-
-    run(go())
+    first = dp_gather(pc, sems, wqkv, rows_of(wqkv_all, wrows))
+    out_weights = dp_gather(pc, sems, wout, rows_of(wout_all, wrows))
+    behind = Behind(
+        pipeline(
+            [
+                out_weights,
+                spread(pc, sems, lambda d: wgate.at[d], rows_of(wgate_all, wrows)),
+                spread(pc, sems, lambda d: wup.at[d], rows_of(wup_all, wrows)),
+                plane_gather(pc, sems, cot, cot_all, 2),
+                spread(pc, sems, lambda d: wdown.at[d], rows_of(wdown_all, wrows)),
+            ]
+        )
+    )
+    beside = head()
+    next(beside)
+    next(first)
+    next(first)
+    for state in first:
+        next(beside, None)
+        if state == "tail":
+            break
+    behind()
+    run(beside)
+    run(first)
+
+    here = jnp.concatenate([normed_all[0, s] for s in range(normed_all.shape[1])], axis=0)
+    size = 256
+    for at in range(0, wide, size):
+        pre = jnp.dot(here, wqkv_all[:, at : at + size], preferred_element_type=F32)
+        for lanes in range(0, size, 128):
+            turned = turn(pre[:, lanes : lanes + 128], cosine[...], sine[...])
+            query[:, at + lanes : at + lanes + 128] = (turned * 0.125).astype(BF)
+    pre = jnp.dot(here, wqkv_all[:, wide : wide + 128], preferred_element_type=F32)
+    own_kv[...] = jnp.where(halves(), turn(pre, cosine[...], sine[...]), pre).astype(BF)
+    behind.along(dp_gather(pc, sems, own_kv, rows_of(kv_all, local)))
+    spread_lanes(kv_all, kk, vv)
+    low, high = key_range(pc.d * local, local, kk.shape[0], size)
+    fill_bias(bias, low, high, size, qseg, qpos, kseg, kmark)
+    attend(pc, query, kk, vv, bias, mixed, mixed_low, lse, behind)
+
+    run(out_weights)
+
+    def put(cols, value):
+        for s in range(part.shape[1]):
+            part[0, s, :, cols] = value[s * rows : (s + 1) * rows].astype(BF)
+
+    tiled_nt(mixed_low[...], wout_all, put)
+    behind.along(plane_reduce(near, sems, part, scratch, total))
+
+    def norm(r):
+        v = tok[r, :].astype(F32) + total[r, :]
+        middle[r, :] = v
+        two[r, :] = (v * unit(v) * gains[1:2, :]).astype(BF)
+
+    each_rows(rows, norm)
+    behind.along(plane_gather(pc, sems, two, two_all, 2))
+    behind.drain()
 
 
 def back_kernel(chain, *refs):
@@ -712,9 +935,7 @@
 
     run(
         go(),
-        collect(pc, sems, ggate, s_gate, cgate),
-        collect(pc, sems, gup, s_up, cup),
-        collect(pc, sems, gdown, s_down, cdown),
+        collect(pc, sems, (ggate, gup, gdown), (s_gate, s_up, s_down), (cgate, cup, cdown)),
         last(),
     )
 
@@ -724,7 +945,7 @@
     sems = Sems(send, recv)
     pc = Place(chain)
     greet(pc)
-    run(dp_reduce(pc, sems, part, scratch, out))
+    run(dp_reduce(pc, sems, (part,), (scratch,), (out,)))
 
 
 def end_kernel(chain, *refs):
@@ -762,99 +983,12 @@
 
     run(
         go(),
-        dp_reduce(pc, sems, gqkv, s_qkv, qkv_out),
-        dp_reduce(pc, sems, gwout, s_out, wout_out),
+        dp_reduce(pc, sems, (gwout, gqkv), (s_out, s_qkv), (wout_out, qkv_out)),
     )
 
 
-def attend_kernel(bounds, q, k, v, qseg, qpos, kseg, kmark, mixed, lse, bias):
-    size = math_gcd(k.shape[0])
-    rows = q.shape[0]
-    scale = q.shape[1] ** -0.5
-
-    @pl.when(pl.program_id(0) == 0)
-    def _():
-        def fill(j, carry):
-            at = pl.multiple_of(j * size, size)
-            cols = pl.ds(at, size)
-            kpos = at + lax.broadcasted_iota(jnp.int32, (1, size), 1)
-            same = kpos == qpos[...]
-            allowed = (
-                (kseg[:, cols] == qseg[...]) & (kpos <= qpos[...]) & ((kmark[:, cols] == 1) | same)
-            )
-            bias[:, cols] = jnp.where(allowed, 0.0, NEG)
-            return carry
-
-        lax.fori_loop(bounds[0], bounds[1], fill, 0)
-
-    def step(j, carry):
-        top, total, acc = carry
-        cols = pl.ds(pl.multiple_of(j * size, size), size)
-        scores = lax.dot_general(
-            q[...], k[cols, :], (((1,), (1,)), ((), ())), preferred_element_type=F32
-        ) * scale + bias[:, cols]
-        new = jnp.maximum(top, jnp.max(scores, axis=1, keepdims=True))
-        shrink = jnp.exp(top - new)
-        probs = jnp.exp(scores - new)
-        total = total * shrink + jnp.sum(probs, axis=1, keepdims=True)
-        acc = acc * shrink + jnp.dot(probs.astype(BF), v[cols, :], preferred_element_type=F32)
-        return new, total, acc
-
-    top, total, acc = lax.fori_loop(
-        bounds[0],
-        bounds[1],
-        step,
-        (jnp.full((rows, 1), NEG, F32), jnp.zeros((rows, 1), F32), jnp.zeros((rows, q.shape[1]), F32)),
-    )
-    mixed[...] = acc / total
-    lse[...] = top + jnp.log(total)
-
-
-def math_gcd(n):
-    size = 256
-    while n % size:
-        size //= 2
-    return size
-
-
-def attend(bounds, q, k, v, qseg, qpos, kseg, kmark):
-    heads, rows, dim = q.shape
-    keys = k.shape[0]
-
-    def whole(shape):
-        return pl.BlockSpec(shape, lambda h, b: (0, 0))
-
-    def head(shape):
-        return pl.BlockSpec((pl.Squeezed(),) + shape, lambda h, b: (h, 0, 0))
-
-    return pl.pallas_call(
-        attend_kernel,
-        out_shape=[
-            jax.ShapeDtypeStruct((heads, rows, dim), F32),
-            jax.ShapeDtypeStruct((heads, rows, 1), F32),
-        ],
-        grid_spec=pltpu.PrefetchScalarGridSpec(
-            num_scalar_prefetch=1,
-            grid=(heads,),
-            in_specs=[
-                head((rows, dim)),
-                whole((keys, dim)),
-                whole((keys, dim)),
-                whole((rows, 1)),
-                whole((rows, 1)),
-                whole((1, keys)),
-                whole((1, keys)),
-            ],
-            out_specs=[head((rows, dim)), head((rows, 1))],
-            scratch_shapes=[pltpu.VMEM((rows, keys), F32)],
-        ),
-        name="attend",
-        compiler_params=pltpu.CompilerParams(vmem_limit_bytes=48 << 20),
-    )(bounds, q, k, v, qseg, qpos, kseg, kmark)
-
-
 def attend_back_kernel(bounds, q, dmix, lse, delta, k, v, qseg, qpos, kseg, kmark, dq, dk, dv, bias):
-    size = math_gcd(k.shape[0])
+    size = gcd_of(k.shape[0], 256)
     scale = q.shape[1] ** -0.5
 
     @pl.when(pl.program_id(0) == 0)
@@ -987,10 +1121,10 @@
     units = w_gate.shape[1] // chain
     qkv = w_query.shape[1] + 2 * dim
     me = lax.axis_index("dp")
-    first_row = me * local
     share = attn_gain.shape[0]
     tile = 128 // share
 
+    first_row = me * local
     own_gain = jnp.concatenate(
         [
             jnp.tile(attn_gain, tile)[None],
@@ -1007,77 +1141,87 @@
 
     plane = chain * n_t * rows
     nbytes = 60 << 20
-    (normed, gains, wqkv, wout, wgate, wup, wdown, cot) = call(
-        functools.partial(gather_kernel, chain),
-        "gather",
+    positions = first_row + jnp.arange(local, dtype=jnp.int32)
+    cosine, sine = angles(positions, dim // 2)
+    own_segments = lax.dynamic_slice(segment_ids, (first_row,), (local,))
+    wide = heads * dim
+    (
+        normed,
+        gains,
+        wqkv,
+        wout,
+        wgate,
+        wup,
+        wdown,
+        cot,
+        query,
+        kv,
+        mixed,
+        mixed_low,
+        lse,
+        middle,
+        two,
+    ) = call(
+        functools.partial(forward_kernel, chain),
+        "forward",
         0,
-        [VM, VM] + [ANY] * 6,
+        [VM, VM] + [ANY] * 6 + [VM] * 6,
         [
-            ((1, n_t, rows, width), BF, ANY),
+            ((1, n_t, rows, width), BF, VM),
             ((8, width), F32, VM),
-            ((n_dp, wrows, qkv), BF, ANY),
-            ((n_dp, wrows, heads * dim), BF, ANY),
-            ((n_dp, wrows, units), BF, ANY),
-            ((n_dp, wrows, units), BF, ANY),
-            ((n_dp, wrows, units), BF, ANY),
+            ((width, qkv), BF, VM),
+            ((width, wide), BF, VM),
+            ((width, units), BF, ANY),
+            ((width, units), BF, ANY),
+            ((width, units), BF, ANY),
+            ((chain, n_t, rows, width), BF, ANY),
+            ((local, wide), BF, VM),
+            ((total, 2 * dim), BF, VM),
+            ((local, wide), F32, VM),
+            ((local, wide), BF, VM),
+            ((local, 128), F32, VM),
+            ((rows, width), F32, VM),
             ((chain, n_t, rows, width), BF, ANY),
         ],
-        [pltpu.VMEM((n_dp, n_t, 8, 128), F32), pltpu.VMEM((rows, width), BF)],
-        (tokens, own_gain, wqkv, wout, by_chain(w_gate), by_chain(w_up), by_chain(w_down.T), cotangent),
+        [
+            pltpu.VMEM((n_dp, n_t, 8, 128), F32),
+            pltpu.VMEM((rows, width), BF),
+            pltpu.VMEM((local, 2 * dim), BF),
+            pltpu.VMEM((total, 128), BF),
+            pltpu.VMEM((total, 128), BF),
+            pltpu.VMEM((local, total), F32),
+            pltpu.VMEM((1, n_t, rows, width), BF),
+            pltpu.VMEM((rows, width), F32),
+            pltpu.VMEM((rows, width), BF),
+        ]
+        + plane_scratch(1, rows, width),
+        (
+            tokens,
+            own_gain,
+            wqkv,
+            wout,
+            by_chain(w_gate),
+            by_chain(w_up),
+            by_chain(w_down.T),
+            cotangent,
+            jnp.tile(cosine, (1, 4)),
+            jnp.tile(jnp.concatenate([-sine, sine], axis=1), (1, 2)),
+            own_segments[:, None],
+            positions[:, None],
+            segment_ids[None],
+            key_mask[None],
+        ),
         nbytes,
     )
     normed = normed.reshape(local, width)
-    wqkv = wqkv.reshape(width, qkv)
-    wout = wout.reshape(width, heads * dim)
-    wgate = wgate.reshape(width, units)
-    wup = wup.reshape(width, units)
-    wdown = wdown.reshape(width, units)
     cot = cot.reshape(plane, width)
-
-    positions = first_row + jnp.arange(local, dtype=jnp.int32)
-    cosine, sine = angles(positions, dim // 2)
-    pre = mm(normed, wqkv)
-    turned = rotate(pre[:, : (heads + 1) * dim].reshape(local, heads + 1, dim), cosine, sine).astype(BF)
-    query = turned[:, :heads].transpose(1, 0, 2)
-    own_kv = jnp.concatenate([turned[:, heads], pre[:, (heads + 1) * dim :].astype(BF)], axis=1)
-    (kv,) = call(
-        functools.partial(keys_kernel, chain),
-        "keys",
-        1,
-        [ANY],
-        [((n_dp, local, 2 * dim), BF, ANY)],
-        [],
-        (own_kv,),
-        1 << 20,
-    )
-    kv = kv.reshape(total, 2 * dim)
     keys, values = kv[:, :dim], kv[:, dim:]
-    own_segments = lax.dynamic_slice(segment_ids, (first_row,), (local,))
-    size = math_gcd(total)
+    query = (query * 8.0).astype(BF).reshape(local, heads, dim).transpose(1, 0, 2)
+    mixed = mixed.reshape(local, heads, dim).transpose(1, 0, 2)
+    lse = lse[:, :heads].T
+    size = gcd_of(total, 256)
     start = jnp.sum((segment_ids < own_segments[0]).astype(jnp.int32))
     bounds = jnp.stack([start // size, (first_row + local + size - 1) // size])
-    mixed, lse = attend(
-        bounds,
-        query,
-        keys,
-        values,
-        own_segments[:, None],
-        positions[:, None],
-        segment_ids[None],
-        key_mask[None],
-    )
-    mixed_low = mixed.transpose(1, 0, 2).reshape(local, heads * dim).astype(BF)
-    part = mm_nt(mixed_low, wout).astype(BF).reshape(1, n_t, rows, width)
-    middle, two = call(
-        functools.partial(middle_kernel, chain),
-        "middle",
-        2,
-        [VM, VM, VM],
-        [((rows, width), F32, VM), ((chain, n_t, rows, width), BF, ANY)],
-        plane_scratch(1, rows, width) + [pltpu.VMEM((rows, width), F32), pltpu.VMEM((rows, width), BF)],
-        (part, tokens, gains),
-        nbytes // 4,
-    )
 
     two = two.reshape(plane, width)
     gate = mm(two, wgate)

time: 670 us -> 538 us (0.80)
  Pallas kernels: 533 us -> 422 us
  matrix products: 58.5 us -> 47.2 us
  local copies, waits for them, and re-layouts: 52.9 us -> 46.1 us
    pallas_call x6 -> x4, Pallas kernels: 510 us -> 408 us  [call(): pl.pallas_call(kernel, out_shape=[jax.ShapeDtypeStruct(shape, kind) for s...]
    pallas_call x1 -> x0, Pallas kernels: 9.49 us -> none  [attend(): pl.pallas_call(attend_kernel, out_shape=[jax.ShapeDtypeStruct((heads, row...]
    unnamed x94 -> x86, local copies, waits for them, and re-layouts: 18 us -> 13.4 us
    dot_general x5 -> x4, matrix products: 21 us -> 17.2 us  [mm_nt(): lax.dot_general(a, b, (((1,), (1,)), ((), ())), preferred_element_type=F32)]
    dot_general x5 -> x4, matrix products: 15.2 us -> 12.5 us  [mm(): return jnp.dot(a, b, preferred_element_type=F32)]
where the time goes in v2:
time: 538 us; the launch traced here: 531 us
  Pallas kernels  422 us (78%)
  matrix products  47.2 us (9%)
  local copies, waits for them, and re-layouts  46.1 us (9%)
  other arithmetic  10.8 us (2%)
    pallas_call x4, Pallas kernels, call(): pl.pallas_call(kernel, out_shape=[jax.ShapeDtypeStruct(shape, kind) for s...  408 us
    dot_general x5, matrix products, mm_tn(): lax.dot_general(a, b, (((0,), (0,)), ((), ())), preferred_element_type=F32)  17.5 us
    dot_general x4, matrix products, mm_nt(): lax.dot_general(a, b, (((1,), (1,)), ((), ())), preferred_element_type=F32)  17.2 us
    pallas_call x1, Pallas kernels, attend_back(): pl.pallas_call(attend_back_kernel, out_shape=[jax.ShapeDtypeStruct((heads...  14.3 us
    unnamed x86, local copies, waits for them, and re-layouts  13.4 us
    dot_general x4, matrix products, mm(): return jnp.dot(a, b, preferred_element_type=F32)  12.5 us

profile of v2, /device:TPU:0, one launch (start us, length us, event | category | flops | bytes accessed | tf_op | source)
XLA Modules:
  0.0 530.8 jit_solution(10220143535770073735)
XLA Ops:
  0.7 0.8 dynamic_slice.6
  1.5 0.8 broadcast_in_dim.38.refs_10_
  2.6 0.8 copy.78.refs_9_
  3.4 0.8 copy.77.refs_8_
  5.2 1.2 copy.73
  6.6 1.2 copy.75
  7.8 1.2 copy.76
  9.2 0.8 pad_maximum_fusion.4.refs_2_
  10.0 0.8 copy.71
  13.0 180.5 %forward.1 = (bf16[1,4,80,2048]{3,2,1,0:T(8,128)(2,1)}, f32[8,2048]{1,0:T(8,128)}, bf16[2048,640]{1,0:T(8,128)(2,1)}, bf16[2048,512]{1,0:T(8,128)(2,1)}, bf16[20...) custom-call(bf16[80,2048]{1,0:T(8,128)(2,1)} %refs_3_.1, ...), custom_call_target="tpu_custom_call" | custom-call | bytes 62914560 | tf_op jit(solution)/shard_map/forward/pallas_call | solution.py:665
  193.6 5.2 fusion.8
  198.8 2.2 fusion.7
  201.1 4.2 multiply_convert_fusion
  205.4 0.9 copy-done.34
  206.3 2.0 convolution_convert_fusion.3
  208.3 1.7 copy.82
  210.1 4.8 convolution_convert_fusion.4
  214.9 1.6 copy.81
  216.4 4.8 convolution_convert_fusion.5
  221.3 1.6 copy.80
  222.9 7.1 %convolution_convert_fusion = bf16[1280,2048]{1,0:T(8,128)(2,1)} fusion(bf16[1280,352]{0,1:T(8,128)(2,1)} %copy-done.34, bf16[2048,352]{1,0:T(8,128)(2,1)} %get-tuple-element.41), kind=kOutput, calls=%fused_computation.1 | convolution fusion | flops 1848115200 | bytes 7585792 | tf_op jit(solution)/shard_map/dot_general | solution.py:1094
  230.0 3.0 fusion.9
  232.9 4.8 add_convert_fusion
  237.7 110.5 %back.1 = (bf16[80,2048]{1,0:T(8,128)(2,1)}, f32[80,2048]{1,0:T(8,128)}, bf16[1,4,80,2048]{3,2,1,0:T(8,128)(2,1)}, f32[8,2048]{1,0:T(8,128)}, bf16[4,256,352]{2,...) custom-call(bf16[4,4,80,2048]{3,2,1,0:T(8,128)(2,1)} %bitcast.84, ...), custom_call_target="tpu_custom_call" | custom-call | bytes 62914560 | tf_op jit(solution)/shard_map/back/pallas_call | solution.py:665
  348.3 1.6 convert_bitcast_fusion
  349.8 1.6 copy.97
  351.4 2.9 copy.103
  354.3 1.6 copy.98
  355.9 2.7 convolution_convert_fusion.2
  358.5 0.8 convolution_convert_fusion.7
  362.8 1.3 convert_reduce_fusion
  367.3 1.4 fusion.6
  368.9 1.1 copy.84
  371.9 2.0 broadcast_in_dim.39.kseg
  373.8 2.0 broadcast_in_dim.40.kmark
  375.8 14.3 %attend_back.1 = (f32[8,320,64]{2,1,0:T(8,128)}, f32[2560,64]{1,0:T(8,128)}, f32[2560,64]{1,0:T(8,128)}) custom-call(s32[2]{0:T(128)} %pad_add_fusion.bounds, bf16[8,320,64]{2,1,0:T(8,128)(2,1)} %bitcast.101, bf16[8,320,64]{2,1,0:T(8,128)(2,1)} %bitcast.88, f32[8,1,320]{2,1,0:T(1,128)} %reshape.220.lse, f32[8,1,320]{2,1,0:T(1,128)} %reshape.222.delta, ...), custom_call_target="tpu_custom_call" | custom-call | tf_op jit(solution)/shard_map/attend_back/pallas_call | solution.py:1042
  390.1 1.5 convert.27
  391.9 1.2 pad_maximum_fusion.2.part
  393.1 50.7 %key_grads.1 = f32[320,128]{1,0:T(8,128)} custom-call(bf16[8,320,128]{2,1,0:T(8,128)(2,1)} %pad_maximum_fusion.2.part), custom_call_target="tpu_custom_call" | custom-call | bytes 2097152 | tf_op jit(solution)/shard_map/key_grads/pallas_call | solution.py:665
  443.8 0.9 slice_bitcast_fusion
  447.0 3.2 convolution_convert_fusion.1
  450.2 2.3 convolution_convert_fusion.6
  452.6 66.3 %end.1 = (f32[80,2048]{1,0:T(8,128)}, f32[256,640]{1,0:T(8,128)}, f32[256,512]{1,0:T(8,128)}, f32[8,128]{1,0:T(8,128)}) custom-call(bf16[1,4,80,2048]{3,2,1,0:T(8,128)(2,1)} %bitcast.107, bf16[8,256,640]{2,1,0:T(8,128)(2,1)} %bitcast.98, bf16[8,256,512]{2,1,0:T(8,128)(2,1)} %bitcast.102, bf16[80,2048]{1,0:T(8,128)(2,1)} %refs_3_.1, ...), custom_call_target="tpu_custom_call" | custom-call | bytes 31457280 | tf_op jit(solution)/shard_map/end/pallas_call | solution.py:665
  518.9 2.1 copy.101
  521.0 1.9 slice.49
  524.2 1.1 fusion.5
  527.3 1.5 copy.102
  529.5 0.8 copy.107
  (124 shorter events, 16.5 us)
Async XLA Ops:
  0.6 4.2 copy-start.10
  4.2 2.1 copy-start.11
  6.3 1.5 copy-start.12
  6.6 2.4 copy-start.22
  6.6 2.5 copy-start.23
  6.6 2.6 copy-start.18
  7.8 2.3 copy-start.17
  7.8 3.1 copy-start.20
  7.8 3.7 copy-start.21
  7.8 4.3 copy-start.32
  7.8 4.4 copy-start.33
  193.6 5.3 copy-start.24
  193.6 5.3 copy-start.27
  193.6 7.5 %slice-start = ((s8[5242880]{0:T(1024)(128)(4,1)}), s8[4194304]{0:T(1024)(128)(4,1)S(1)}, s32[]{:S(2)}) async-start(s8[5242880]{0:T(1024)(128)(4,1)} %bitcast.118), calls=%async_computation | async-start | bytes 8388608
  198.8 2.3 slice-start.1
  198.8 2.3 copy-start.3
  205.4 0.9 copy-start.34
  222.9 7.1 %copy-start.2 = (bf16[2048,352]{1,0:T(8,128)(2,1)S(1)}, bf16[2048,352]{1,0:T(8,128)(2,1)}, u32[]{:S(2)}) copy-start(bf16[2048,352]{1,0:T(8,128)(2,1)} %get-tuple-element.44) | copy-start | bytes 4325380
  222.9 7.1 %copy-start.7 = (bf16[1280,352]{0,1:T(8,128)(2,1)S(1)}, bf16[1280,352]{0,1:T(8,128)(2,1)}, u32[]{:S(2)}) copy-start(bf16[1280,352]{0,1:T(8,128)(2,1)} %get-tuple-element.103) | copy-start | bytes 2703364
  230.0 3.0 copy-start.8
  354.3 1.6 copy-start.29
  354.3 1.6 copy-start.31
  355.9 2.7 copy-start.26
  355.9 2.7 copy-start.30
  359.4 1.1 copy-start.13
  360.0 1.2 copy-start
  360.7 6.5 %copy-start.1 = (bf16[2560,128]{1,0:T(8,128)(2,1)S(1)}, bf16[2560,128]{1,0:T(8,128)(2,1)}, u32[]{:S(2)}) copy-start(bf16[2560,128]{1,0:T(8,128)(2,1)} %get-tuple-element.53) | copy-start | bytes 1966084
  361.7 7.0 %copy-start.16 = (bf16[320,512]{1,0:T(8,128)(2,1)S(1)}, bf16[320,512]{1,0:T(8,128)(2,1)}, u32[]{:S(2)}) copy-start(bf16[320,512]{1,0:T(8,128)(2,1)} %get-tuple-element.48) | copy-start | bytes 983044
  368.6 1.4 copy-start.19
  390.1 1.7 copy-start.5
  391.9 53.1 %copy-start.4 = (f32[8,320,64]{2,1,0:T(8,128)S(1)}, f32[8,320,64]{2,1,0:T(8,128)}, u32[]{:S(2)}) copy-start(f32[8,320,64]{2,1,0:T(8,128)} %get-tuple-element.54) | copy-start | bytes 1966084
  445.6 0.9 copy-start.6
  445.6 1.4 copy-start.28
  447.0 3.2 copy-start.25
  518.9 7.8 %copy-start.9 = (bf16[4,256,352]{2,1,0:T(8,128)(2,1)S(1)}, bf16[4,256,352]{2,1,0:T(8,128)(2,1)}, u32[]{:S(2)}) copy-start(bf16[4,256,352]{2,1,0:T(8,128)(2,1)} %get-tuple-element.66) | copy-start | bytes 2162692
  527.2 1.6 copy-start.15
  527.3 2.3 copy-start.14

commit v3 on v2

--- a/solution.py
+++ b/solution.py
@@ -96,6 +96,16 @@
             device_id_type=MESH,
         )
         when(pred, copy.wait_recv)
+
+    def describe(self, i, src):
+        return pltpu.make_async_remote_copy(
+            src_ref=src,
+            dst_ref=src,
+            send_sem=self.sems.send.at[i],
+            recv_sem=self.sems.recv.at[i],
+            device_id={"dp": lax.axis_index("dp"), "tensor": lax.axis_index("tensor")},
+            device_id_type=MESH,
+        )
 
     def finish(self):
         for copy, pred in self.sent:
@@ -140,6 +150,13 @@
     for task in tasks:
         for _ in task:
             yield
+
+
+def rounds(*tasks):
+    live = list(tasks)
+    while live:
+        live = [task for task in live if next(task, "end") != "end"]
+        yield
 
 
 class Behind:
@@ -232,11 +249,11 @@
 
 
 def far_first(chain, z, j):
-    if j == chain - 1:
+    if isinstance(j, int) and j == chain - 1:
         return z
     up = jnp.where(j < chain - 1 - z, chain - 1 - j, j - (chain - 1 - z))
     down = jnp.where(j < z, j, chain - 1 - (j - z))
-    return jnp.where(2 * z < chain, up, down)
+    return jnp.where(j == chain - 1, z, jnp.where(2 * z < chain, up, down))
 
 
 def each_rows(count, fn, rows=16):
@@ -247,37 +264,32 @@
     lax.fori_loop(0, count // rows, body, 0)
 
 
-def chain_reduce(pc, cp, right, left, b, last, value, zsend, lrecv, rrecv, store, rows, cols):
+def chain_reduce(pc, cp, right, left, b, last, value, zsend, came, store, rows, cols):
     chain, z = pc.chain, pc.z
     if not last:
         fromleft = jnp.logical_and(b > z, z > 0)
         fromright = jnp.logical_and(b < z, z < chain - 1)
-        cp.arrive(right, lrecv.at[b, :, cols], pc.at(), fromleft)
-        cp.arrive(left, rrecv.at[b, :, cols], pc.at(), fromright)
-
-        @pl.when(fromleft)
+        cp.arrive(right, came.at[b, :, cols], pc.at(), fromleft)
+        cp.arrive(left, came.at[b, :, cols], pc.at(), fromright)
+        some = jnp.logical_or(fromleft, fromright)
+
+        @pl.when(some)
         def _():
             def add(r):
-                zsend[b, r, cols] = (value(r) + lrecv[b, r, cols].astype(F32)).astype(BF)
+                zsend[b, r, cols] = (value(r) + came[b, r, cols].astype(F32)).astype(BF)
 
             each_rows(rows, add)
 
-        @pl.when(fromright)
-        def _():
-            def add(r):
-                zsend[b, r, cols] = (value(r) + rrecv[b, r, cols].astype(F32)).astype(BF)
-
-            each_rows(rows, add)
-
-        @pl.when(jnp.logical_not(jnp.logical_or(fromleft, fromright)))
+        @pl.when(jnp.logical_not(some))
         def _():
             def add(r):
                 zsend[b, r, cols] = value(r).astype(BF)
 
             each_rows(rows, add)
 
-        cp.go(right, zsend.at[b, :, cols], lrecv.at[b, :, cols], pc.above, b > z)
-        cp.go(left, zsend.at[b, :, cols], rrecv.at[b, :, cols], pc.below, b < z)
+        cp.go(right, zsend.at[b, :, cols], came.at[b, :, cols], pc.above, b > z)
+        slot = jnp.where(b == z - 1, chain, b)
+        cp.go(left, zsend.at[b, :, cols], came.at[slot, :, cols], pc.below, b < z)
         return
 
     def first(r):
@@ -288,19 +300,19 @@
 
         @pl.when(z > 0)
         def _():
-            cp.arrive(right, lrecv.at[b, :, cols], pc.at())
+            cp.arrive(right, came.at[b, :, cols], pc.at())
 
             def add(r):
-                store(r, lrecv[b, r, cols].astype(F32), True)
+                store(r, came[b, r, cols].astype(F32), True)
 
             each_rows(rows, add)
 
         @pl.when(z < chain - 1)
         def _():
-            cp.arrive(left, rrecv.at[b, :, cols], pc.at())
+            cp.arrive(left, came.at[chain, :, cols], pc.at())
 
             def add(r):
-                store(r, rrecv[b, r, cols].astype(F32), True)
+                store(r, came[chain, r, cols].astype(F32), True)
 
             each_rows(rows, add)
 
@@ -310,91 +322,108 @@
         pltpu.VMEM((chain, 2, rows, width), BF),
         pltpu.VMEM((chain, rows, width), BF),
         pltpu.VMEM((chain, rows, width), BF),
-        pltpu.VMEM((chain, rows, width), BF),
-        pltpu.VMEM((chain, rows, width), BF),
-        pltpu.VMEM((chain, rows, width), BF),
+        pltpu.VMEM((chain if chain > 1 else 1, rows, width) if chain > 1 else (1, 16, 128), BF),
+        pltpu.VMEM((chain + 1, rows, width) if chain > 1 else (1, 16, 128), BF),
     ]
 
 
-def plane_reduce(pc, sems, part, scratch, out, parts=1):
-    crecv, csum, yrecv, zsend, lrecv, rrecv = scratch
-    chain, z = pc.chain, pc.z
-    count = out.shape[0]
-    width = out.shape[1] // parts
-    cp = Copies(sems)
-    base = sems.take(5 * chain * parts)
-
-    def sem(kind, i, p):
-        return base + (kind * chain + i) * parts + p
-
-    todo = [(j, far_first(chain, z, j), p) for j in range(chain) for p in range(parts)]
-    mine = pc.s
-
-    def cols_of(p):
-        return pl.ds(p * width, width)
-
-    def pass_core(over):
-        for j, b, p in todo:
-            cp.go(
-                sem(over, j, p),
-                part.at[b, pc.so if over else pc.sc, :, cols_of(p)],
-                crecv.at[b, over, :, cols_of(p)],
-                pc.at(s=pc.sc),
+class PlaneReduce:
+    def __init__(self, pc, sems, part, scratch, out):
+        self.pc, self.part, self.out = pc, part, out
+        self.crecv, self.csum, self.yrecv, self.zsend, self.came = scratch
+        self.cp = Copies(sems)
+        self.base = sems.take(5 * pc.chain)
+        self.rows, self.width = out.shape
+
+    def sem(self, kind, i):
+        return self.base + kind * self.pc.chain + i
+
+    def block(self, j):
+        return far_first(self.pc.chain, self.pc.z, j)
+
+    def pass_core(self, over, j, b, cp=None):
+        pc = self.pc
+        (cp or self.cp).go(
+            self.sem(over, j),
+            self.part.at[b, pc.so if over else pc.sc],
+            self.crecv.at[b, over],
+            pc.at(s=pc.sc),
+        )
+
+    def cross(self, j, b, cp=None):
+        pc, part, crecv, csum = self.pc, self.part, self.crecv, self.csum
+        cp = cp or self.cp
+        cp.arrive(self.sem(1, j), crecv.at[b, 1], pc.at())
+
+        def add(r):
+            csum[b, r, :] = (part[b, pc.sy, r, :].astype(F32) + crecv[b, 1, r, :].astype(F32)).astype(BF)
+
+        each_rows(self.rows, add)
+        cp.go(self.sem(2, j), csum.at[b], self.yrecv.at[b], pc.at(s=pc.sy))
+
+    def started(self):
+        for j in range(self.pc.chain):
+            b = self.block(j)
+            for kind, src in ((1, self.part.at[b, 0]), (0, self.part.at[b, 0]), (2, self.csum.at[b])):
+                self.cp.sent.append((self.cp.describe(self.sem(kind, j), src), None))
+
+    def steps(self, crossed=False):
+        pc = self.pc
+        chain, z = pc.chain, pc.z
+        part, crecv, yrecv, out = self.part, self.crecv, self.yrecv, self.out
+        cp = self.cp
+        todo = [(j, self.block(j)) for j in range(chain)]
+        ahead = []
+        if crossed:
+            self.started()
+        else:
+            for j, b in todo:
+                self.pass_core(1, j, b)
+            yield
+            ahead = list(todo)
+            for _ in range(min(2, chain)):
+                self.cross(*ahead.pop(0))
+                yield
+            for j, b in todo:
+                self.pass_core(0, j, b)
+            yield
+        for j, b in todo:
+            cp.arrive(self.sem(0, j), crecv.at[b, 0], pc.at())
+            cp.arrive(self.sem(2, j), yrecv.at[b], pc.at())
+            if ahead:
+                self.cross(*ahead.pop(0))
+
+            def value(r):
+                return (
+                    part[b, pc.s, r, :].astype(F32)
+                    + crecv[b, 0, r, :].astype(F32)
+                    + yrecv[b, r, :].astype(F32)
+                )
+
+            def store(r, term, more):
+                out[r, :] = out[r, :] + term if more else term
+
+            chain_reduce(
+                pc,
+                cp,
+                self.sem(3, b),
+                self.sem(4, b),
+                b,
+                j == chain - 1,
+                value,
+                self.zsend,
+                self.came,
+                store,
+                self.rows,
+                pl.ds(0, self.width),
             )
-
-    def cross(j, b, p):
-        cols = cols_of(p)
-        cp.arrive(sem(1, j, p), crecv.at[b, 1, :, cols], pc.at())
-
-        def add(r):
-            csum[b, r, cols] = (part[b, pc.sy, r, cols].astype(F32) + crecv[b, 1, r, cols].astype(F32)).astype(BF)
-
-        each_rows(count, add)
-        cp.go(sem(2, j, p), csum.at[b, :, cols], yrecv.at[b, :, cols], pc.at(s=pc.sy))
-
-    pass_core(1)
-    yield
-    ahead = list(todo)
-    for _ in range(min(2, len(ahead))):
-        cross(*ahead.pop(0))
+            yield
+        cp.finish()
         yield
-    pass_core(0)
-    yield
-    for j, b, p in todo:
-        cols = cols_of(p)
-        cp.arrive(sem(0, j, p), crecv.at[b, 0, :, cols], pc.at())
-        cp.arrive(sem(2, j, p), yrecv.at[b, :, cols], pc.at())
-        if ahead:
-            cross(*ahead.pop(0))
-
-        def value(r):
-            return (
-                part[b, mine, r, cols].astype(F32)
-                + crecv[b, 0, r, cols].astype(F32)
-                + yrecv[b, r, cols].astype(F32)
-            )
-
-        def store(r, term, more):
-            out[r, cols] = out[r, cols] + term if more else term
-
-        chain_reduce(
-            pc,
-            cp,
-            sem(3, 0, 0) + b * parts + p,
-            sem(4, 0, 0) + b * parts + p,
-            b,
-            j == chain - 1,
-            value,
-            zsend,
-            lrecv,
-            rrecv,
-            store,
-            count,
-            cols,
-        )
-        yield
-    cp.finish()
-    yield
+
+
+def plane_reduce(pc, sems, part, scratch, out):
+    return PlaneReduce(pc, sems, part, scratch, out).steps()
 
 
 def dp_gather(pc, sems, own, out):
@@ -428,7 +457,7 @@
             cp.arrive(across + i * groups + g, out(b * groups + (t - g + groups) % groups), pc.at(), got)
     keep.wait()
     cp.finish()
-    yield
+    yield "end"
 
 
 def spread(pc, sems, blocks, out):
@@ -457,88 +486,73 @@
             cp.arrive(across + k * groups + g, block, pc.at())
     keep.wait()
     cp.finish()
-    yield
-
-
-def side_sums(pc, cp, bases, parts, recvs, order, put, window=2):
-    groups, t = pc.groups, pc.t
-    todo = [(m, j, b) for m in range(len(parts)) for j, b in order]
-
-    def send(m, j, b):
-        for g in range(1, groups):
-            to = (t + g) % groups
-            cp.go(bases[m] + j * groups + g, parts[m].at[b * groups + to], recvs[m].at[g - 1, b], pc.at(t=to))
-
-    ahead = list(todo)
-    for _ in range(min(window, len(ahead))):
-        send(*ahead.pop(0))
-    yield None
-    for m, j, b in todo:
-        for g in range(1, groups):
-            cp.arrive(bases[m] + j * groups + g, recvs[m].at[g - 1, b], pc.at())
-        if ahead:
-            send(*ahead.pop(0))
-
-        def add(r):
-            total = parts[m][b * groups + t, r, :].astype(F32)
-            for g in range(1, groups):
-                total = total + recvs[m][g - 1, b, r, :].astype(F32)
-            put(m, b, r, total)
-
-        each_rows(parts[m].shape[1], add)
-        yield m, j, b
+    yield "end"
+
+
+class Side:
+    def __init__(self, pc, sems, part, recv):
+        self.pc, self.part, self.recv = pc, part, recv
+        self.rows, self.width = recv.shape[2], recv.shape[3]
+        self.base = sems.take(pc.chain * pc.groups)
+
+    def start(self, i):
+        return pl.multiple_of(i * self.rows, self.rows)
+
+    def send(self, cp, j, b):
+        pc = self.pc
+        for g in range(1, pc.groups):
+            to = (pc.t + g) % pc.groups
+            cp.go(
+                self.base + j * pc.groups + g,
+                self.part.at[pl.ds(self.start(b * pc.groups + to), self.rows)],
+                self.recv.at[g - 1, b],
+                pc.at(t=to),
+            )
+
+    def arrive(self, cp, j, b):
+        for g in range(1, self.pc.groups):
+            cp.arrive(self.base + j * self.pc.groups + g, self.recv.at[g - 1, b], self.pc.at())
+
+    def value(self, b, r):
+        at = self.start(b * self.pc.groups + self.pc.t)
+        total = self.part[pl.ds(pl.multiple_of(at + r.start, 16), r.size), :].astype(F32)
+        for g in range(1, self.pc.groups):
+            total = total + self.recv[g - 1, b, r, :].astype(F32)
+        return total
 
 
 def dp_scratch(chain, groups, rows, width):
     return [
         pltpu.VMEM((max(groups - 1, 1), chain, rows, width), BF),
-        pltpu.VMEM((chain, rows, width), F32),
         pltpu.VMEM((chain, rows, width), BF),
-        pltpu.VMEM((chain, rows, width), BF),
-        pltpu.VMEM((chain, rows, width), BF),
+        pltpu.VMEM((chain + 1, rows, width), BF),
     ]
 
 
-def dp_reduce(pc, sems, parts, scratches, outs):
-    chain, groups, z = pc.chain, pc.groups, pc.z
+def dp_reduce(pc, sems, part, scratch, out, window=2):
+    recv, zsend, came = scratch
+    chain, z = pc.chain, pc.z
     cp = Copies(sems)
-    count = len(parts)
-    bases = [sems.take(chain * groups) for _ in range(count)]
-    ups = [sems.take(chain) for _ in range(count)]
-    downs = [sems.take(chain) for _ in range(count)]
-    order = [(j, far_first(chain, z, j)) for j in range(chain)]
-
-    def put(m, b, r, total):
-        scratches[m][1][b, r, :] = total
-
-    for made in side_sums(pc, cp, bases, parts, [s[0] for s in scratches], order, put):
-        if made is None:
-            yield
-            continue
-        m, j, b = made
-        _, sums, zsend, lrecv, rrecv = scratches[m]
-        out = outs[m]
+    side = Side(pc, sems, part, recv)
+    up, down = sems.take(chain), sems.take(chain)
+    todo = [(j, far_first(chain, z, j)) for j in range(chain)]
+    ahead = list(todo)
+    for _ in range(min(window, chain)):
+        side.send(cp, *ahead.pop(0))
+    yield
+    for j, b in todo:
+        side.arrive(cp, j, b)
+        if ahead:
+            side.send(cp, *ahead.pop(0))
 
         def value(r):
-            return sums[b, r, :]
+            return side.value(b, r)
 
         def store(r, term, more):
             out[r, :] = out[r, :] + term if more else term
 
         chain_reduce(
-            pc,
-            cp,
-            ups[m] + b,
-            downs[m] + b,
-            b,
-            j == chain - 1,
-            value,
-            zsend,
-            lrecv,
-            rrecv,
-            store,
-            out.shape[0],
-            pl.ds(0, out.shape[1]),
+            pc, cp, up + b, down + b, b, j == chain - 1, value, zsend, came, store, side.rows, pl.ds(0, side.width)
         )
         yield
     cp.finish()
@@ -552,37 +566,53 @@
     ]
 
 
-def collect(pc, sems, parts, scratches, outs):
-    chain, groups, z = pc.chain, pc.groups, pc.z
-    count = len(parts)
+def collect(pc, sems, part, scratch, out, window=2):
+    recv, sums = scratch
+    chain, z = pc.chain, pc.z
     cp = Copies(sems)
-    bases = [sems.take(chain * groups) for _ in range(count)]
-    along = [sems.take(chain) for _ in range(count)]
-    order = [(k, (z + chain - 1 - k) % chain) for k in range(chain)]
-    kept = []
-
-    def put(m, b, r, total):
-        scratches[m][1][b, r, :] = total.astype(BF)
-
-    for made in side_sums(pc, cp, bases, parts, [s[0] for s in scratches], order, put, 3):
-        if made is None:
+    side = Side(pc, sems, part, recv)
+    along = sems.take(chain)
+    todo = [(k, (z + chain - 1 - k) % chain) for k in range(chain)]
+    ahead = list(todo)
+    for _ in range(min(window, chain)):
+        side.send(cp, *ahead.pop(0))
+    yield "own"
+    for k, b in todo:
+        side.arrive(cp, k, b)
+        if ahead:
+            side.send(cp, *ahead.pop(0))
+
+        def add(r):
+            sums[b, r, :] = side.value(b, r).astype(BF)
+
+        each_rows(side.rows, add)
+        if k < chain - 1:
+            cp.go(along + k, sums.at[b], out.at[z], pc.at(z=b))
+        else:
+            keep = cp.keep(along + k, sums.at[b], out.at[z])
+        yield "more"
+    yield "tail"
+    for k in range(chain - 1):
+        b = (z - (chain - 1 - k) + chain) % chain
+        cp.arrive(along + k, out.at[b], pc.at())
+    keep.wait()
+    cp.finish()
+    yield "end"
+
+
+def follow(tasks):
+    next(tasks[0])
+    yield
+    for i, task in enumerate(tasks):
+        steps = 0
+        while next(task, "tail") != "tail":
+            steps += 1
+            if steps == 2 and i + 1 < len(tasks):
+                next(tasks[i + 1])
             yield
-            continue
-        m, k, b = made
-        block = scratches[m][1].at[b]
-        if k < chain - 1:
-            cp.go(along[m] + k, block, outs[m].at[z], pc.at(z=b))
-        else:
-            kept.append(cp.keep(along[m] + k, block, outs[m].at[z]))
-        yield
-    for m in range(count):
-        for k in range(chain - 1):
-            b = (z - (chain - 1 - k) + chain) % chain
-            cp.arrive(along[m] + k, outs[m].at[b], pc.at())
-    for copy in kept:
-        copy.wait()
-    cp.finish()
-    yield
+    for task in tasks:
+        for _ in task:
+            yield
 
 
 def share_gains(pc, sems, own, table):
@@ -671,7 +701,7 @@
         name=name,
         cost_estimate=pl.CostEstimate(flops=0, bytes_accessed=cost, transcendentals=0),
         compiler_params=pltpu.CompilerParams(
-            collective_id=number, has_side_effects=True, vmem_limit_bytes=58 << 20
+            collective_id=number, has_side_effects=True, vmem_limit_bytes=63 << 20
         ),
     )(*operands)
 
@@ -717,7 +747,7 @@
             & (kpos <= qpos[...])
             & ((kmark[:, cols] == 1) | (kpos == qpos[...]))
         )
-        bias[:, cols] = jnp.where(allowed, 0.0, NEG)
+        bias[:, cols] = jnp.where(allowed, 0.0, NEG).astype(BF)
         return carry
 
     lax.fori_loop(low, high, fill, 0)
@@ -757,7 +787,7 @@
 
             def body(j, carry):
                 cols = pl.ds(pl.multiple_of(j * size, size), size)
-                key, value, mask = kk[cols, :], vv[cols, :], bias[rows, cols]
+                key, value, mask = kk[cols, :], vv[cols, :], bias[rows, cols].astype(F32)
                 out = []
                 for q, (top, tot, acc) in zip(heads, carry):
                     s = lax.dot_general(q, key, (((1,), (1,)), ((), ())), preferred_element_type=F32) + mask
@@ -806,16 +836,17 @@
         wdown_all,
         cot_all,
         query,
-        kv_all,
+        kk,
+        vv,
         mixed,
         mixed_low,
         lse,
         middle,
         two_all,
-    ) = refs[14:29]
-    rest = refs[29:]
-    table, normed, own_kv, kk, vv, bias, part, total, two = rest[:9]
-    scratch, (send, recv) = rest[9:15], rest[15:]
+    ) = refs[14:30]
+    rest = refs[30:]
+    table, normed, own_kv, kv_all, bias, part, total, two = rest[:8]
+    scratch, (send, recv) = rest[8:13], rest[13:]
     sems = Sems(send, recv)
     pc, near = Place(chain), Place(1)
     rows, width = tok.shape
@@ -894,86 +925,260 @@
     behind.drain()
 
 
-def back_kernel(chain, *refs):
-    (npart, opart, ggate, gup, gdown, middle, cot, gains) = refs[:8]
-    (layer_out, middle_grad, branch_all, gain_out, cgate, cup, cdown) = refs[8:15]
+def dot_nt(a, b):
+    return lax.dot_general(a, b, (((1,), (1,)), ((), ())), preferred_element_type=F32)
+
+
+def dot_tn(a, b):
+    return lax.dot_general(a, b, (((0,), (0,)), ((), ())), preferred_element_type=F32)
+
+
+def grads_into(left, right, out, size=256):
+    def body(j, carry):
+        at = pl.ds(pl.multiple_of(j * size, size), size)
+        out[at, :] = dot_tn(left[:, at], right[...]).astype(BF)
+        return carry
+
+    lax.fori_loop(0, out.shape[0] // size, body, 0)
+
+
+def norm_back(r, v, grad, gain, extra, gain_acc):
+    root = unit(v)
+    xhat = v * root
+    e = grad * gain
+    gain_acc[...] += grad * xhat
+    return extra + root * (e - xhat * jnp.mean(e * xhat, axis=-1, keepdims=True))
+
+
+def feed_kernel(chain, *refs):
+    (two, cotan, wgate, wup, wdown, middle, cot, gains) = refs[:8]
+    (opart, middle_grad, branch_all, gain_out, cgate, cup, cdown) = refs[8:15]
     rest = refs[15:]
-    s_one, s_two = rest[:6], rest[6:12]
+    npart, hidden, dgate, dup, ggate, gup, gdown = rest[:7]
+    s_part = rest[7:12]
     s_gate, s_up, s_down = rest[12:14], rest[14:16], rest[16:18]
-    ngrad, osum, branch, gain_acc, send, recv = rest[18:]
+    ngrad, branch, gain_acc, send, recv = rest[18:]
     sems = Sems(send, recv)
     pc, near = Place(chain), Place(1)
     greet(pc)
     rows = middle.shape[0]
-
-    def go():
-        yield from plane_reduce(pc, sems, npart, s_one, ngrad)
-        gain_acc[...] = jnp.zeros_like(gain_acc)
-
-        def back(r):
-            m = middle[r, :]
-            root = unit(m)
-            xhat = m * root
-            g = ngrad[r, :]
-            e = g * gains[1:2, :]
-            grad = cot[r, :].astype(F32) + root * (e - xhat * jnp.mean(e * xhat, axis=-1, keepdims=True))
-            middle_grad[r, :] = grad
-            branch[r, :] = grad.astype(BF)
-            gain_acc[...] += g * xhat
-
-        each_rows(rows, back)
-        yield from plane_gather(near, sems, branch, branch_all)
-        gain_out[...] = jnp.broadcast_to(jnp.sum(gain_acc[...], axis=0, keepdims=True), gain_out.shape)
-
-    def last():
-        yield from plane_reduce(pc, sems, opart, s_two, osum)
-
-        def finish(r):
-            layer_out[r, :] = (middle[r, :] + osum[r, :]).astype(BF)
-
-        each_rows(rows, finish)
-
-    run(
-        go(),
-        collect(pc, sems, (ggate, gup, gdown), (s_gate, s_up, s_down), (cgate, cup, cdown)),
-        last(),
+    n_t = npart.shape[1]
+    local = n_t * rows
+    reduce = PlaneReduce(pc, sems, npart, s_part, ngrad)
+
+    def tile(j, carry):
+        b = far_first(chain, pc.z, j)
+        at = pl.ds(pl.multiple_of(b * local, local), local)
+        x = two[at, :]
+        g = jnp.dot(x, wgate[...], preferred_element_type=F32)
+        u = jnp.dot(x, wup[...], preferred_element_type=F32)
+        sigma = 1.0 / (1.0 + jnp.exp(-g))
+        silu = g * sigma
+        hidden[at, :] = (silu * u).astype(BF)
+        h = jnp.dot(cotan[at, :], wdown[...], preferred_element_type=F32)
+        dg = (h * u * sigma * (1.0 + g * (1.0 - sigma))).astype(BF)
+        du = (h * silu).astype(BF)
+        dgate[at, :] = dg
+        dup[at, :] = du
+
+        def back(i, inner):
+            cols = pl.ds(pl.multiple_of(i * 256, 256), 256)
+            value = (dot_nt(dg, wgate[cols, :]) + dot_nt(du, wup[cols, :])).astype(BF)
+            for s in range(n_t):
+                npart[b, s, :, cols] = value[s * rows : (s + 1) * rows]
+            return inner
+
+        lax.fori_loop(0, two.shape[1] // 256, back, 0)
+        mine = Copies(sems)
+        reduce.pass_core(1, j, b, mine)
+        reduce.pass_core(0, j, b, mine)
+
+        @pl.when(j > 0)
+        def _():
+            reduce.cross(j - 1, far_first(chain, pc.z, j - 1), mine)
+
+        return carry
+
+    lax.fori_loop(0, chain, tile, 0)
+    reduce.cross(chain - 1, pc.z, Copies(sems))
+    steps = reduce.steps(True)
+    grads_into(two, dgate, ggate)
+    behind = Behind(
+        follow(
+            [
+                collect(pc, sems, ggate, s_gate, cgate),
+                collect(pc, sems, gup, s_up, cup),
+                collect(pc, sems, gdown, s_down, cdown),
+            ]
+        )
     )
-
-
-def key_grads_kernel(chain, part, out, *rest):
-    scratch, (send, recv) = rest[:5], rest[5:]
-    sems = Sems(send, recv)
-    pc = Place(chain)
-    greet(pc)
-    run(dp_reduce(pc, sems, (part,), (scratch,), (out,)))
-
-
-def end_kernel(chain, *refs):
-    (part, gqkv, gwout, tok, middle_grad, gains, gain_two) = refs[:7]
-    (input_grad, qkv_out, wout_out, gain_out) = refs[7:11]
-    rest = refs[11:]
-    s_part, s_qkv, s_out = rest[:6], rest[6:11], rest[11:16]
-    total, gain_acc, by_group, stage, mid, second, send, recv = rest[16:]
+    behind()
+    next(steps)
+    grads_into(two, dup, gup)
+    behind()
+    next(steps)
+    grads_into(cotan, hidden, gdown)
+    behind()
+    next(steps)
+
+    def out_tile(i, carry):
+        cols = pl.ds(pl.multiple_of(i * 256, 256), 256)
+        for b in range(chain):
+            value = dot_nt(hidden[b * local : (b + 1) * local, :], wdown[cols, :]).astype(BF)
+            for s in range(n_t):
+                opart[b, s, :, cols] = value[s * rows : (s + 1) * rows]
+        return carry
+
+    lax.fori_loop(0, two.shape[1] // 256, out_tile, 0)
+    behind.along(steps)
+    gain_acc[...] = jnp.zeros_like(gain_acc)
+
+    def back(r):
+        grad = norm_back(r, middle[r, :], ngrad[r, :], gains[1:2, :], cot[r, :].astype(F32), gain_acc)
+        middle_grad[r, :] = grad
+        branch[r, :] = grad.astype(BF)
+
+    each_rows(rows, back)
+    behind.along(plane_gather(near, sems, branch, branch_all))
+    gain_out[...] = jnp.broadcast_to(jnp.sum(gain_acc[...], axis=0, keepdims=True), gain_out.shape)
+    behind.drain()
+
+
+def attend_back(pc, query, dmix, mixed, lse, kk, vv, bias, dsum, dquery, step):
+    local, total = query.shape[0], kk.shape[0]
+    size = gcd_of(total, 256)
+    tile = local // 2
+    left = lax.broadcasted_iota(jnp.int32, (tile, 128), 1) < 64
+    even = jnp.where(halves(), 1.0, 0.0).astype(BF)
+    odd = jnp.where(halves(), 0.0, 1.0).astype(BF)
+    for i in range(local // tile):
+        rows = slice(i * tile, (i + 1) * tile)
+        low, high = key_range(pc.d * local + i * tile, tile, total, size)
+        for chunk in range(query.shape[1] // 128):
+            lanes = slice(chunk * 128, (chunk + 1) * 128)
+            q, dm = query[rows, lanes], dmix[rows, lanes]
+            product = dm.astype(F32) * mixed[rows, lanes]
+            heads = []
+            for k, pick in enumerate((even, odd)):
+                mask = left if k == 0 else jnp.logical_not(left)
+                delta = jnp.sum(jnp.where(mask, product, 0.0), axis=1, keepdims=True)
+                heads.append((q * pick, dm * pick, lse[rows, 2 * chunk + k : 2 * chunk + k + 1], delta))
+
+            def body(j, carry):
+                cols = pl.ds(pl.multiple_of(j * size, size), size)
+                key, value, mask = kk[cols, :], vv[cols, :], bias[rows, cols].astype(F32)
+                out = []
+                dk = jnp.zeros((size, 128), F32)
+                dv = jnp.zeros((size, 128), F32)
+                for (qh, dh, top, delta), acc in zip(heads, carry):
+                    p = jnp.exp(dot_nt(qh, key) + mask - top)
+                    dp = dot_nt(dh, value)
+                    ds = (p * (dp - delta)).astype(BF)
+                    dk = dk + dot_tn(ds, qh)
+                    dv = dv + dot_tn(p.astype(BF), dh)
+                    out.append(acc + jnp.dot(ds, key, preferred_element_type=F32))
+                dsum[cols, :] += jnp.where(halves(), dk + pltpu.roll(dk, 64, 1), dv + pltpu.roll(dv, 64, 1))
+                return tuple(out)
+
+            zero = jnp.zeros((tile, 128), F32)
+            acc0, acc1 = lax.fori_loop(low, high, body, (zero, zero))
+            dquery[rows, lanes] = jnp.where(left, acc0, acc1)
+            step()
+
+
+def low_rows(full, low):
+    size = gcd_of(full.shape[0], 256)
+
+    def body(j, carry):
+        r = pl.ds(pl.multiple_of(j * size, size), size)
+        low[r, :] = full[r, :].astype(BF)
+        return carry
+
+    lax.fori_loop(0, full.shape[0] // size, body, 0)
+
+
+def zero_rows(*refs):
+    size = gcd_of(refs[0].shape[0], 256)
+
+    def body(j, carry):
+        r = pl.ds(pl.multiple_of(j * size, size), size)
+        for ref in refs:
+            ref[r, :] = jnp.zeros((size, ref.shape[1]), ref.dtype)
+        return carry
+
+    lax.fori_loop(0, refs[0].shape[0] // size, body, 0)
+
+
+def backward_kernel(chain, *refs):
+    (branch, wout, wqkv, normed, query, kk, vv, mixed, mixed_low, lse) = refs[:10]
+    (tok, middle_grad, gains, gain_two, middle, opart) = refs[10:16]
+    (cosine, sine, qseg, qpos, kseg, kmark) = refs[16:22]
+    (layer_out, input_grad, qkv_out, kv_out, wout_out, gain_out) = refs[22:28]
+    rest = refs[28:]
+    (bias, dmix, dsum, dkv, dquery, dkv_own, dqkv, gwo, gq, gkv, part, osum, gain_acc) = rest[:13]
+    rest = rest[13:]
+    s_out, s_near = rest[:5], rest[5:10]
+    s_gwo, s_gq, s_gkv, s_keys = rest[10:13], rest[13:16], rest[16:19], rest[19:22]
+    by_group, stage, mid, second, send, recv = rest[22:]
     sems = Sems(send, recv)
     pc, near = Place(chain), Place(1)
+    rows, width = tok.shape
+    local, wide = query.shape
     greet(pc)
 
-    def go():
-        yield from plane_reduce(near, sems, part, s_part, total)
+    def finish():
+        yield from plane_reduce(pc, sems, opart, s_out, osum)
+
+        def add(r):
+            layer_out[r, :] = (middle[r, :] + osum[r, :]).astype(BF)
+
+        each_rows(rows, add)
+
+    whole = branch[...]
+    grads_into(branch, mixed_low, gwo)
+    behind = Behind(rounds(dp_reduce(pc, sems, gwo, s_gwo, wout_out), finish()))
+    behind()
+    for at in range(0, wide, 256):
+        dmix[:, at : at + 256] = jnp.dot(whole, wout[:, at : at + 256], preferred_element_type=F32).astype(BF)
+    size = gcd_of(kk.shape[0], 256)
+    low, high = key_range(pc.d * local, local, kk.shape[0], size)
+    fill_bias(bias, low, high, size, qseg, qpos, kseg, kmark)
+    zero_rows(dsum)
+    attend_back(pc, query, dmix, mixed, lse, kk, vv, bias, dsum, dquery, behind)
+    low_rows(dsum, dkv)
+    keys = dp_reduce(pc, sems, dkv, s_keys, dkv_own)
+    next(keys)
+    for at in range(0, wide, 128):
+        turned = turn(dquery[:, at : at + 128] * 0.125, cosine[...], -sine[...])
+        dqkv[:, at : at + 128] = turned.astype(BF)
+    def query_grads(j, carry):
+        at = pl.ds(pl.multiple_of(j * 256, 256), 256)
+        left = jnp.concatenate([normed[0, s, :, at] for s in range(normed.shape[1])], axis=0)
+        gq[at, :] = dot_tn(left, dqkv[:, :wide]).astype(BF)
+        return carry
+
+    lax.fori_loop(0, width // 256, query_grads, 0)
+    last = [dp_reduce(pc, sems, gq, s_gq, qkv_out), dp_reduce(pc, sems, gkv, s_gkv, kv_out)]
+    behind.along(keys)
+    next(last[0])
+    pre = dkv_own[...]
+    dqkv[:, wide : wide + 128] = jnp.where(halves(), turn(pre, cosine[...], -sine[...]), pre).astype(BF)
+
+    def put(cols, value):
+        for s in range(part.shape[1]):
+            part[0, s, :, cols] = value[s * rows : (s + 1) * rows].astype(BF)
+
+    tiled_nt(dqkv[...], wqkv, put)
+
+    def ending():
+        yield from plane_reduce(near, sems, part, s_near, input_grad)
         gain_acc[...] = jnp.zeros_like(gain_acc)
 
         def back(r):
             v = tok[r, :].astype(F32)
-            root = unit(v)
-            xhat = v * root
-            g = total[r, :]
-            e = g * gains[0:1, :]
-            input_grad[r, :] = middle_grad[r, :] + root * (
-                e - xhat * jnp.mean(e * xhat, axis=-1, keepdims=True)
-            )
-            gain_acc[...] += g * xhat
-
-        each_rows(total.shape[0], back)
+            input_grad[r, :] = norm_back(r, v, input_grad[r, :], gains[0:1, :], middle_grad[r, :], gain_acc)
+
+        each_rows(rows, back)
         own = jnp.sum(gain_acc[...], axis=0, keepdims=True)
         row = lax.broadcasted_iota(jnp.int32, (8, 128), 0)
         for j in range(by_group.shape[0]):
@@ -981,117 +1186,23 @@
             by_group[j] = jnp.where(row == 0, jnp.broadcast_to(own[:, cols], (8, 128)), gain_two[:, cols])
         yield from sum_gains(pc, sems, by_group, stage, mid, second, gain_out)
 
-    run(
-        go(),
-        dp_reduce(pc, sems, (gwout, gqkv), (s_out, s_qkv), (wout_out, qkv_out)),
-    )
-
-
-def attend_back_kernel(bounds, q, dmix, lse, delta, k, v, qseg, qpos, kseg, kmark, dq, dk, dv, bias):
-    size = gcd_of(k.shape[0], 256)
-    scale = q.shape[1] ** -0.5
-
-    @pl.when(pl.program_id(0) == 0)
-    def _():
-        dk[...] = jnp.zeros_like(dk)
-        dv[...] = jnp.zeros_like(dv)
-
-        def fill(j, carry):
-            at = pl.multiple_of(j * size, size)
-            rows = pl.ds(at, size)
-            kpos = at + lax.broadcasted_iota(jnp.int32, (size, 1), 0)
-            same = kpos == qpos[...]
-            allowed = (
-                (kseg[rows, :] == qseg[...]) & (kpos <= qpos[...]) & ((kmark[rows, :] == 1) | same)
-            )
-            bias[rows, :] = jnp.where(allowed, 0.0, NEG)
-            return carry
-
-        lax.fori_loop(bounds[0], bounds[1], fill, 0)
-
-    def step(j, acc):
-        rows = pl.ds(pl.multiple_of(j * size, size), size)
-        kb = k[rows, :]
-        scores = (
-            lax.dot_general(kb, q[...], (((1,), (1,)), ((), ())), preferred_element_type=F32) * scale
-            + bias[rows, :]
-        )
-        probs = jnp.exp(scores - lse[...])
-        pgrad = lax.dot_general(
-            v[rows, :], dmix[...], (((1,), (1,)), ((), ())), preferred_element_type=F32
-        )
-        sgrad = (probs * (pgrad - delta[...])).astype(BF)
-        dk[rows, :] += jnp.dot(sgrad, q[...], preferred_element_type=F32) * scale
-        dv[rows, :] += jnp.dot(probs.astype(BF), dmix[...], preferred_element_type=F32)
-        return acc + lax.dot_general(sgrad, kb, (((0,), (0,)), ((), ())), preferred_element_type=F32)
-
-    acc = lax.fori_loop(bounds[0], bounds[1], step, jnp.zeros(dq.shape, F32))
-    dq[...] = acc * scale
-
-
-def attend_back(bounds, q, dmix, lse, delta, k, v, qseg, qpos, kseg, kmark):
-    heads, rows, dim = q.shape
-    keys = k.shape[0]
-
-    def whole(shape):
-        return pl.BlockSpec(shape, lambda h, b: (0, 0))
-
-    def head(shape):
-        return pl.BlockSpec((pl.Squeezed(),) + shape, lambda h, b: (h, 0, 0))
-
-    return pl.pallas_call(
-        attend_back_kernel,
-        out_shape=[
-            jax.ShapeDtypeStruct((heads, rows, dim), F32),
-            jax.ShapeDtypeStruct((keys, dim), F32),
-            jax.ShapeDtypeStruct((keys, dim), F32),
-        ],
-        grid_spec=pltpu.PrefetchScalarGridSpec(
-            num_scalar_prefetch=1,
-            grid=(heads,),
-            in_specs=[
-                head((rows, dim)),
-                head((rows, dim)),
-                head((1, rows)),
-                head((1, rows)),
-                whole((keys, dim)),
-                whole((keys, dim)),
-                whole((1, rows)),
-                whole((1, rows)),
-                whole((keys, 1)),
-                whole((keys, 1)),
-            ],
-            out_specs=[head((rows, dim)), whole((keys, dim)), whole((keys, dim))],
-            scratch_shapes=[pltpu.VMEM((keys, rows), F32)],
-        ),
-        name="attend_back",
-        compiler_params=pltpu.CompilerParams(vmem_limit_bytes=56 << 20),
-    )(bounds, q, dmix, lse, delta, k, v, qseg, qpos, kseg, kmark)
+    end = ending()
+    next(end)
+
+    def key_grads(j, carry):
+        at = pl.ds(pl.multiple_of(j * 256, 256), 256)
+        left = jnp.concatenate([normed[0, s, :, at] for s in range(normed.shape[1])], axis=0)
+        gkv[at, :] = dot_tn(left, dqkv[:, wide : wide + 128]).astype(BF)
+        return carry
+
+    lax.fori_loop(0, width // 256, key_grads, 0)
+    run(end, *last, behind.task)
 
 
 def angles(positions, half_dim):
     frequency = THETA ** (-jnp.arange(half_dim, dtype=F32) / half_dim)
     turned = positions.astype(F32)[:, None] * frequency[None, :]
     return jnp.cos(turned), jnp.sin(turned)
-
-
-def rotate(values, cosine, sine):
-    half = values.shape[-1] // 2
-    a, b = values[..., :half], values[..., half:]
-    cosine, sine = cosine[:, None, :], sine[:, None, :]
-    return jnp.concatenate([a * cosine - b * sine, b * cosine + a * sine], axis=-1)
-
-
-def mm(a, b):
-    return jnp.dot(a, b, preferred_element_type=F32)
-
-
-def mm_tn(a, b):
-    return lax.dot_general(a, b, (((0,), (0,)), ((), ())), preferred_element_type=F32)
-
-
-def mm_nt(a, b):
-    return lax.dot_general(a, b, (((1,), (1,)), ((), ())), preferred_element_type=F32)
 
 
 def shards(
@@ -1143,6 +1254,8 @@
     nbytes = 60 << 20
     positions = first_row + jnp.arange(local, dtype=jnp.int32)
     cosine, sine = angles(positions, dim // 2)
+    cosine = jnp.tile(cosine, (1, 4))
+    sine = jnp.tile(jnp.concatenate([-sine, sine], axis=1), (1, 2))
     own_segments = lax.dynamic_slice(segment_ids, (first_row,), (local,))
     wide = heads * dim
     (
@@ -1155,7 +1268,8 @@
         wdown,
         cot,
         query,
-        kv,
+        kk,
+        vv,
         mixed,
         mixed_low,
         lse,
@@ -1176,7 +1290,8 @@
             ((width, units), BF, ANY),
             ((chain, n_t, rows, width), BF, ANY),
             ((local, wide), BF, VM),
-            ((total, 2 * dim), BF, VM),
+            ((total, 128), BF, VM),
+            ((total, 128), BF, VM),
             ((local, wide), F32, VM),
             ((local, wide), BF, VM),
             ((local, 128), F32, VM),
@@ -1188,8 +1303,7 @@
             pltpu.VMEM((rows, width), BF),
             pltpu.VMEM((local, 2 * dim), BF),
             pltpu.VMEM((total, 128), BF),
-            pltpu.VMEM((total, 128), BF),
-            pltpu.VMEM((local, total), F32),
+            pltpu.VMEM((local, total), BF),
             pltpu.VMEM((1, n_t, rows, width), BF),
             pltpu.VMEM((rows, width), F32),
             pltpu.VMEM((rows, width), BF),
@@ -1204,8 +1318,8 @@
             by_chain(w_up),
             by_chain(w_down.T),
             cotangent,
-            jnp.tile(cosine, (1, 4)),
-            jnp.tile(jnp.concatenate([-sine, sine], axis=1), (1, 2)),
+            cosine,
+            sine,
             own_segments[:, None],
             positions[:, None],
             segment_ids[None],
@@ -1213,65 +1327,39 @@
         ),
         nbytes,
     )
-    normed = normed.reshape(local, width)
-    cot = cot.reshape(plane, width)
-    keys, values = kv[:, :dim], kv[:, dim:]
-    query = (query * 8.0).astype(BF).reshape(local, heads, dim).transpose(1, 0, 2)
-    mixed = mixed.reshape(local, heads, dim).transpose(1, 0, 2)
-    lse = lse[:, :heads].T
-    size = gcd_of(total, 256)
-    start = jnp.sum((segment_ids < own_segments[0]).astype(jnp.int32))
-    bounds = jnp.stack([start // size, (first_row + local + size - 1) // size])
-
-    two = two.reshape(plane, width)
-    gate = mm(two, wgate)
-    up = mm(two, wup)
-    sigma = jax.nn.sigmoid(gate)
-    silu = gate * sigma
-    hidden = (silu * up).astype(BF)
-    hidden_grad = mm(cot, wdown)
-    gate_grad = (hidden_grad * up * sigma * (1.0 + gate * (1.0 - sigma))).astype(BF)
-    up_grad = (hidden_grad * silu).astype(BF)
-    npart = (mm_nt(gate_grad, wgate) + mm_nt(up_grad, wup)).astype(BF)
-    opart = mm_nt(hidden, wdown).astype(BF)
-
-    def by_dp(g):
-        return g.astype(BF).reshape(n_dp, wrows, g.shape[1])
-
-    ggate, gup, gdown = by_dp(mm_tn(two, gate_grad)), by_dp(mm_tn(two, up_grad)), by_dp(mm_tn(cot, hidden))
+    cols_sums = [s for _ in range(3) for s in collect_scratch(chain, groups, wrows, units)]
     block = ((chain, wrows, units), BF, ANY)
-    (layer_out, middle_grad, branch, gain_two, ggate, gup, gdown) = call(
-        functools.partial(back_kernel, chain),
-        "back",
-        3,
+    (opart, middle_grad, branch, gain_two, ggate, gup, gdown) = call(
+        functools.partial(feed_kernel, chain),
+        "feed",
+        1,
         [VM] * 8,
         [
-            ((rows, width), BF, VM),
+            ((chain, n_t, rows, width), BF, VM),
             ((rows, width), F32, VM),
-            ((1, n_t, rows, width), BF, ANY),
+            ((1, n_t, rows, width), BF, VM),
             ((8, width), F32, VM),
             block,
             block,
             block,
         ],
-        plane_scratch(chain, rows, width) * 2
-        + collect_scratch(chain, groups, wrows, units) * 3
+        [
+            pltpu.VMEM((chain, n_t, rows, width), BF),
+            pltpu.VMEM((plane, units), BF),
+            pltpu.VMEM((plane, units), BF),
+            pltpu.VMEM((plane, units), BF),
+            pltpu.VMEM((width, units), BF),
+            pltpu.VMEM((width, units), BF),
+            pltpu.VMEM((width, units), BF),
+        ]
+        + plane_scratch(chain, rows, width)
+        + cols_sums
         + [
-            pltpu.VMEM((rows, width), F32),
             pltpu.VMEM((rows, width), F32),
             pltpu.VMEM((rows, width), BF),
             pltpu.VMEM((16, width), F32),
         ],
-        (
-            npart.reshape(chain, n_t, rows, width),
-            opart.reshape(chain, n_t, rows, width),
-            ggate,
-            gup,
-            gdown,
-            middle,
-            cotangent,
-            gains,
-        ),
+        (two.reshape(plane, width), cot.reshape(plane, width), wgate, wup, wdown, middle, cotangent, gains),
         nbytes,
     )
 
@@ -1280,64 +1368,72 @@
 
     grad_gate, grad_up, grad_down = shard_of(ggate), shard_of(gup), shard_of(gdown).T
 
-    branch = branch.reshape(local, width)
-    gwout = by_dp(mm_tn(branch, mixed_low))
-    mixed_grad = mm(branch, wout).astype(BF).reshape(local, heads, dim).transpose(1, 0, 2)
-    delta = jnp.sum(mixed_grad.astype(F32) * mixed, axis=-1)
-    dq, dk, dv = attend_back(
-        bounds,
-        query,
-        mixed_grad,
-        lse.reshape(heads, 1, local),
-        delta.reshape(heads, 1, local),
-        keys,
-        values,
-        own_segments[None],
-        positions[None],
-        segment_ids[:, None],
-        key_mask[:, None],
-    )
-    dkv = jnp.concatenate([dk, dv], axis=1).astype(BF).reshape(n_dp, local, 2 * dim)
-    (dkv,) = call(
-        functools.partial(key_grads_kernel, chain),
-        "key_grads",
-        4,
-        [VM],
-        [((local, 2 * dim), F32, VM)],
-        dp_scratch(chain, groups, local, 2 * dim),
-        (dkv,),
-        2 << 20,
-    )
-    turn = jnp.concatenate([dq.transpose(1, 0, 2), dkv[:, None, :dim]], axis=1)
-    back = rotate(turn, cosine, -sine).reshape(local, (heads + 1) * dim)
-    qkv_grad = jnp.concatenate([back, dkv[:, dim:]], axis=1).astype(BF)
-    gqkv = by_dp(mm_tn(normed, qkv_grad))
-    part = mm_nt(qkv_grad, wqkv).astype(BF).reshape(1, n_t, rows, width)
     count = max(1, n_t * share // 128)
-    input_grad, gqkv, gwout, gain_sum = call(
-        functools.partial(end_kernel, chain),
-        "end",
-        5,
-        [VM] * 7,
+    layer_out, input_grad, gq, gkv, gwout, gain_sum = call(
+        functools.partial(backward_kernel, chain),
+        "backward",
+        2,
+        [VM] * 22,
         [
+            ((rows, width), BF, VM),
             ((rows, width), F32, VM),
-            ((wrows, qkv), F32, VM),
-            ((wrows, heads * dim), F32, VM),
+            ((wrows, wide), F32, VM),
+            ((wrows, 2 * dim), F32, VM),
+            ((wrows, wide), F32, VM),
             ((8, 128), F32, VM),
         ],
-        plane_scratch(1, rows, width)
-        + dp_scratch(chain, groups, wrows, qkv)
-        + dp_scratch(chain, groups, wrows, heads * dim)
-        + [
+        [
+            pltpu.VMEM((local, total), BF),
+            pltpu.VMEM((local, wide), BF),
+            pltpu.VMEM((total, 128), F32),
+            pltpu.VMEM((total, 128), BF),
+            pltpu.VMEM((local, wide), F32),
+            pltpu.VMEM((local, 128), F32),
+            pltpu.VMEM((local, qkv), BF),
+            pltpu.VMEM((width, wide), BF),
+            pltpu.VMEM((width, wide), BF),
+            pltpu.VMEM((width, 128), BF),
+            pltpu.VMEM((1, n_t, rows, width), BF),
             pltpu.VMEM((rows, width), F32),
             pltpu.VMEM((16, width), F32),
+        ]
+        + plane_scratch(chain, rows, width)
+        + plane_scratch(1, rows, width)
+        + dp_scratch(chain, groups, wrows, wide)
+        + dp_scratch(chain, groups, wrows, wide)
+        + dp_scratch(chain, groups, wrows, 128)
+        + dp_scratch(chain, groups, local, 128)
+        + [
             pltpu.VMEM((width // 128, 8, 128), F32),
             pltpu.VMEM((n_dp, count, 8, 128), F32),
             pltpu.VMEM((count, 8, 128), F32),
             pltpu.VMEM((n_t, 8, 128), F32),
         ],
-        (part, gqkv, gwout, tokens, middle_grad, gains, gain_two),
-        nbytes // 2,
+        (
+            branch.reshape(local, width),
+            wout,
+            wqkv,
+            normed,
+            query,
+            kk,
+            vv,
+            mixed,
+            mixed_low,
+            lse,
+            tokens,
+            middle_grad,
+            gains,
+            gain_two,
+            middle,
+            opart,
+            cosine,
+            sine,
+            own_segments[:, None],
+            positions[:, None],
+            segment_ids[None],
+            key_mask[None],
+        ),
+        nbytes,
     )
     lane = (me * n_t + lax.axis_index("tensor")) * share % 128
     gain_grads = lax.dynamic_slice(gain_sum, (0, lane), (2, share))
@@ -1345,9 +1441,9 @@
         layer_out,
         input_grad,
         gain_grads[0],
-        gqkv[:, : heads * dim],
-        gqkv[:, heads * dim : (heads + 1) * dim],
-        gqkv[:, (heads + 1) * dim :],
+        gq,
+        gkv[:, :dim],
+        gkv[:, dim:],
         gwout.T,
         gain_grads[1],
         grad_gate,

time: 538 us -> 469 us (0.87); the launches traced: 531 us -> 469 us
  matrix products: 47.2 us -> 0 us
  local copies, waits for them, and re-layouts: 46.1 us -> 27.8 us
  Pallas kernels: 422 us -> 436 us
  other arithmetic: 10.8 us -> 4.11 us
    dot_general x13 -> x0, matrix products: 47.2 us -> none  [the longest x5 17.5 us: mm_tn(): lax.dot_general(a, b, (((0,), (0,)), ((), ())), preferred_element_type=F32)]
    pallas_call x4 -> x3, Pallas kernels: 408 us -> 436 us  [call(): pl.pallas_call(kernel, out_shape=[jax.ShapeDtypeStruct(shape, kind) for s...]
    pallas_call x1 -> x0, Pallas kernels: 14.3 us -> none  [attend_back(): pl.pallas_call(attend_back_kernel, out_shape=[jax.ShapeDtypeStruct((heads...]
    broadcast_in_dim x4 -> x0, local copies, waits for them, and re-layouts: 5.42 us -> none  [the longest x1 1.97 us: shards(): key_mask[:, None]]
    unnamed x86 -> x31, local copies, waits for them, and re-layouts: 13.4 us -> 12.1 us
where the time goes in v3:
time: 469 us
  Pallas kernels  436 us (93%)
  local copies, waits for them, and re-layouts  27.8 us (6%)
    pallas_call x3, Pallas kernels, call(): pl.pallas_call(kernel, out_shape=[jax.ShapeDtypeStruct(shape, kind) for s...  436 us
    unnamed x31, local copies, waits for them, and re-layouts  12.1 us

profile of v3, /device:TPU:0, one launch (start us, length us, event | category | flops | bytes accessed | tf_op | source)
XLA Modules:
  0.0 468.8 jit_solution(14038005836373636989)
XLA Ops:
  0.6 0.0 copy-start.7
  0.7 0.0 copy-start.8
  0.7 0.1 pad.7.clone
  0.8 0.7 tile.12
  1.4 0.1 broadcast_in_dim_tile.6
  1.5 0.7 tile.13
  2.2 0.1 broadcast_in_dim_tile.7
  2.3 0.8 dynamic_slice.6
  3.0 0.7 maximum_maximum_fusion.refs_1_
  3.7 1.3 broadcast_in_dim.22.refs_13_.refs_21_
  5.0 1.3 broadcast_in_dim.10.refs_12_.refs_20_
  6.3 0.9 copy.30
  7.2 0.9 copy.31
  8.1 0.0 copy-start.1
  8.1 0.3 fusion
  8.4 0.8 copy.39.refs_9_.refs_17_
  9.2 0.8 broadcast_in_dim.23.refs_10_.refs_18_
  10.0 0.7 iota_add_fusion.refs_11_.refs_19_
  10.6 0.8 copy.38.refs_8_.refs_16_
  11.4 0.0 copy-done.8
  11.4 0.8 pad_maximum_fusion.refs_2_
  12.2 0.0 copy-done.7
  12.3 0.8 copy.32
  13.1 0.3 copy.33
  13.4 1.2 copy.34
  14.5 0.3 copy.35
  14.8 1.2 copy.36
  16.0 1.2 copy.37
  17.1 180.6 %forward.1 = (bf16[1,4,80,2048]{3,2,1,0:T(8,128)(2,1)}, f32[8,2048]{1,0:T(8,128)}, bf16[2048,640]{1,0:T(8,128)(2,1)}, bf16[2048,512]{1,0:T(8,128)(2,1)}, bf16[20...) custom-call(bf16[80,2048]{1,0:T(8,128)(2,1)} %refs_10_.1, ...), custom_call_target="tpu_custom_call" | custom-call | bytes 62914560 | tf_op jit(solution)/shard_map/forward/pallas_call | solution.py:695
  197.7 121.5 %feed.1 = (bf16[4,4,80,2048]{3,2,1,0:T(8,128)(2,1)}, f32[80,2048]{1,0:T(8,128)}, bf16[1,4,80,2048]{3,2,1,0:T(8,128)(2,1)}, f32[8,2048]{1,0:T(8,128)}, bf16[4,256...) custom-call(bf16[1280,2048]{1,0:T(8,128)(2,1)} %bitcast.33, ...), custom_call_target="tpu_custom_call" | custom-call | bytes 62914560 | tf_op jit(solution)/shard_map/feed/pallas_call | solution.py:695
  319.3 134.0 %backward.1 = (bf16[80,2048]{1,0:T(8,128)(2,1)}, f32[80,2048]{1,0:T(8,128)}, f32[256,512]{1,0:T(8,128)}, f32[256,128]{1,0:T(8,128)}, f32[256,512]{1,0:T(8,128)}, /*index=5*/f32[8,128]{1,0:T(8,128)}) custom-call(bf16[320,2048]{1,0:T(8,128)(2,1)} %bitcast.40, bf16[2048,512]{1,0:T(8,128)(2,1)} %get-tuple-element.48.refs_1_, ...), custom_call_target="tpu_custom_call" | custom-call | bytes 62914560 | tf_op jit(solution)/shard_map/backward/pallas_call | solution.py:695
  453.2 0.8 constant_dynamic-slice_fusion
  454.1 0.5 slice_bitcast_fusion
  454.6 1.1 fusion.1
  455.7 0.7 copy.48
  456.4 0.7 copy.47
  457.1 2.0 copy.49
  459.1 0.1 convert_bitcast_fusion.2
  459.2 0.5 copy.44
  459.7 1.5 copy.50
  461.3 1.6 convert_bitcast_fusion
  462.8 1.6 copy.46
  464.4 0.5 copy.45
  464.9 1.5 copy.51
  466.4 0.7 copy.55
  467.2 0.0 copy-done.4
  467.2 0.8 copy.56
  468.0 0.8 copy.57
  (18 shorter events, 0.1 us)
Async XLA Ops:
  0.6 11.6 %copy-start.7 = (bf16[512,256]{1,0:T(8,128)(2,1)S(1)}, bf16[512,256]{1,0:T(8,128)(2,1)}, u32[]{:S(2)}) copy-start(bf16[512,256]{1,0:T(8,128)(2,1)} %param.20) | copy-start | bytes 786436
  0.7 10.8 %copy-start.8 = (bf16[256,512]{1,0:T(8,128)(2,1)S(1)}, bf16[256,512]{1,0:T(8,128)(2,1)}, u32[]{:S(2)}) copy-start(bf16[256,512]{1,0:T(8,128)(2,1)} %param.17) | copy-start | bytes 786436
  8.1 5.0 %copy-start.1 = (bf16[256,1408]{1,0:T(8,128)(2,1)S(1)}, bf16[256,1408]{1,0:T(8,128)(2,1)}, u32[]{:S(2)}) copy-start(bf16[256,1408]{1,0:T(8,128)(2,1)} %param.22) | copy-start | bytes 2162692
  13.1 1.4 copy-start.2
  14.5 1.4 copy-start.3
  453.2 5.9 %copy-start = (bf16[4,256,352]{2,1,0:T(8,128)(2,1)S(1)}, bf16[4,256,352]{2,1,0:T(8,128)(2,1)}, u32[]{:S(2)}) copy-start(bf16[4,256,352]{2,1,0:T(8,128)(2,1)} %get-tuple-element.66) | copy-start | bytes 2162692
  464.9 1.6 copy-start.6
  464.9 2.3 copy-start.4
  466.4 1.6 copy-start.5

commit v4 on v3

--- a/solution.py
+++ b/solution.py
@@ -18,7 +18,7 @@
 
 
 def sem_count():
-    return 200 + 12 * lax.axis_size("dp")
+    return 200 + 18 * lax.axis_size("dp")
 
 
 class Sems:
@@ -131,48 +131,23 @@
         live = [task for task in live if next(task, "end") != "end"]
 
 
-def pipeline(tasks):
-    next(tasks[0])
-    next(tasks[0])
-    yield
-    for i, task in enumerate(tasks):
-        ahead = i + 1 < len(tasks)
-        while next(task, "tail") != "tail":
-            if ahead:
-                next(tasks[i + 1])
-                next(tasks[i + 1])
-                ahead = False
-            yield
-        if ahead:
-            next(tasks[i + 1])
-            next(tasks[i + 1])
-        yield
-    for task in tasks:
-        for _ in task:
-            yield
-
-
-def rounds(*tasks):
-    live = list(tasks)
-    while live:
-        live = [task for task in live if next(task, "end") != "end"]
-        yield
-
-
-class Behind:
-    def __init__(self, task):
-        self.task = task
-
-    def __call__(self, steps=1):
-        for _ in range(steps):
-            next(self.task, None)
-
-    def along(self, task, steps=1):
-        for _ in task:
-            self(steps)
+def go(task, steps):
+    for _ in range(steps):
+        next(task, None)
+
+
+class Points:
+    def __init__(self, *acts):
+        self.acts = list(acts)
+
+    def __call__(self):
+        if self.acts:
+            for act in self.acts.pop(0):
+                act()
 
     def drain(self):
-        run(self.task)
+        while self.acts:
+            self()
 
 
 def chain_steps(pc):
@@ -426,35 +401,88 @@
     return PlaneReduce(pc, sems, part, scratch, out).steps()
 
 
-def dp_gather(pc, sems, own, out):
+def dp_gather(pc, sems, own, out, parts=1):
     chain, groups, z, t = pc.chain, pc.groups, pc.z, pc.t
     cp = Copies(sems)
-    base = sems.take(1 + 2 * chain + 2 * chain * groups)
-    along = (base + 1, base + 1 + chain)
-    across = base + 1 + 2 * chain
+    base = sems.take(1 + (2 * chain + 2 * chain * groups) * parts)
+    rows = own.shape[0] // parts
+
+    def cut(ref, p):
+        return ref.at[pl.ds(p * rows, rows)]
+
+    def along(side, k, p):
+        return base + 1 + (side * chain + k) * parts + p
+
+    def across(i, g, p):
+        return base + 1 + (2 * chain + i * groups + g) * parts + p
+
     keep = cp.keep(base, own, out(pc.d))
-    for g in range(1, groups):
-        cp.go(across + g, own, out(pc.d), pc.at(t=(t + g) % groups))
+    for p in range(parts):
+        for g in range(1, groups):
+            cp.go(across(0, g, p), cut(own, p), cut(out(pc.d), p), pc.at(t=(t + g) % groups))
     yield "own"
     if chain > 1:
-        cp.go(along[0], own, out(pc.d), pc.above, z + 1 < chain)
-        cp.go(along[1], own, out(pc.d), pc.below, z > 0)
+        for p in range(parts):
+            cp.go(along(0, 0, p), cut(own, p), cut(out(pc.d), p), pc.above, z + 1 < chain)
+            cp.go(along(1, 0, p), cut(own, p), cut(out(pc.d), p), pc.below, z > 0)
     yield "start"
     landed = [(z, None, 0)]
-    for k, side, b, got, onward, more in chain_steps(pc):
-        i = 1 + k if side == 0 else chain + k
-        block = out(b * groups + t)
-        cp.arrive(along[side] + k, block, pc.at(), got)
-        if k < chain - 2:
-            cp.go(along[side] + k + 1, block, block, onward, more)
-        for g in range(1, groups):
-            cp.go(across + i * groups + g, block, block, pc.at(t=(t + g) % groups), got)
-        landed.append((b, got, i))
-        yield "more"
+    for k in range(chain - 1):
+        for p in range(parts):
+            for step, side, b, got, onward, more in chain_steps(pc):
+                if step != k:
+                    continue
+                i = 1 + k if side == 0 else chain + k
+                block = cut(out(b * groups + t), p)
+                cp.arrive(along(side, k, p), block, pc.at(), got)
+                if k < chain - 2:
+                    cp.go(along(side, k + 1, p), block, block, onward, more)
+                for g in range(1, groups):
+                    cp.go(across(i, g, p), block, block, pc.at(t=(t + g) % groups), got)
+                if p == 0:
+                    landed.append((b, got, i))
+            yield "more"
     yield "tail"
     for b, got, i in landed:
-        for g in range(1, groups):
-            cp.arrive(across + i * groups + g, out(b * groups + (t - g + groups) % groups), pc.at(), got)
+        for p in range(parts):
+            for g in range(1, groups):
+                cp.arrive(across(i, g, p), cut(out(b * groups + (t - g + groups) % groups), p), pc.at(), got)
+    keep.wait()
+    cp.finish()
+    yield "end"
+
+
+def plane_direct(pc, sems, own, out):
+    chain, z, s = pc.chain, pc.z, pc.s
+    cp = Copies(sems)
+    base = sems.take(1 + 4 * chain)
+
+    def sem(kind, k):
+        return base + 1 + kind * chain + k
+
+    keep = cp.keep(base, own, out.at[z, s])
+    cp.go(sem(1, 0), own, out.at[z, s], pc.at(s=pc.sy))
+    cp.go(sem(2, 0), own, out.at[z, s], pc.at(s=pc.sc))
+    yield "own"
+    for k in range(1, chain):
+        to = (z + k) % chain
+        cp.go(sem(0, k), own, out.at[z, s], pc.at(z=to))
+    yield "start"
+    for k in range(1, chain):
+        b = (z - k + chain) % chain
+        cp.arrive(sem(0, k), out.at[b, s], pc.at())
+        cp.go(sem(1, k), out.at[b, s], out.at[b, s], pc.at(s=pc.sy))
+        cp.go(sem(2, k), out.at[b, s], out.at[b, s], pc.at(s=pc.sc))
+    yield "turned"
+    for k in range(chain):
+        b = (z - k + chain) % chain
+        cp.arrive(sem(1, k), out.at[b, pc.sy], pc.at())
+        cp.go(sem(3, k), out.at[b, pc.sy], out.at[b, pc.sy], pc.at(s=pc.sc))
+    yield "crossed"
+    for k in range(chain):
+        b = (z - k + chain) % chain
+        cp.arrive(sem(2, k), out.at[b, pc.sc], pc.at())
+        cp.arrive(sem(3, k), out.at[b, pc.so], pc.at())
     keep.wait()
     cp.finish()
     yield "end"
@@ -525,94 +553,67 @@
     return [
         pltpu.VMEM((max(groups - 1, 1), chain, rows, width), BF),
         pltpu.VMEM((chain, rows, width), BF),
-        pltpu.VMEM((chain + 1, rows, width), BF),
-    ]
-
-
-def dp_reduce(pc, sems, part, scratch, out, window=2):
-    recv, zsend, came = scratch
-    chain, z = pc.chain, pc.z
-    cp = Copies(sems)
-    side = Side(pc, sems, part, recv)
-    up, down = sems.take(chain), sems.take(chain)
-    todo = [(j, far_first(chain, z, j)) for j in range(chain)]
-    ahead = list(todo)
-    for _ in range(min(window, chain)):
-        side.send(cp, *ahead.pop(0))
-    yield
-    for j, b in todo:
-        side.arrive(cp, j, b)
-        if ahead:
-            side.send(cp, *ahead.pop(0))
-
-        def value(r):
-            return side.value(b, r)
-
-        def store(r, term, more):
-            out[r, :] = out[r, :] + term if more else term
-
-        chain_reduce(
-            pc, cp, up + b, down + b, b, j == chain - 1, value, zsend, came, store, side.rows, pl.ds(0, side.width)
-        )
-        yield
-    cp.finish()
-    yield
-
-
-def collect_scratch(chain, groups, rows, width):
-    return [
-        pltpu.VMEM((max(groups - 1, 1), chain, rows, width), BF),
         pltpu.VMEM((chain, rows, width), BF),
     ]
 
 
-def collect(pc, sems, part, scratch, out, window=2):
-    recv, sums = scratch
-    chain, z = pc.chain, pc.z
-    cp = Copies(sems)
-    side = Side(pc, sems, part, recv)
-    along = sems.take(chain)
-    todo = [(k, (z + chain - 1 - k) % chain) for k in range(chain)]
-    ahead = list(todo)
-    for _ in range(min(window, chain)):
-        side.send(cp, *ahead.pop(0))
-    yield "own"
-    for k, b in todo:
-        side.arrive(cp, k, b)
-        if ahead:
-            side.send(cp, *ahead.pop(0))
-
-        def add(r):
-            sums[b, r, :] = side.value(b, r).astype(BF)
-
-        each_rows(side.rows, add)
-        if k < chain - 1:
-            cp.go(along + k, sums.at[b], out.at[z], pc.at(z=b))
-        else:
-            keep = cp.keep(along + k, sums.at[b], out.at[z])
-        yield "more"
-    yield "tail"
-    for k in range(chain - 1):
-        b = (z - (chain - 1 - k) + chain) % chain
-        cp.arrive(along + k, out.at[b], pc.at())
-    keep.wait()
-    cp.finish()
-    yield "end"
-
-
-def follow(tasks):
-    next(tasks[0])
-    yield
-    for i, task in enumerate(tasks):
-        steps = 0
-        while next(task, "tail") != "tail":
-            steps += 1
-            if steps == 2 and i + 1 < len(tasks):
-                next(tasks[i + 1])
-            yield
-    for task in tasks:
-        for _ in task:
-            yield
+class Collect:
+    def __init__(self, pc, sems, part, scratch, out, summed):
+        self.pc, self.out, self.summed = pc, out, summed
+        self.side = Side(pc, sems, part, scratch[0])
+        self.sums = scratch[1]
+        self.came = scratch[2] if summed else out
+        self.cp = Copies(sems)
+        self.along = sems.take(pc.chain)
+        self.kept = None
+
+    def block(self, k):
+        return (self.pc.z + self.pc.chain - 1 - k) % self.pc.chain
+
+    def send(self, *which):
+        for k in which or range(self.pc.chain):
+            self.side.send(self.cp, k, self.block(k))
+
+    def turn(self, *which):
+        pc, chain, z, side = self.pc, self.pc.chain, self.pc.z, self.side
+        for k in which or range(chain):
+            b = self.block(k)
+            side.arrive(self.cp, k, b)
+            if k == chain - 1 and self.summed:
+
+                def first(r):
+                    self.out[r, :] = side.value(b, r)
+
+                each_rows(side.rows, first)
+                continue
+
+            def add(r):
+                self.sums[b, r, :] = side.value(b, r).astype(BF)
+
+            each_rows(side.rows, add)
+            if k < chain - 1:
+                self.cp.go(self.along + k, self.sums.at[b], self.came.at[z], pc.at(z=b))
+            else:
+                self.kept = self.cp.keep(self.along + k, self.sums.at[b], self.out.at[z])
+
+    def finish(self):
+        pc, chain, z, side = self.pc, self.pc.chain, self.pc.z, self.side
+        for k in range(chain - 1):
+            b = (z - (chain - 1 - k) + chain) % chain
+            self.cp.arrive(self.along + k, self.came.at[b], pc.at())
+            if self.summed:
+
+                def add(r):
+                    self.out[r, :] = self.out[r, :] + self.came[b, r, :].astype(F32)
+
+                each_rows(side.rows, add)
+        if self.kept is not None:
+            self.kept.wait()
+        self.cp.finish()
+
+
+def collect_scratch(chain, groups, rows, width):
+    return dp_scratch(chain, groups, rows, width)[:2]
 
 
 def share_gains(pc, sems, own, table):
@@ -747,67 +748,66 @@
             & (kpos <= qpos[...])
             & ((kmark[:, cols] == 1) | (kpos == qpos[...]))
         )
-        bias[:, cols] = jnp.where(allowed, 0.0, NEG).astype(BF)
+        bias[cols, :] = jnp.where(allowed, 0.0, NEG).T.astype(BF)
         return carry
 
     lax.fori_loop(low, high, fill, 0)
 
 
-def spread_lanes(kv, kk, vv):
+def turn_values(kv, vt):
     size = gcd_of(kv.shape[0], 256)
-    left = lax.broadcasted_iota(jnp.int32, (size, 128), 1) < 64
+    vt[64:80, :] = jnp.ones((16, kv.shape[0]), BF)
 
     def body(j, carry):
         r = pl.ds(pl.multiple_of(j * size, size), size)
-        x = kv[r, :].astype(F32)
-        y = pltpu.roll(x, 64, 1)
-        kk[r, :] = jnp.where(left, x, y).astype(BF)
-        vv[r, :] = jnp.where(left, y, x).astype(BF)
+        vt[0:64, r] = kv[r, :].astype(F32).T[64:128, :].astype(BF)
         return carry
 
     lax.fori_loop(0, kv.shape[0] // size, body, 0)
 
 
-def attend(pc, query, kk, vv, bias, mixed, mixed_low, lse, step):
-    local, total = query.shape[0], kk.shape[0]
+def turn_keys(kv, kt):
+    size = gcd_of(kv.shape[0], 256)
+
+    def body(j, carry):
+        r = pl.ds(pl.multiple_of(j * size, size), size)
+        kt[:, r] = kv[r, :].astype(F32).T[0:64, :].astype(BF)
+        return carry
+
+    lax.fori_loop(0, kv.shape[0] // size, body, 0)
+
+
+def attend(pc, query_t, kv, vt, bias, mixed_t, mixed_low, lse, step):
+    local, total = query_t.shape[1], kv.shape[0]
     size = gcd_of(total, 256)
-    tile = local // 2
-    left = lax.broadcasted_iota(jnp.int32, (tile, 128), 1) < 64
-    lane = lax.broadcasted_iota(jnp.int32, (tile, 128), 1)
-    even = jnp.where(halves(), 1.0, 0.0).astype(BF)
-    odd = jnp.where(halves(), 0.0, 1.0).astype(BF)
-    for i in range(local // tile):
-        rows = slice(i * tile, (i + 1) * tile)
-        low, high = key_range(pc.d * local + i * tile, tile, total, size)
-        stats = jnp.zeros((tile, 128), F32)
-        for chunk in range(query.shape[1] // 128):
-            lanes = slice(chunk * 128, (chunk + 1) * 128)
-            both = query[rows, lanes]
-            heads = (both * even, both * odd)
-
-            def body(j, carry):
-                cols = pl.ds(pl.multiple_of(j * size, size), size)
-                key, value, mask = kk[cols, :], vv[cols, :], bias[rows, cols].astype(F32)
-                out = []
-                for q, (top, tot, acc) in zip(heads, carry):
-                    s = lax.dot_general(q, key, (((1,), (1,)), ((), ())), preferred_element_type=F32) + mask
-                    new = jnp.maximum(top, jnp.max(s, axis=1, keepdims=True))
-                    shrink = jnp.exp(top - new)
-                    p = jnp.exp(s - new)
-                    tot = tot * shrink + jnp.sum(p, axis=1, keepdims=True)
-                    acc = acc * shrink + jnp.dot(p.astype(BF), value, preferred_element_type=F32)
-                    out.append((new, tot, acc))
-                return tuple(out)
-
-            start = (jnp.full((tile, 1), NEG, F32), jnp.zeros((tile, 1), F32), jnp.zeros((tile, 128), F32))
-            (top0, tot0, acc0), (top1, tot1, acc1) = lax.fori_loop(low, high, body, (start, start))
-            result = jnp.where(left, acc0 / tot0, acc1 / tot1)
-            mixed[rows, lanes] = result
-            mixed_low[rows, lanes] = result.astype(BF)
-            stats = jnp.where(lane == 2 * chunk, top0 + jnp.log(tot0), stats)
-            stats = jnp.where(lane == 2 * chunk + 1, top1 + jnp.log(tot1), stats)
-            step()
-        lse[rows, :] = stats
+    low, high = key_range(pc.d * local, local, total, size)
+    for chunk in range(query_t.shape[0] // 128):
+        first = chunk * 128
+        queries = (query_t[first : first + 64, :], query_t[first + 64 : first + 128, :])
+
+        def body(j, carry):
+            rows = pl.ds(pl.multiple_of(j * size, size), size)
+            key, value, mask = kv[rows, 0:64], vt[:, rows], bias[rows, :].astype(F32)
+            out = []
+            for q, (top, acc) in zip(queries, carry):
+                s = jnp.dot(key, q, preferred_element_type=F32) + mask
+                new = jnp.maximum(top, jnp.max(s, axis=0, keepdims=True))
+                p = jnp.exp(s - new).astype(BF)
+                acc = acc * jnp.exp(top - new) + jnp.dot(value, p, preferred_element_type=F32)
+                out.append((new, acc))
+            return tuple(out)
+
+        start = (jnp.full((1, local), NEG, F32), jnp.zeros((80, local), F32))
+        done = lax.fori_loop(low, high, body, (start, start))
+        pair = []
+        for k, (top, acc) in enumerate(done):
+            tot = acc[64:65, :]
+            pair.append(acc[0:64, :] / tot)
+            lse[2 * chunk + k : 2 * chunk + k + 1, :] = top + jnp.log(tot)
+        both = jnp.concatenate(pair, axis=0)
+        mixed_t[first : first + 128, :] = both
+        mixed_low[:, first : first + 128] = both.T.astype(BF)
+        step()
 
 
 def tiled_nt(left, right, put, size=256):
@@ -831,21 +831,20 @@
         gains,
         wqkv_all,
         wout_all,
-        wgate_all,
-        wup_all,
+        wgu_all,
         wdown_all,
         cot_all,
         query,
-        kk,
-        vv,
-        mixed,
+        query_t,
+        kv_all,
+        mixed_t,
         mixed_low,
         lse,
         middle,
         two_all,
-    ) = refs[14:30]
-    rest = refs[30:]
-    table, normed, own_kv, kv_all, bias, part, total, two = rest[:8]
+    ) = refs[14:29]
+    rest = refs[29:]
+    table, normed, own_kv, vt, bias, part, total, two = rest[:8]
     scratch, (send, recv) = rest[8:13], rest[13:]
     sems = Sems(send, recv)
     pc, near = Place(chain), Place(1)
@@ -866,30 +865,28 @@
         each_rows(rows, norm)
         yield from plane_gather(near, sems, normed, normed_all)
 
-    first = dp_gather(pc, sems, wqkv, rows_of(wqkv_all, wrows))
-    out_weights = dp_gather(pc, sems, wout, rows_of(wout_all, wrows))
-    behind = Behind(
-        pipeline(
-            [
-                out_weights,
-                spread(pc, sems, lambda d: wgate.at[d], rows_of(wgate_all, wrows)),
-                spread(pc, sems, lambda d: wup.at[d], rows_of(wup_all, wrows)),
-                plane_gather(pc, sems, cot, cot_all, 2),
-                spread(pc, sems, lambda d: wdown.at[d], rows_of(wdown_all, wrows)),
-            ]
-        )
-    )
+    first = dp_gather(pc, sems, wqkv, rows_of(wqkv_all, wrows), 2)
+    outw = dp_gather(pc, sems, wout, rows_of(wout_all, wrows), 2)
+    half = wgu_all.shape[1] // 2
+    gatew = spread(pc, sems, lambda d: wgate.at[d], rows_of(wgu_all.at[:, pl.ds(0, half)], wrows))
+    upw = spread(pc, sems, lambda d: wup.at[d], rows_of(wgu_all.at[:, pl.ds(half, half)], wrows))
+    downw = spread(pc, sems, lambda d: wdown.at[d], rows_of(wdown_all, wrows))
+    cots = plane_gather(pc, sems, cot, cot_all, 2)
     beside = head()
-    next(beside)
-    next(first)
-    next(first)
-    for state in first:
-        next(beside, None)
-        if state == "tail":
-            break
-    behind()
+    go(first, 2)
+    go(beside, 1)
+    go(cots, 1)
+    go(first, 2)
+    go(beside, 1)
+    go(first, 2)
+    go(cots, 1)
+    go(beside, 2)
+    go(first, 3)
+    go(outw, 2)
     run(beside)
     run(first)
+    go(outw, 2)
+    go(cots, 2)
 
     here = jnp.concatenate([normed_all[0, s] for s in range(normed_all.shape[1])], axis=0)
     size = 256
@@ -897,23 +894,37 @@
         pre = jnp.dot(here, wqkv_all[:, at : at + size], preferred_element_type=F32)
         for lanes in range(0, size, 128):
             turned = turn(pre[:, lanes : lanes + 128], cosine[...], sine[...])
-            query[:, at + lanes : at + lanes + 128] = (turned * 0.125).astype(BF)
+            turned = turned * 0.125
+            query[:, at + lanes : at + lanes + 128] = turned.astype(BF)
+            query_t[at + lanes : at + lanes + 128, :] = turned.T.astype(BF)
     pre = jnp.dot(here, wqkv_all[:, wide : wide + 128], preferred_element_type=F32)
     own_kv[...] = jnp.where(halves(), turn(pre, cosine[...], sine[...]), pre).astype(BF)
-    behind.along(dp_gather(pc, sems, own_kv, rows_of(kv_all, local)))
-    spread_lanes(kv_all, kk, vv)
-    low, high = key_range(pc.d * local, local, kk.shape[0], size)
+    go(outw, 2)
+    run(dp_gather(pc, sems, own_kv, rows_of(kv_all, local)))
+    go(gatew, 2)
+    go(outw, 3)
+    go(cots, 2)
+    turn_values(kv_all, vt)
+    low, high = key_range(pc.d * local, local, kv_all.shape[0], size)
     fill_bias(bias, low, high, size, qseg, qpos, kseg, kmark)
-    attend(pc, query, kk, vv, bias, mixed, mixed_low, lse, behind)
-
-    run(out_weights)
+    go(upw, 2)
+    stops = Points(
+        [lambda: go(cots, 2)],
+        [lambda: go(downw, 2)],
+        [lambda: go(gatew, 3)],
+        [lambda: run(outw)],
+    )
+    attend(pc, query_t, kv_all, vt, bias, mixed_t, mixed_low, lse, stops)
+    stops.drain()
+
 
     def put(cols, value):
         for s in range(part.shape[1]):
             part[0, s, :, cols] = value[s * rows : (s + 1) * rows].astype(BF)
 
     tiled_nt(mixed_low[...], wout_all, put)
-    behind.along(plane_reduce(near, sems, part, scratch, total))
+    run(plane_reduce(near, sems, part, scratch, total))
+    go(upw, 3)
 
     def norm(r):
         v = tok[r, :].astype(F32) + total[r, :]
@@ -921,8 +932,13 @@
         two[r, :] = (v * unit(v) * gains[1:2, :]).astype(BF)
 
     each_rows(rows, norm)
-    behind.along(plane_gather(pc, sems, two, two_all, 2))
-    behind.drain()
+    twos = plane_gather(pc, sems, two, two_all, 2)
+    go(twos, 2)
+    go(cots, 3)
+    go(twos, 2)
+    go(downw, 3)
+    run(twos)
+    run(cots, gatew, upw, downw)
 
 
 def dot_nt(a, b):
@@ -951,139 +967,139 @@
 
 
 def feed_kernel(chain, *refs):
-    (two, cotan, wgate, wup, wdown, middle, cot, gains) = refs[:8]
-    (opart, middle_grad, branch_all, gain_out, cgate, cup, cdown) = refs[8:15]
-    rest = refs[15:]
-    npart, hidden, dgate, dup, ggate, gup, gdown = rest[:7]
-    s_part = rest[7:12]
-    s_gate, s_up, s_down = rest[12:14], rest[14:16], rest[16:18]
-    ngrad, branch, gain_acc, send, recv = rest[18:]
+    (two_all, cot_all, wgu_all, wdn_all, middle, cot, gains) = refs[:7]
+    (opart_all, middle_grad, branch_all, gain_out, cgu, cdn) = refs[7:13]
+    rest = refs[13:]
+    two, cotan, wgu, wdn, opart, gu, h, both, hidden, npart, ggu, gdn = rest[:12]
+    s_part = rest[12:17]
+    s_gu, s_dn = rest[17:19], rest[19:21]
+    branch, gain_acc, local_sem, send, recv = rest[21:]
     sems = Sems(send, recv)
     pc, near = Place(chain), Place(1)
+    fetches = []
+    for i, (src, dst) in enumerate(((wgu_all, wgu), (two_all, two), (wdn_all, wdn), (cot_all, cotan))):
+        fetches.append(pltpu.make_async_copy(src, dst, local_sem.at[i]))
+        fetches[-1].start()
     greet(pc)
-    rows = middle.shape[0]
+    rows, width = middle.shape
     n_t = npart.shape[1]
-    local = n_t * rows
-    reduce = PlaneReduce(pc, sems, npart, s_part, ngrad)
-
-    def tile(j, carry):
-        b = far_first(chain, pc.z, j)
-        at = pl.ds(pl.multiple_of(b * local, local), local)
-        x = two[at, :]
-        g = jnp.dot(x, wgate[...], preferred_element_type=F32)
-        u = jnp.dot(x, wup[...], preferred_element_type=F32)
-        sigma = 1.0 / (1.0 + jnp.exp(-g))
-        silu = g * sigma
-        hidden[at, :] = (silu * u).astype(BF)
-        h = jnp.dot(cotan[at, :], wdown[...], preferred_element_type=F32)
-        dg = (h * u * sigma * (1.0 + g * (1.0 - sigma))).astype(BF)
-        du = (h * silu).astype(BF)
-        dgate[at, :] = dg
-        dup[at, :] = du
-
-        def back(i, inner):
+    units = hidden.shape[1]
+    reduce = PlaneReduce(pc, sems, npart, s_part, middle_grad)
+    fetches[0].wait()
+    fetches[1].wait()
+    for at in range(0, 2 * units, 256):
+        gu[:, at : at + 256] = jnp.dot(two[...], wgu[:, at : at + 256], preferred_element_type=F32)
+    fetches[2].wait()
+    fetches[3].wait()
+    for at in range(0, units, 128):
+        h[:, at : at + 128] = jnp.dot(cotan[...], wdn[:, at : at + 128], preferred_element_type=F32)
+
+    def gates(r):
+        for at in range(0, units, 128):
+            left, right = pl.ds(at, 128), pl.ds(units + at, 128)
+            g, u, k = gu[r, left], gu[r, right], h[r, left]
+            sigma = 1.0 / (1.0 + jnp.exp(-g))
+            silu = g * sigma
+            hidden[r, left] = (silu * u).astype(BF)
+            both[r, left] = (k * u * sigma * (1.0 + g * (1.0 - sigma))).astype(BF)
+            both[r, right] = (k * silu).astype(BF)
+
+    each_rows(two.shape[0], gates, 32)
+
+    def tiled_out(left, right, out):
+        def body(i, carry):
             cols = pl.ds(pl.multiple_of(i * 256, 256), 256)
-            value = (dot_nt(dg, wgate[cols, :]) + dot_nt(du, wup[cols, :])).astype(BF)
-            for s in range(n_t):
-                npart[b, s, :, cols] = value[s * rows : (s + 1) * rows]
-            return inner
-
-        lax.fori_loop(0, two.shape[1] // 256, back, 0)
-        mine = Copies(sems)
-        reduce.pass_core(1, j, b, mine)
-        reduce.pass_core(0, j, b, mine)
-
-        @pl.when(j > 0)
-        def _():
-            reduce.cross(j - 1, far_first(chain, pc.z, j - 1), mine)
-
-        return carry
-
-    lax.fori_loop(0, chain, tile, 0)
-    reduce.cross(chain - 1, pc.z, Copies(sems))
-    steps = reduce.steps(True)
-    grads_into(two, dgate, ggate)
-    behind = Behind(
-        follow(
-            [
-                collect(pc, sems, ggate, s_gate, cgate),
-                collect(pc, sems, gup, s_up, cup),
-                collect(pc, sems, gdown, s_down, cdown),
-            ]
-        )
-    )
-    behind()
-    next(steps)
-    grads_into(two, dup, gup)
-    behind()
-    next(steps)
-    grads_into(cotan, hidden, gdown)
-    behind()
-    next(steps)
-
-    def out_tile(i, carry):
-        cols = pl.ds(pl.multiple_of(i * 256, 256), 256)
-        for b in range(chain):
-            value = dot_nt(hidden[b * local : (b + 1) * local, :], wdown[cols, :]).astype(BF)
-            for s in range(n_t):
-                opart[b, s, :, cols] = value[s * rows : (s + 1) * rows]
-        return carry
-
-    lax.fori_loop(0, two.shape[1] // 256, out_tile, 0)
-    behind.along(steps)
+            value = dot_nt(left[...], right[cols, :]).astype(BF)
+            out[:, :, :, cols] = value.reshape(chain, n_t, rows, 256)
+            return carry
+
+        lax.fori_loop(0, width // 256, body, 0)
+
+    tiled_out(both, wgu, npart)
+    steps = reduce.steps()
+    go(steps, 4)
+    gus = Collect(pc, sems, ggu, s_gu, cgu, False)
+    dns = Collect(pc, sems, gdn, s_dn, cdn, False)
+    grads_into(two, both, ggu)
+    gus.send(0, 1)
+    go(steps, 1)
+    grads_into(cotan, hidden, gdn)
+    go(steps, 1)
+    gus.turn(0, 1)
+    gus.send(2, 3)
+    go(steps, 1)
+    dns.send()
+    run(steps)
+    gus.turn(2, 3)
     gain_acc[...] = jnp.zeros_like(gain_acc)
 
     def back(r):
-        grad = norm_back(r, middle[r, :], ngrad[r, :], gains[1:2, :], cot[r, :].astype(F32), gain_acc)
+        grad = norm_back(r, middle[r, :], middle_grad[r, :], gains[1:2, :], cot[r, :].astype(F32), gain_acc)
         middle_grad[r, :] = grad
         branch[r, :] = grad.astype(BF)
 
     each_rows(rows, back)
-    behind.along(plane_gather(near, sems, branch, branch_all))
+    spreading = plane_gather(near, sems, branch, branch_all)
+    go(spreading, 2)
+    tiled_out(hidden, wdn, opart)
+    store = pltpu.make_async_copy(opart, opart_all, local_sem.at[0])
+    store.start()
+    run(spreading)
     gain_out[...] = jnp.broadcast_to(jnp.sum(gain_acc[...], axis=0, keepdims=True), gain_out.shape)
-    behind.drain()
-
-
-def attend_back(pc, query, dmix, mixed, lse, kk, vv, bias, dsum, dquery, step):
-    local, total = query.shape[0], kk.shape[0]
+    dns.turn()
+    gus.finish()
+    dns.finish()
+    store.wait()
+
+
+def attend_back(pc, query, query_t, dmix, mixed_t, lse, kv, kt, bias, dsum, put, step):
+    local, total = query.shape[0], kv.shape[0]
     size = gcd_of(total, 256)
-    tile = local // 2
-    left = lax.broadcasted_iota(jnp.int32, (tile, 128), 1) < 64
+    low, high = key_range(pc.d * local, local, total, size)
     even = jnp.where(halves(), 1.0, 0.0).astype(BF)
     odd = jnp.where(halves(), 0.0, 1.0).astype(BF)
-    for i in range(local // tile):
-        rows = slice(i * tile, (i + 1) * tile)
-        low, high = key_range(pc.d * local + i * tile, tile, total, size)
-        for chunk in range(query.shape[1] // 128):
-            lanes = slice(chunk * 128, (chunk + 1) * 128)
-            q, dm = query[rows, lanes], dmix[rows, lanes]
-            product = dm.astype(F32) * mixed[rows, lanes]
-            heads = []
-            for k, pick in enumerate((even, odd)):
-                mask = left if k == 0 else jnp.logical_not(left)
-                delta = jnp.sum(jnp.where(mask, product, 0.0), axis=1, keepdims=True)
-                heads.append((q * pick, dm * pick, lse[rows, 2 * chunk + k : 2 * chunk + k + 1], delta))
-
-            def body(j, carry):
-                cols = pl.ds(pl.multiple_of(j * size, size), size)
-                key, value, mask = kk[cols, :], vv[cols, :], bias[rows, cols].astype(F32)
-                out = []
-                dk = jnp.zeros((size, 128), F32)
-                dv = jnp.zeros((size, 128), F32)
-                for (qh, dh, top, delta), acc in zip(heads, carry):
-                    p = jnp.exp(dot_nt(qh, key) + mask - top)
-                    dp = dot_nt(dh, value)
-                    ds = (p * (dp - delta)).astype(BF)
-                    dk = dk + dot_tn(ds, qh)
-                    dv = dv + dot_tn(p.astype(BF), dh)
-                    out.append(acc + jnp.dot(ds, key, preferred_element_type=F32))
-                dsum[cols, :] += jnp.where(halves(), dk + pltpu.roll(dk, 64, 1), dv + pltpu.roll(dv, 64, 1))
-                return tuple(out)
-
-            zero = jnp.zeros((tile, 128), F32)
-            acc0, acc1 = lax.fori_loop(low, high, body, (zero, zero))
-            dquery[rows, lanes] = jnp.where(left, acc0, acc1)
-            step()
+    none = jnp.zeros((64, local), BF)
+    for chunk in range(query.shape[1] // 128):
+        first = chunk * 128
+        lanes = slice(first, first + 128)
+        q, dm = query[:, lanes], dmix[:, lanes]
+        turned = dm.astype(F32).T
+        product = turned * mixed_t[lanes, :]
+        turned = turned.astype(BF)
+        heads = []
+        for k, pick in enumerate((even, odd)):
+            at = slice(k * 64, k * 64 + 64)
+            heads.append(
+                (
+                    query_t[first + k * 64 : first + k * 64 + 64, :],
+                    jnp.concatenate([none, turned[at, :]], axis=0),
+                    q * pick,
+                    dm * pick,
+                    lse[2 * chunk + k : 2 * chunk + k + 1, :],
+                    jnp.sum(product[at, :], axis=0, keepdims=True),
+                )
+            )
+
+        def body(j, carry):
+            rows = pl.ds(pl.multiple_of(j * size, size), size)
+            both, key, key_t, mask = kv[rows, :], kv[rows, 0:64], kt[:, rows], bias[rows, :].astype(F32)
+            out = []
+            dk = jnp.zeros((size, 128), F32)
+            dv = jnp.zeros((size, 128), F32)
+            for (qt, dmt, qh, dh, top, delta), acc in zip(heads, carry):
+                p = jnp.exp(jnp.dot(key, qt, preferred_element_type=F32) + mask - top)
+                dp = jnp.dot(both, dmt, preferred_element_type=F32)
+                ds = (p * (dp - delta)).astype(BF)
+                dk = dk + jnp.dot(ds, qh, preferred_element_type=F32)
+                dv = dv + jnp.dot(p.astype(BF), dh, preferred_element_type=F32)
+                out.append(acc + jnp.dot(key_t, ds, preferred_element_type=F32))
+            dsum[rows, :] += jnp.where(halves(), dk + pltpu.roll(dk, 64, 1), dv + pltpu.roll(dv, 64, 1))
+            return tuple(out)
+
+        zero = jnp.zeros((64, local), F32)
+        done = lax.fori_loop(low, high, body, (zero, zero))
+        put(lanes, jnp.concatenate(done, axis=0).T)
+        step()
 
 
 def low_rows(full, low):
@@ -1110,13 +1126,14 @@
 
 
 def backward_kernel(chain, *refs):
-    (branch, wout, wqkv, normed, query, kk, vv, mixed, mixed_low, lse) = refs[:10]
+    (branch, wout, wqkv, normed, query, query_t, kv, mixed_t, mixed_low, lse) = refs[:10]
     (tok, middle_grad, gains, gain_two, middle, opart) = refs[10:16]
     (cosine, sine, qseg, qpos, kseg, kmark) = refs[16:22]
     (layer_out, input_grad, qkv_out, kv_out, wout_out, gain_out) = refs[22:28]
     rest = refs[28:]
-    (bias, dmix, dsum, dkv, dquery, dkv_own, dqkv, gwo, gq, gkv, part, osum, gain_acc) = rest[:13]
-    rest = rest[13:]
+    (kt, bias, dmix, dsum, dkv, dkv_own, dqkv, gwo, gkv, part, osum, gain_acc) = rest[:12]
+    gq = gwo
+    rest = rest[12:]
     s_out, s_near = rest[:5], rest[5:10]
     s_gwo, s_gq, s_gkv, s_keys = rest[10:13], rest[13:16], rest[16:19], rest[19:22]
     by_group, stage, mid, second, send, recv = rest[22:]
@@ -1136,21 +1153,33 @@
 
     whole = branch[...]
     grads_into(branch, mixed_low, gwo)
-    behind = Behind(rounds(dp_reduce(pc, sems, gwo, s_gwo, wout_out), finish()))
-    behind()
+    out_sum = Collect(pc, sems, gwo, s_gwo, wout_out, True)
+    out_sum.send()
+    laying = finish()
+    go(laying, 1)
     for at in range(0, wide, 256):
         dmix[:, at : at + 256] = jnp.dot(whole, wout[:, at : at + 256], preferred_element_type=F32).astype(BF)
-    size = gcd_of(kk.shape[0], 256)
-    low, high = key_range(pc.d * local, local, kk.shape[0], size)
+    turn_keys(kv, kt)
+    size = gcd_of(kv.shape[0], 256)
+    low, high = key_range(pc.d * local, local, kv.shape[0], size)
     fill_bias(bias, low, high, size, qseg, qpos, kseg, kmark)
     zero_rows(dsum)
-    attend_back(pc, query, dmix, mixed, lse, kk, vv, bias, dsum, dquery, behind)
+    stops = Points(
+        [lambda: go(laying, 3)],
+        [lambda: go(laying, 1)],
+        [out_sum.turn, lambda: go(laying, 1)],
+        [lambda: go(laying, 1)],
+    )
+
+    def put_query(lanes, value):
+        dqkv[:, lanes] = turn(value * 0.125, cosine[...], -sine[...]).astype(BF)
+
+    attend_back(pc, query, query_t, dmix, mixed_t, lse, kv, kt, bias, dsum, put_query, stops)
+    stops.drain()
     low_rows(dsum, dkv)
-    keys = dp_reduce(pc, sems, dkv, s_keys, dkv_own)
-    next(keys)
-    for at in range(0, wide, 128):
-        turned = turn(dquery[:, at : at + 128] * 0.125, cosine[...], -sine[...])
-        dqkv[:, at : at + 128] = turned.astype(BF)
+    keys = Collect(pc, sems, dkv, s_keys, dkv_own, True)
+    keys.send()
+    out_sum.finish()
     def query_grads(j, carry):
         at = pl.ds(pl.multiple_of(j * 256, 256), 256)
         left = jnp.concatenate([normed[0, s, :, at] for s in range(normed.shape[1])], axis=0)
@@ -1158,9 +1187,11 @@
         return carry
 
     lax.fori_loop(0, width // 256, query_grads, 0)
-    last = [dp_reduce(pc, sems, gq, s_gq, qkv_out), dp_reduce(pc, sems, gkv, s_gkv, kv_out)]
-    behind.along(keys)
-    next(last[0])
+    query_sum = Collect(pc, sems, gq, s_gq, qkv_out, True)
+    kv_sum = Collect(pc, sems, gkv, s_gkv, kv_out, True)
+    keys.turn()
+    query_sum.send()
+    keys.finish()
     pre = dkv_own[...]
     dqkv[:, wide : wide + 128] = jnp.where(halves(), turn(pre, cosine[...], -sine[...]), pre).astype(BF)
 
@@ -1187,7 +1218,7 @@
         yield from sum_gains(pc, sems, by_group, stage, mid, second, gain_out)
 
     end = ending()
-    next(end)
+    go(end, 1)
 
     def key_grads(j, carry):
         at = pl.ds(pl.multiple_of(j * 256, 256), 256)
@@ -1196,7 +1227,15 @@
         return carry
 
     lax.fori_loop(0, width // 256, key_grads, 0)
-    run(end, *last, behind.task)
+    kv_sum.send()
+    query_sum.turn(0, 1)
+    go(end, 5)
+    query_sum.turn(2, 3)
+    kv_sum.turn()
+    run(end)
+    run(laying)
+    query_sum.finish()
+    kv_sum.finish()
 
 
 def angles(positions, half_dim):
@@ -1247,8 +1286,11 @@
     wqkv = jnp.concatenate([w_query, w_key, w_value], axis=1)
     wout = w_out.T
 
+    held = (units + 127) // 128 * 128
+
     def by_chain(w):
-        return w.reshape(wrows, chain, units).transpose(1, 0, 2)
+        w = jnp.pad(w.reshape(wrows, chain, units), ((0, 0), (0, 0), (0, held - units)))
+        return w.transpose(1, 0, 2)
 
     plane = chain * n_t * rows
     nbytes = 60 << 20
@@ -1263,13 +1305,12 @@
         gains,
         wqkv,
         wout,
-        wgate,
-        wup,
-        wdown,
+        wgu,
+        wdn,
         cot,
         query,
-        kk,
-        vv,
+        query_t,
+        kv,
         mixed,
         mixed_low,
         lse,
@@ -1285,16 +1326,15 @@
             ((8, width), F32, VM),
             ((width, qkv), BF, VM),
             ((width, wide), BF, VM),
-            ((width, units), BF, ANY),
-            ((width, units), BF, ANY),
-            ((width, units), BF, ANY),
+            ((width, 2 * held), BF, ANY),
+            ((width, held), BF, ANY),
             ((chain, n_t, rows, width), BF, ANY),
             ((local, wide), BF, VM),
+            ((wide, local), BF, VM),
             ((total, 128), BF, VM),
-            ((total, 128), BF, VM),
-            ((local, wide), F32, VM),
+            ((wide, local), F32, VM),
             ((local, wide), BF, VM),
-            ((local, 128), F32, VM),
+            ((heads, local), F32, VM),
             ((rows, width), F32, VM),
             ((chain, n_t, rows, width), BF, ANY),
         ],
@@ -1302,8 +1342,8 @@
             pltpu.VMEM((n_dp, n_t, 8, 128), F32),
             pltpu.VMEM((rows, width), BF),
             pltpu.VMEM((local, 2 * dim), BF),
-            pltpu.VMEM((total, 128), BF),
-            pltpu.VMEM((local, total), BF),
+            pltpu.VMEM((80, total), BF),
+            pltpu.VMEM((total, local), BF),
             pltpu.VMEM((1, n_t, rows, width), BF),
             pltpu.VMEM((rows, width), F32),
             pltpu.VMEM((rows, width), BF),
@@ -1327,46 +1367,49 @@
         ),
         nbytes,
     )
-    cols_sums = [s for _ in range(3) for s in collect_scratch(chain, groups, wrows, units)]
-    block = ((chain, wrows, units), BF, ANY)
-    (opart, middle_grad, branch, gain_two, ggate, gup, gdown) = call(
+    (opart, middle_grad, branch, gain_two, ggu, gdn) = call(
         functools.partial(feed_kernel, chain),
         "feed",
         1,
-        [VM] * 8,
+        [ANY] * 4 + [VM] * 3,
         [
-            ((chain, n_t, rows, width), BF, VM),
+            ((chain, n_t, rows, width), BF, ANY),
             ((rows, width), F32, VM),
-            ((1, n_t, rows, width), BF, VM),
+            ((1, n_t, rows, width), BF, ANY),
             ((8, width), F32, VM),
-            block,
-            block,
-            block,
+            ((chain, wrows, 2 * held), BF, ANY),
+            ((chain, wrows, held), BF, ANY),
         ],
         [
+            pltpu.VMEM((plane, width), BF),
+            pltpu.VMEM((plane, width), BF),
+            pltpu.VMEM((width, 2 * held), BF),
+            pltpu.VMEM((width, held), BF),
             pltpu.VMEM((chain, n_t, rows, width), BF),
-            pltpu.VMEM((plane, units), BF),
-            pltpu.VMEM((plane, units), BF),
-            pltpu.VMEM((plane, units), BF),
-            pltpu.VMEM((width, units), BF),
-            pltpu.VMEM((width, units), BF),
-            pltpu.VMEM((width, units), BF),
+            pltpu.VMEM((plane, 2 * held), F32),
+            pltpu.VMEM((plane, held), F32),
+            pltpu.VMEM((plane, 2 * held), BF),
+            pltpu.VMEM((plane, held), BF),
+            pltpu.VMEM((chain, n_t, rows, width), BF),
+            pltpu.VMEM((width, 2 * held), BF),
+            pltpu.VMEM((width, held), BF),
         ]
         + plane_scratch(chain, rows, width)
-        + cols_sums
+        + collect_scratch(chain, groups, wrows, 2 * held)
+        + collect_scratch(chain, groups, wrows, held)
         + [
-            pltpu.VMEM((rows, width), F32),
             pltpu.VMEM((rows, width), BF),
             pltpu.VMEM((16, width), F32),
+            pltpu.SemaphoreType.DMA((4,)),
         ],
-        (two.reshape(plane, width), cot.reshape(plane, width), wgate, wup, wdown, middle, cotangent, gains),
+        (two.reshape(plane, width), cot.reshape(plane, width), wgu, wdn, middle, cotangent, gains),
         nbytes,
     )
 
     def shard_of(g):
-        return g.transpose(1, 0, 2).reshape(wrows, chain * units).astype(F32)
-
-    grad_gate, grad_up, grad_down = shard_of(ggate), shard_of(gup), shard_of(gdown).T
+        return g[:, :, :units].transpose(1, 0, 2).reshape(wrows, chain * units).astype(F32)
+
+    grad_gate, grad_up, grad_down = shard_of(ggu), shard_of(ggu[:, :, held:]), shard_of(gdn).T
 
     count = max(1, n_t * share // 128)
     layer_out, input_grad, gq, gkv, gwout, gain_sum = call(
@@ -1383,14 +1426,13 @@
             ((8, 128), F32, VM),
         ],
         [
-            pltpu.VMEM((local, total), BF),
+            pltpu.VMEM((64, total), BF),
+            pltpu.VMEM((total, local), BF),
             pltpu.VMEM((local, wide), BF),
             pltpu.VMEM((total, 128), F32),
             pltpu.VMEM((total, 128), BF),
-            pltpu.VMEM((local, wide), F32),
             pltpu.VMEM((local, 128), F32),
             pltpu.VMEM((local, qkv), BF),
-            pltpu.VMEM((width, wide), BF),
             pltpu.VMEM((width, wide), BF),
             pltpu.VMEM((width, 128), BF),
             pltpu.VMEM((1, n_t, rows, width), BF),
@@ -1415,8 +1457,8 @@
             wqkv,
             normed,
             query,
-            kk,
-            vv,
+            query_t,
+            kv,
             mixed,
             mixed_low,
             lse,

time: 469 us -> 431 us (0.919)
  Pallas kernels: 436 us -> 395 us
    pallas_call x3, Pallas kernels: 436 us -> 395 us  [call(): pl.pallas_call(kernel, out_shape=[jax.ShapeDtypeStruct(shape, kind) for s...]
where the time goes in v4:
time: 431 us
  Pallas kernels  395 us (92%)
  local copies, waits for them, and re-layouts  30.6 us (7%)
    pallas_call x3, Pallas kernels, call(): pl.pallas_call(kernel, out_shape=[jax.ShapeDtypeStruct(shape, kind) for s...  395 us
    unnamed x31, local copies, waits for them, and re-layouts  13.9 us

profile of v4, /device:TPU:0, one launch (start us, length us, event | category | flops | bytes accessed | tf_op | source)
XLA Modules:
  0.0 430.6 jit_solution(11158445974965443632)
XLA Ops:
  0.7 0.1 pad.20.clone
  0.8 0.7 tile.12
  1.4 0.1 broadcast_in_dim_tile.6
  1.5 0.7 tile.13
  2.2 0.1 broadcast_in_dim_tile.7
  2.3 0.8 dynamic_slice.6
  3.0 0.7 maximum_maximum_fusion.refs_1_
  3.7 1.3 broadcast_in_dim.22.refs_13_.refs_21_
  5.0 1.3 broadcast_in_dim.10.refs_12_.refs_20_
  6.3 0.9 copy.30
  7.2 0.9 copy.31
  8.1 0.0 copy-start.1
  8.1 0.3 fusion
  8.4 0.8 copy.39.refs_9_.refs_17_
  9.2 0.8 broadcast_in_dim.23.refs_10_.refs_18_
  9.9 0.7 iota_add_fusion.refs_11_.refs_19_
  10.7 0.8 copy.38.refs_8_.refs_16_
  11.4 0.0 copy-done.8
  11.4 0.8 pad_maximum_fusion.refs_2_
  12.3 0.8 copy.32
  13.1 0.3 copy.33
  13.4 0.0 copy-start.2
  13.4 0.4 copy.34
  13.8 1.0 pad_bitcast_fusion.2.refs_4_
  14.7 0.3 copy.35
  15.0 0.4 copy.36
  15.4 0.5 copy-done.3
  15.8 0.4 copy.37
  16.2 1.4 pad_bitcast_fusion
  17.6 155.8 %forward.1 = (bf16[1,4,80,2048]{3,2,1,0:T(8,128)(2,1)}, f32[8,2048]{1,0:T(8,128)}, bf16[2048,640]{1,0:T(8,128)(2,1)}, bf16[2048,512]{1,0:T(8,128)(2,1)}, bf16[20...) custom-call(bf16[80,2048]{1,0:T(8,128)(2,1)} %refs_10_.1, ...), custom_call_target="tpu_custom_call" | custom-call | bytes 62914560 | tf_op jit(solution)/shard_map/forward/pallas_call | solution.py:696
  173.4 115.4 %feed.1 = (bf16[4,4,80,2048]{3,2,1,0:T(8,128)(2,1)}, f32[80,2048]{1,0:T(8,128)}, bf16[1,4,80,2048]{3,2,1,0:T(8,128)(2,1)}, f32[8,2048]{1,0:T(8,128)}, bf16[4,256...) custom-call(bf16[1280,2048]{1,0:T(8,128)(2,1)} %bitcast.36, bf16[1280,2048]{1,0:T(8,128)(2,1)} %bitcast.35, ...), custom_call_target="tpu_custom_call" | custom-call | bytes 62914560 | tf_op jit(solution)/shard_map/feed/pallas_call | solution.py:696
  288.8 123.8 %backward.1 = (bf16[80,2048]{1,0:T(8,128)(2,1)}, f32[80,2048]{1,0:T(8,128)}, f32[256,512]{1,0:T(8,128)}, f32[256,128]{1,0:T(8,128)}, f32[256,512]{1,0:T(8,128)}, /*index=5*/f32[8,128]{1,0:T(8,128)}) custom-call(bf16[320,2048]{1,0:T(8,128)(2,1)} %bitcast.40, bf16[2048,512]{1,0:T(8,128)(2,1)} %get-tuple-element.45.refs_1_, ...), custom_call_target="tpu_custom_call" | custom-call | bytes 62914560 | tf_op jit(solution)/shard_map/backward/pallas_call | solution.py:696
  412.6 0.8 constant_dynamic-slice_fusion
  413.4 0.5 slice_bitcast_fusion
  413.9 1.1 fusion.1
  415.0 0.7 copy.48
  415.7 0.7 copy.47
  416.4 2.0 copy.49
  418.5 0.1 convert_bitcast_fusion
  418.6 1.6 copy.46
  420.1 1.6 convert_bitcast_fusion.1
  421.7 1.6 copy.45
  423.3 2.9 copy.51
  426.2 0.5 copy.44
  426.7 1.5 copy.50
  428.2 0.7 copy.55
  428.9 0.8 copy.56
  429.8 0.8 copy.57
  (20 shorter events, 0.1 us)
Async XLA Ops:
  0.6 11.6 %copy-start.7 = (bf16[512,256]{1,0:T(8,128)(2,1)S(1)}, bf16[512,256]{1,0:T(8,128)(2,1)}, u32[]{:S(2)}) copy-start(bf16[512,256]{1,0:T(8,128)(2,1)} %param.20) | copy-start | bytes 786436
  0.7 10.8 %copy-start.8 = (bf16[256,512]{1,0:T(8,128)(2,1)S(1)}, bf16[256,512]{1,0:T(8,128)(2,1)}, u32[]{:S(2)}) copy-start(bf16[256,512]{1,0:T(8,128)(2,1)} %param.17) | copy-start | bytes 786436
  8.1 5.0 %copy-start.1 = (bf16[256,1408]{1,0:T(8,128)(2,1)S(1)}, bf16[256,1408]{1,0:T(8,128)(2,1)}, u32[]{:S(2)}) copy-start(bf16[256,1408]{1,0:T(8,128)(2,1)} %param.22) | copy-start | bytes 2162692
  13.4 1.3 copy-start.2
  14.7 1.1 copy-start.3
  412.6 5.9 %copy-start = (bf16[4,256,384]{2,1,0:T(8,128)(2,1)S(1)}, bf16[4,256,384]{2,1,0:T(8,128)(2,1)}, u32[]{:S(2)}) copy-start(bf16[4,256,384]{2,1,0:T(8,128)(2,1)} %get-tuple-element.64) | copy-start | bytes 2359300
  426.6 1.6 copy-start.6
  426.7 2.3 copy-start.4
  428.2 1.6 copy-start.5

commit v5 on v4

--- a/solution.py
+++ b/solution.py
@@ -303,8 +303,8 @@
 
 
 class PlaneReduce:
-    def __init__(self, pc, sems, part, scratch, out):
-        self.pc, self.part, self.out = pc, part, out
+    def __init__(self, pc, sems, part, scratch, out, held=None):
+        self.pc, self.part, self.out, self.held = pc, part, out, held
         self.crecv, self.csum, self.yrecv, self.zsend, self.came = scratch
         self.cp = Copies(sems)
         self.base = sems.take(5 * pc.chain)
@@ -326,42 +326,37 @@
         )
 
     def cross(self, j, b, cp=None):
-        pc, part, crecv, csum = self.pc, self.part, self.crecv, self.csum
+        pc, crecv, csum = self.pc, self.crecv, self.csum
         cp = cp or self.cp
         cp.arrive(self.sem(1, j), crecv.at[b, 1], pc.at())
 
         def add(r):
-            csum[b, r, :] = (part[b, pc.sy, r, :].astype(F32) + crecv[b, 1, r, :].astype(F32)).astype(BF)
+            csum[b, r, :] = (self.own(0, b, r).astype(F32) + crecv[b, 1, r, :].astype(F32)).astype(BF)
 
         each_rows(self.rows, add)
         cp.go(self.sem(2, j), csum.at[b], self.yrecv.at[b], pc.at(s=pc.sy))
 
-    def started(self):
-        for j in range(self.pc.chain):
-            b = self.block(j)
-            for kind, src in ((1, self.part.at[b, 0]), (0, self.part.at[b, 0]), (2, self.csum.at[b])):
-                self.cp.sent.append((self.cp.describe(self.sem(kind, j), src), None))
-
-    def steps(self, crossed=False):
+    def own(self, here, b, r):
+        if self.held is not None:
+            return self.held[here, b, r, :]
+        return self.part[b, self.pc.s if here else self.pc.sy, r, :]
+
+    def steps(self):
         pc = self.pc
         chain, z = pc.chain, pc.z
-        part, crecv, yrecv, out = self.part, self.crecv, self.yrecv, self.out
+        crecv, yrecv, out = self.crecv, self.yrecv, self.out
         cp = self.cp
         todo = [(j, self.block(j)) for j in range(chain)]
-        ahead = []
-        if crossed:
-            self.started()
-        else:
-            for j, b in todo:
-                self.pass_core(1, j, b)
+        for j, b in todo:
+            self.pass_core(1, j, b)
+        yield
+        ahead = list(todo)
+        for _ in range(min(2, chain)):
+            self.cross(*ahead.pop(0))
             yield
-            ahead = list(todo)
-            for _ in range(min(2, chain)):
-                self.cross(*ahead.pop(0))
-                yield
-            for j, b in todo:
-                self.pass_core(0, j, b)
-            yield
+        for j, b in todo:
+            self.pass_core(0, j, b)
+        yield
         for j, b in todo:
             cp.arrive(self.sem(0, j), crecv.at[b, 0], pc.at())
             cp.arrive(self.sem(2, j), yrecv.at[b], pc.at())
@@ -370,7 +365,7 @@
 
             def value(r):
                 return (
-                    part[b, pc.s, r, :].astype(F32)
+                    self.own(1, b, r).astype(F32)
                     + crecv[b, 0, r, :].astype(F32)
                     + yrecv[b, r, :].astype(F32)
                 )
@@ -557,6 +552,17 @@
     ]
 
 
+class Moves:
+    def __init__(self, sem):
+        self.sem, self.count = sem, 0
+
+    def start(self, src, dst):
+        copy = pltpu.make_async_copy(src, dst, self.sem.at[self.count])
+        self.count += 1
+        copy.start()
+        return copy
+
+
 class Collect:
     def __init__(self, pc, sems, part, scratch, out, summed):
         self.pc, self.out, self.summed = pc, out, summed
@@ -738,16 +744,14 @@
     return low // size, (first + count + size - 1) // size
 
 
-def fill_bias(bias, low, high, size, qseg, qpos, kseg, kmark):
+def fill_bias(bias, first, low, high, size, qinfo, kinfo):
+    qpos = first + lax.broadcasted_iota(jnp.int32, qinfo.shape, 0)
+
     def fill(j, carry):
         at = pl.multiple_of(j * size, size)
         cols = pl.ds(at, size)
         kpos = at + lax.broadcasted_iota(jnp.int32, (1, size), 1)
-        allowed = (
-            (kseg[:, cols] == qseg[...])
-            & (kpos <= qpos[...])
-            & ((kmark[:, cols] == 1) | (kpos == qpos[...]))
-        )
+        allowed = (kpos == qpos) | ((kinfo[:, cols] == qinfo[...]) & (kpos < qpos))
         bias[cols, :] = jnp.where(allowed, 0.0, NEG).T.astype(BF)
         return carry
 
@@ -779,7 +783,7 @@
 
 def attend(pc, query_t, kv, vt, bias, mixed_t, mixed_low, lse, step):
     local, total = query_t.shape[1], kv.shape[0]
-    size = gcd_of(total, 256)
+    size = gcd_of(total, 640)
     low, high = key_range(pc.d * local, local, total, size)
     for chunk in range(query_t.shape[0] // 128):
         first = chunk * 128
@@ -825,27 +829,27 @@
 
 
 def forward_kernel(chain, *refs):
-    (tok, own_gain, wqkv, wout, wgate, wup, wdown, cot, cosine, sine, qseg, qpos, kseg, kmark) = refs[:14]
+    (tok, own_gain, wqkv, wout, wgate, wup, wdown, cot, cosine, sine, qinfo, kinfo) = refs[:12]
     (
-        normed_all,
         gains,
-        wqkv_all,
-        wout_all,
         wgu_all,
         wdown_all,
         cot_all,
-        query,
-        query_t,
-        kv_all,
-        mixed_t,
-        mixed_low,
         lse,
         middle,
         two_all,
-    ) = refs[14:29]
-    rest = refs[29:]
-    table, normed, own_kv, vt, bias, part, total, two = rest[:8]
-    scratch, (send, recv) = rest[8:13], rest[13:]
+    ) = refs[12:19]
+    kept, rest = refs[19:29], refs[29:]
+    (normed_all, wqkv_all, wout_all, query, query_t, kv_all, kt, bias, mixed_t, mixed_low) = rest[:10]
+    table, normed, own_kv, vt, part, total, two, local_sem = rest[10:18]
+    scratch, (send, recv) = rest[18:23], rest[23:]
+    moves = Moves(local_sem)
+    stores = []
+
+    def keep(*names):
+        for i in names:
+            stores.append(moves.start(rest[i], kept[i]))
+
     sems = Sems(send, recv)
     pc, near = Place(chain), Place(1)
     rows, width = tok.shape
@@ -901,19 +905,16 @@
     own_kv[...] = jnp.where(halves(), turn(pre, cosine[...], sine[...]), pre).astype(BF)
     go(outw, 2)
     run(dp_gather(pc, sems, own_kv, rows_of(kv_all, local)))
+    keep(0, 1, 3, 4, 5)
     go(gatew, 2)
     go(outw, 3)
     go(cots, 2)
     turn_values(kv_all, vt)
+    size = gcd_of(kv_all.shape[0], 640)
     low, high = key_range(pc.d * local, local, kv_all.shape[0], size)
-    fill_bias(bias, low, high, size, qseg, qpos, kseg, kmark)
+    fill_bias(bias, pc.d * local, low, high, size, qinfo, kinfo)
     go(upw, 2)
-    stops = Points(
-        [lambda: go(cots, 2)],
-        [lambda: go(downw, 2)],
-        [lambda: go(gatew, 3)],
-        [lambda: run(outw)],
-    )
+    stops = Points([], [lambda: go(cots, 2)], [lambda: go(downw, 2)], [lambda: run(outw)])
     attend(pc, query_t, kv_all, vt, bias, mixed_t, mixed_low, lse, stops)
     stops.drain()
 
@@ -923,8 +924,13 @@
             part[0, s, :, cols] = value[s * rows : (s + 1) * rows].astype(BF)
 
     tiled_nt(mixed_low[...], wout_all, put)
-    run(plane_reduce(near, sems, part, scratch, total))
-    go(upw, 3)
+    totals = plane_reduce(near, sems, part, scratch, total)
+    go(totals, 1)
+    keep(2, 7, 8, 9)
+    go(gatew, 3)
+    turn_keys(kv_all, kt)
+    keep(6)
+    run(totals)
 
     def norm(r):
         v = tok[r, :].astype(F32) + total[r, :]
@@ -933,12 +939,16 @@
 
     each_rows(rows, norm)
     twos = plane_gather(pc, sems, two, two_all, 2)
+    go(twos, 2)
+    go(upw, 3)
     go(twos, 2)
     go(cots, 3)
     go(twos, 2)
     go(downw, 3)
     run(twos)
     run(cots, gatew, upw, downw)
+    for store in stores:
+        store.wait()
 
 
 def dot_nt(a, b):
@@ -1054,7 +1064,7 @@
 
 def attend_back(pc, query, query_t, dmix, mixed_t, lse, kv, kt, bias, dsum, put, step):
     local, total = query.shape[0], kv.shape[0]
-    size = gcd_of(total, 256)
+    size = gcd_of(total, 640)
     low, high = key_range(pc.d * local, local, total, size)
     even = jnp.where(halves(), 1.0, 0.0).astype(BF)
     odd = jnp.where(halves(), 0.0, 1.0).astype(BF)
@@ -1126,14 +1136,15 @@
 
 
 def backward_kernel(chain, *refs):
-    (branch, wout, wqkv, normed, query, query_t, kv, mixed_t, mixed_low, lse) = refs[:10]
-    (tok, middle_grad, gains, gain_two, middle, opart) = refs[10:16]
-    (cosine, sine, qseg, qpos, kseg, kmark) = refs[16:22]
-    (layer_out, input_grad, qkv_out, kv_out, wout_out, gain_out) = refs[22:28]
-    rest = refs[28:]
-    (kt, bias, dmix, dsum, dkv, dkv_own, dqkv, gwo, gkv, part, osum, gain_acc) = rest[:12]
+    kept, branch_all, opart = refs[:10], refs[10], refs[11]
+    (lse, tok, middle_grad, gains, gain_two, middle, cosine, sine) = refs[12:20]
+    (layer_out, input_grad, qkv_out, kv_out, wout_out, gain_out) = refs[20:26]
+    rest = refs[26:]
+    (normed, wqkv, wout, query, query_t, kv, kt, bias, mixed_t, mixed_low) = rest[:10]
+    (branch_in, held, local_sem) = rest[10:13]
+    (dmix, dsum, dkv, dkv_own, dqkv, gwo, gkv, part, osum, gain_acc) = rest[13:23]
     gq = gwo
-    rest = rest[12:]
+    rest = rest[23:]
     s_out, s_near = rest[:5], rest[5:10]
     s_gwo, s_gq, s_gkv, s_keys = rest[10:13], rest[13:16], rest[16:19], rest[19:22]
     by_group, stage, mid, second, send, recv = rest[22:]
@@ -1141,29 +1152,44 @@
     pc, near = Place(chain), Place(1)
     rows, width = tok.shape
     local, wide = query.shape
+    moves = Moves(local_sem)
+    inner = (normed, wqkv, wout, query, query_t, kv, kt, bias, mixed_t, mixed_low)
+    fetches = {}
+    fetches[10] = moves.start(branch_all, branch_in)
+    for i in (9, 2):
+        fetches[i] = moves.start(kept[i], inner[i])
+    halves_of = [
+        moves.start(opart.at[:, col], held.at[i]) for i, col in enumerate((pc.sy, pc.s))
+    ]
+    for i in (7, 5, 6, 3, 4, 8, 0, 1):
+        fetches[i] = moves.start(kept[i], inner[i])
     greet(pc)
 
     def finish():
-        yield from plane_reduce(pc, sems, opart, s_out, osum)
+        yield from PlaneReduce(pc, sems, opart, s_out, osum, held).steps()
 
         def add(r):
             layer_out[r, :] = (middle[r, :] + osum[r, :]).astype(BF)
 
         each_rows(rows, add)
 
+    fetches[10].wait()
+    fetches[9].wait()
+    branch = branch_in
     whole = branch[...]
     grads_into(branch, mixed_low, gwo)
     out_sum = Collect(pc, sems, gwo, s_gwo, wout_out, True)
     out_sum.send()
     laying = finish()
     go(laying, 1)
+    for fetch in halves_of:
+        fetch.wait()
+    fetches[2].wait()
     for at in range(0, wide, 256):
         dmix[:, at : at + 256] = jnp.dot(whole, wout[:, at : at + 256], preferred_element_type=F32).astype(BF)
-    turn_keys(kv, kt)
-    size = gcd_of(kv.shape[0], 256)
-    low, high = key_range(pc.d * local, local, kv.shape[0], size)
-    fill_bias(bias, low, high, size, qseg, qpos, kseg, kmark)
     zero_rows(dsum)
+    for i in (7, 5, 6, 3, 4, 8):
+        fetches[i].wait()
     stops = Points(
         [lambda: go(laying, 3)],
         [lambda: go(laying, 1)],
@@ -1180,6 +1206,9 @@
     keys = Collect(pc, sems, dkv, s_keys, dkv_own, True)
     keys.send()
     out_sum.finish()
+    fetches[0].wait()
+    fetches[1].wait()
+
     def query_grads(j, carry):
         at = pl.ds(pl.multiple_of(j * 256, 256), 256)
         left = jnp.concatenate([normed[0, s, :, at] for s in range(normed.shape[1])], axis=0)
@@ -1236,12 +1265,6 @@
     run(laying)
     query_sum.finish()
     kv_sum.finish()
-
-
-def angles(positions, half_dim):
-    frequency = THETA ** (-jnp.arange(half_dim, dtype=F32) / half_dim)
-    turned = positions.astype(F32)[:, None] * frequency[None, :]
-    return jnp.cos(turned), jnp.sin(turned)
 
 
 def shards(
@@ -1295,58 +1318,50 @@
     plane = chain * n_t * rows
     nbytes = 60 << 20
     positions = first_row + jnp.arange(local, dtype=jnp.int32)
-    cosine, sine = angles(positions, dim // 2)
-    cosine = jnp.tile(cosine, (1, 4))
-    sine = jnp.tile(jnp.concatenate([-sine, sine], axis=1), (1, 2))
+    lane = jnp.arange(128, dtype=jnp.int32)
+    frequency = THETA ** (-(lane % (dim // 2)).astype(F32) / (dim // 2))
+    turned = positions.astype(F32)[:, None] * frequency[None, :]
+    cosine = jnp.cos(turned)
+    sine = jnp.sin(turned) * jnp.where(lane % dim < dim // 2, -1.0, 1.0)
     own_segments = lax.dynamic_slice(segment_ids, (first_row,), (local,))
     wide = heads * dim
-    (
-        normed,
-        gains,
-        wqkv,
-        wout,
-        wgu,
-        wdn,
-        cot,
-        query,
-        query_t,
-        kv,
-        mixed,
-        mixed_low,
-        lse,
-        middle,
-        two,
-    ) = call(
+    saved = [
+        ((1, n_t, rows, width), BF),
+        ((width, qkv), BF),
+        ((width, wide), BF),
+        ((local, wide), BF),
+        ((wide, local), BF),
+        ((total, 128), BF),
+        ((64, total), BF),
+        ((total, local), BF),
+        ((wide, local), F32),
+        ((local, wide), BF),
+    ]
+    (gains, wgu, wdn, cot, lse, middle, two, *kept) = call(
         functools.partial(forward_kernel, chain),
         "forward",
         0,
-        [VM, VM] + [ANY] * 6 + [VM] * 6,
+        [VM, VM] + [ANY] * 6 + [VM] * 4,
         [
-            ((1, n_t, rows, width), BF, VM),
             ((8, width), F32, VM),
-            ((width, qkv), BF, VM),
-            ((width, wide), BF, VM),
             ((width, 2 * held), BF, ANY),
             ((width, held), BF, ANY),
             ((chain, n_t, rows, width), BF, ANY),
-            ((local, wide), BF, VM),
-            ((wide, local), BF, VM),
-            ((total, 128), BF, VM),
-            ((wide, local), F32, VM),
-            ((local, wide), BF, VM),
             ((heads, local), F32, VM),
             ((rows, width), F32, VM),
             ((chain, n_t, rows, width), BF, ANY),
-        ],
-        [
+        ]
+        + [(shape, kind, ANY) for shape, kind in saved],
+        [pltpu.VMEM(shape, kind) for shape, kind in saved]
+        + [
             pltpu.VMEM((n_dp, n_t, 8, 128), F32),
             pltpu.VMEM((rows, width), BF),
             pltpu.VMEM((local, 2 * dim), BF),
             pltpu.VMEM((80, total), BF),
-            pltpu.VMEM((total, local), BF),
             pltpu.VMEM((1, n_t, rows, width), BF),
             pltpu.VMEM((rows, width), F32),
             pltpu.VMEM((rows, width), BF),
+            pltpu.SemaphoreType.DMA((10,)),
         ]
         + plane_scratch(1, rows, width),
         (
@@ -1360,10 +1375,8 @@
             cotangent,
             cosine,
             sine,
-            own_segments[:, None],
-            positions[:, None],
-            segment_ids[None],
-            key_mask[None],
+            own_segments[:, None] * 2 + 1,
+            (segment_ids * 2 + key_mask)[None],
         ),
         nbytes,
     )
@@ -1407,7 +1420,7 @@
     )
 
     def shard_of(g):
-        return g[:, :, :units].transpose(1, 0, 2).reshape(wrows, chain * units).astype(F32)
+        return jnp.concatenate([g[z, :, :units].astype(F32) for z in range(chain)], axis=1)
 
     grad_gate, grad_up, grad_down = shard_of(ggu), shard_of(ggu[:, :, held:]), shard_of(gdn).T
 
@@ -1416,7 +1429,7 @@
         functools.partial(backward_kernel, chain),
         "backward",
         2,
-        [VM] * 22,
+        [ANY] * 12 + [VM] * 8,
         [
             ((rows, width), BF, VM),
             ((rows, width), F32, VM),
@@ -1425,9 +1438,11 @@
             ((wrows, wide), F32, VM),
             ((8, 128), F32, VM),
         ],
-        [
-            pltpu.VMEM((64, total), BF),
-            pltpu.VMEM((total, local), BF),
+        [pltpu.VMEM(shape, kind) for shape, kind in saved]
+        + [
+            pltpu.VMEM((local, width), BF),
+            pltpu.VMEM((2, chain, rows, width), BF),
+            pltpu.SemaphoreType.DMA((13,)),
             pltpu.VMEM((local, wide), BF),
             pltpu.VMEM((total, 128), F32),
             pltpu.VMEM((total, 128), BF),
@@ -1452,28 +1467,17 @@
             pltpu.VMEM((n_t, 8, 128), F32),
         ],
         (
+            *kept,
             branch.reshape(local, width),
-            wout,
-            wqkv,
-            normed,
-            query,
-            query_t,
-            kv,
-            mixed,
-            mixed_low,
+            opart,
             lse,
             tokens,
             middle_grad,
             gains,
             gain_two,
             middle,
-            opart,
             cosine,
             sine,
-            own_segments[:, None],
-            positions[:, None],
-            segment_ids[None],
-            key_mask[None],
         ),
         nbytes,
     )

time: 431 us -> 431 us (level); the launches traced: 431 us -> 424 us
  local copies, waits for them, and re-layouts: 30.6 us -> 24.5 us
  Pallas kernels: 395 us -> 390 us
    pallas_call x3, Pallas kernels: 395 us -> 390 us  [call(): pl.pallas_call(kernel, out_shape=[jax.ShapeDtypeStruct(shape, kind) for s...]
    unnamed x31 -> x28, local copies, waits for them, and re-layouts: 13.9 us -> 12 us
where the time goes in v5:
time: 431 us; the launch traced here: 424 us
  Pallas kernels  390 us (90%)
  local copies, waits for them, and re-layouts  24.5 us (6%)
  other arithmetic  7.8 us (2%)
    pallas_call x3, Pallas kernels, call(): pl.pallas_call(kernel, out_shape=[jax.ShapeDtypeStruct(shape, kind) for s...  390 us
    unnamed x28, local copies, waits for them, and re-layouts  12 us

profile of v5, /device:TPU:0, one launch (start us, length us, event | category | flops | bytes accessed | tf_op | source)
XLA Modules:
  0.0 423.7 jit_solution(2987090559737663489)
XLA Ops:
  0.7 0.1 pad.18.clone
  0.8 0.7 tile.4
  1.5 0.1 broadcast_in_dim_tile.6
  1.6 0.7 tile.5
  2.2 0.1 broadcast_in_dim_tile.7
  2.3 0.8 multiply_add_fusion.1
  3.1 0.7 maximum_maximum_fusion.refs_1_
  3.8 0.7 multiply_add_fusion
  4.5 0.6 broadcast_in_dim.21.refs_11_
  5.1 0.9 copy.31
  6.0 0.9 copy.32
  6.8 0.8 add.70.refs_10_
  7.6 1.8 pad_maximum_fusion.refs_2_
  9.4 1.8 copy.33
  11.2 1.4 fusion
  12.6 0.3 copy.34
  12.8 0.0 copy-start.3
  12.9 0.4 copy.35
  13.2 1.0 pad_bitcast_fusion.2.refs_4_
  14.2 0.0 copy-done.3
  14.2 0.3 copy.36
  14.5 0.4 copy.37
  14.8 0.5 copy-done.4
  15.3 0.4 copy.38
  15.7 1.4 pad_bitcast_fusion
  17.0 153.3 %forward.1 = (f32[8,2048]{1,0:T(8,128)}, bf16[2048,768]{1,0:T(8,128)(2,1)}, bf16[2048,384]{1,0:T(8,128)(2,1)}, bf16[4,4,80,2048]{3,2,1,0:T(8,128)(2,1)}, f32[8,3...) custom-call(bf16[80,2048]{1,0:T(8,128)(2,1)} %refs_13_.1, ...), custom_call_target="tpu_custom_call" | custom-call | bytes 62914560 | tf_op jit(solution)/shard_map/forward/pallas_call | solution.py:702
  170.3 122.1 %feed.1 = (bf16[4,4,80,2048]{3,2,1,0:T(8,128)(2,1)}, f32[80,2048]{1,0:T(8,128)}, bf16[1,4,80,2048]{3,2,1,0:T(8,128)(2,1)}, f32[8,2048]{1,0:T(8,128)}, bf16[4,256...) custom-call(bf16[1280,2048]{1,0:T(8,128)(2,1)} %bitcast.47, bf16[1280,2048]{1,0:T(8,128)(2,1)} %bitcast.46, ...), custom_call_target="tpu_custom_call" | custom-call | bytes 62914560 | tf_op jit(solution)/shard_map/feed/pallas_call | solution.py:702
  292.4 114.7 %backward.1 = (bf16[80,2048]{1,0:T(8,128)(2,1)}, f32[80,2048]{1,0:T(8,128)}, f32[256,512]{1,0:T(8,128)}, f32[256,128]{1,0:T(8,128)}, f32[256,512]{1,0:T(8,128)}, /*index=5*/f32[8,128]{1,0:T(8,128)}) custom-call(bf16[1,4,80,2048]{3,2,1,0:T(8,128)(2,1)} %get-tuple-element.40.refs_0_, bf16[2048,640]{1,0:T(8,128)(2,1)} %get-tuple-element.41.refs_1_, ...), custom_call_target="tpu_custom_call" | custom-call | bytes 62914560 | tf_op jit(solution)/shard_map/backward/pallas_call | solution.py:702
  407.1 0.8 constant_dynamic-slice_fusion
  408.0 0.5 slice_bitcast_fusion.12
  408.5 1.1 fusion.5
  409.6 0.7 copy.41
  410.3 0.7 copy.40
  411.0 2.0 copy.42
  413.0 0.1 slice_bitcast_fusion
  413.1 0.6 concatenate.28
  413.7 0.1 convert_bitcast_fusion
  413.9 0.0 copy-start
  413.9 1.5 copy.43
  415.4 0.0 copy-done
  415.4 0.9 slice_bitcast_fusion.4
  416.3 1.5 concatenate.26
  417.8 1.2 concatenate.27
  419.0 0.6 concatenate.24
  419.7 1.2 concatenate.25
  420.9 0.7 copy.47
  421.6 0.8 copy.48
  422.4 0.8 copy.49
  (14 shorter events, 0.0 us)
Async XLA Ops:
  0.6 11.9 %copy-start.2 = (bf16[256,1408]{1,0:T(8,128)(2,1)S(1)}, bf16[256,1408]{1,0:T(8,128)(2,1)}, u32[]{:S(2)}) copy-start(bf16[256,1408]{1,0:T(8,128)(2,1)} %param.22) | copy-start | bytes 2162692
  12.8 1.3 copy-start.3
  14.2 1.1 copy-start.4
  407.1 5.9 %copy-start.1 = (bf16[4,256,384]{2,1,0:T(8,128)(2,1)S(1)}, bf16[4,256,384]{2,1,0:T(8,128)(2,1)}, u32[]{:S(2)}) copy-start(bf16[4,256,384]{2,1,0:T(8,128)(2,1)} %get-tuple-element.68) | copy-start | bytes 2359300
  413.9 1.6 copy-start
  419.0 1.8 copy-start.7
  419.6 1.9 copy-start.5
  419.7 2.8 copy-start.6

commit v6 on v5

--- a/solution.py
+++ b/solution.py
@@ -785,9 +785,10 @@
     local, total = query_t.shape[1], kv.shape[0]
     size = gcd_of(total, 640)
     low, high = key_range(pc.d * local, local, total, size)
-    for chunk in range(query_t.shape[0] // 128):
-        first = chunk * 128
-        queries = (query_t[first : first + 64, :], query_t[first + 64 : first + 128, :])
+
+    def one(chunk, carry):
+        first = pl.multiple_of(chunk * 128, 128)
+        queries = tuple(query_t[pl.ds(pl.multiple_of(first + k * 64, 64), 64), :] for k in range(2))
 
         def body(j, carry):
             rows = pl.ds(pl.multiple_of(j * size, size), size)
@@ -807,10 +808,15 @@
         for k, (top, acc) in enumerate(done):
             tot = acc[64:65, :]
             pair.append(acc[0:64, :] / tot)
-            lse[2 * chunk + k : 2 * chunk + k + 1, :] = top + jnp.log(tot)
+            lse[pl.ds(2 * chunk + k, 1), :] = top + jnp.log(tot)
         both = jnp.concatenate(pair, axis=0)
-        mixed_t[first : first + 128, :] = both
-        mixed_low[:, first : first + 128] = both.T.astype(BF)
+        mixed_t[pl.ds(first, 128), :] = both
+        mixed_low[:, pl.ds(first, 128)] = both.T.astype(BF)
+        return carry
+
+    chunks = query_t.shape[0] // 128
+    for half in range(2):
+        lax.fori_loop(half * chunks // 2, (half + 1) * chunks // 2, one, 0)
         step()
 
 
@@ -914,7 +920,7 @@
     low, high = key_range(pc.d * local, local, kv_all.shape[0], size)
     fill_bias(bias, pc.d * local, low, high, size, qinfo, kinfo)
     go(upw, 2)
-    stops = Points([], [lambda: go(cots, 2)], [lambda: go(downw, 2)], [lambda: run(outw)])
+    stops = Points([lambda: go(cots, 2), lambda: go(downw, 2)], [lambda: run(outw)])
     attend(pc, query_t, kv_all, vt, bias, mixed_t, mixed_low, lse, stops)
     stops.drain()
 
@@ -974,6 +980,15 @@
     e = grad * gain
     gain_acc[...] += grad * xhat
     return extra + root * (e - xhat * jnp.mean(e * xhat, axis=-1, keepdims=True))
+
+
+def tiled_in(left, right, out, size):
+    def body(j, carry):
+        at = pl.ds(pl.multiple_of(j * size, size), size)
+        out[:, at] = jnp.dot(left[...], right[:, at], preferred_element_type=F32)
+        return carry
+
+    lax.fori_loop(0, out.shape[1] // size, body, 0)
 
 
 def feed_kernel(chain, *refs):
@@ -997,12 +1012,10 @@
     reduce = PlaneReduce(pc, sems, npart, s_part, middle_grad)
     fetches[0].wait()
     fetches[1].wait()
-    for at in range(0, 2 * units, 256):
-        gu[:, at : at + 256] = jnp.dot(two[...], wgu[:, at : at + 256], preferred_element_type=F32)
+    tiled_in(two, wgu, gu, 256)
     fetches[2].wait()
     fetches[3].wait()
-    for at in range(0, units, 128):
-        h[:, at : at + 128] = jnp.dot(cotan[...], wdn[:, at : at + 128], preferred_element_type=F32)
+    tiled_in(cotan, wdn, h, 128)
 
     def gates(r):
         for at in range(0, units, 128):

time: 431 us -> 422 us (0.979); the launches traced: 424 us -> 421 us
  no operation moved by 1% of the time
where the time goes in v6:
time: 422 us; the launch traced here: 421 us
  Pallas kernels  388 us (92%)
  local copies, waits for them, and re-layouts  24.5 us (6%)
  other arithmetic  7.8 us (2%)
    pallas_call x3, Pallas kernels, call(): pl.pallas_call(kernel, out_shape=[jax.ShapeDtypeStruct(shape, kind) for s...  388 us
    unnamed x28, local copies, waits for them, and re-layouts  12 us

profile of v6, /device:TPU:0, one launch (start us, length us, event | category | flops | bytes accessed | tf_op | source)
XLA Modules:
  0.0 421.5 jit_solution(10666215813587779869)
XLA Ops:
  0.6 0.0 copy-start.2
  0.7 0.1 pad.18.clone
  0.8 0.7 tile.4
  1.5 0.1 broadcast_in_dim_tile.6
  1.6 0.7 tile.5
  2.2 0.1 broadcast_in_dim_tile.7
  2.3 0.8 multiply_add_fusion.1
  3.1 0.7 maximum_maximum_fusion.refs_1_
  3.8 0.7 multiply_add_fusion
  4.5 0.6 broadcast_in_dim.21.refs_11_
  5.1 0.9 copy.31
  6.0 0.9 copy.32
  6.8 0.8 add.70.refs_10_
  7.6 1.8 pad_maximum_fusion.refs_2_
  9.4 1.8 copy.33
  11.2 1.4 fusion
  12.6 0.0 copy-done.2
  12.6 0.3 copy.34
  12.8 0.0 copy-start.3
  12.9 0.4 copy.35
  13.2 1.0 pad_bitcast_fusion.2.refs_4_
  14.2 0.3 copy.36
  14.5 0.4 copy.37
  14.8 0.5 copy-done.4
  15.3 0.4 copy.38
  15.7 1.4 pad_bitcast_fusion
  17.0 153.3 %forward.1 = (f32[8,2048]{1,0:T(8,128)}, bf16[2048,768]{1,0:T(8,128)(2,1)}, bf16[2048,384]{1,0:T(8,128)(2,1)}, bf16[4,4,80,2048]{3,2,1,0:T(8,128)(2,1)}, f32[8,3...) custom-call(bf16[80,2048]{1,0:T(8,128)(2,1)} %refs_13_.1, ...), custom_call_target="tpu_custom_call" | custom-call | bytes 62914560 | tf_op jit(solution)/shard_map/forward/pallas_call | solution.py:702
  170.3 120.1 %feed.1 = (bf16[4,4,80,2048]{3,2,1,0:T(8,128)(2,1)}, f32[80,2048]{1,0:T(8,128)}, bf16[1,4,80,2048]{3,2,1,0:T(8,128)(2,1)}, f32[8,2048]{1,0:T(8,128)}, bf16[4,256...) custom-call(bf16[1280,2048]{1,0:T(8,128)(2,1)} %bitcast.47, bf16[1280,2048]{1,0:T(8,128)(2,1)} %bitcast.46, ...), custom_call_target="tpu_custom_call" | custom-call | bytes 62914560 | tf_op jit(solution)/shard_map/feed/pallas_call | solution.py:702
  290.4 114.9 %backward.1 = (bf16[80,2048]{1,0:T(8,128)(2,1)}, f32[80,2048]{1,0:T(8,128)}, f32[256,512]{1,0:T(8,128)}, f32[256,128]{1,0:T(8,128)}, f32[256,512]{1,0:T(8,128)}, /*index=5*/f32[8,128]{1,0:T(8,128)}) custom-call(bf16[1,4,80,2048]{3,2,1,0:T(8,128)(2,1)} %get-tuple-element.40.refs_0_, bf16[2048,640]{1,0:T(8,128)(2,1)} %get-tuple-element.41.refs_1_, ...), custom_call_target="tpu_custom_call" | custom-call | bytes 62914560 | tf_op jit(solution)/shard_map/backward/pallas_call | solution.py:702
  405.4 0.8 constant_dynamic-slice_fusion
  406.2 0.5 slice_bitcast_fusion.12
  406.7 1.1 fusion.5
  407.8 0.7 copy.41
  408.5 0.7 copy.40
  409.3 2.0 copy.42
  411.3 0.1 slice_bitcast_fusion
  411.4 0.6 concatenate.28
  412.0 0.1 convert_bitcast_fusion
  412.1 1.5 copy.43
  413.7 0.9 slice_bitcast_fusion.4
  414.6 1.5 concatenate.26
  416.1 1.2 concatenate.27
  417.3 0.6 concatenate.24
  417.9 1.2 concatenate.25
  419.1 0.7 copy.47
  419.8 0.0 copy-done.5
  419.8 0.8 copy.48
  420.7 0.8 copy.49
  (14 shorter events, 0.0 us)
Async XLA Ops:
  0.6 11.9 %copy-start.2 = (bf16[256,1408]{1,0:T(8,128)(2,1)S(1)}, bf16[256,1408]{1,0:T(8,128)(2,1)}, u32[]{:S(2)}) copy-start(bf16[256,1408]{1,0:T(8,128)(2,1)} %param.22) | copy-start | bytes 2162692
  12.8 1.3 copy-start.3
  14.2 1.1 copy-start.4
  405.4 5.9 %copy-start.1 = (bf16[4,256,384]{2,1,0:T(8,128)(2,1)S(1)}, bf16[4,256,384]{2,1,0:T(8,128)(2,1)}, u32[]{:S(2)}) copy-start(bf16[4,256,384]{2,1,0:T(8,128)(2,1)} %get-tuple-element.68) | copy-start | bytes 2359300
  412.1 1.6 copy-start
  417.3 1.8 copy-start.7
  417.9 1.9 copy-start.5
  417.9 2.8 copy-start.6

commit v7 on v6

--- a/solution.py
+++ b/solution.py
@@ -1048,9 +1048,10 @@
     go(steps, 1)
     grads_into(cotan, hidden, gdn)
     go(steps, 1)
+    gus.send(2)
+    go(steps, 1)
     gus.turn(0, 1)
-    gus.send(2, 3)
-    go(steps, 1)
+    gus.send(3)
     dns.send()
     run(steps)
     gus.turn(2, 3)

time: 422 us -> 421 us (level)
  no operation moved by 1% of the time
where the time goes in v7:
time: 421 us; the launch traced here: 420 us
  Pallas kernels  387 us (92%)
  local copies, waits for them, and re-layouts  24.5 us (6%)
  other arithmetic  7.8 us (2%)
    pallas_call x3, Pallas kernels, call(): pl.pallas_call(kernel, out_shape=[jax.ShapeDtypeStruct(shape, kind) for s...  387 us
    unnamed x28, local copies, waits for them, and re-layouts  12 us

profile of v7, /device:TPU:0, one launch (start us, length us, event | category | flops | bytes accessed | tf_op | source)
XLA Modules:
  0.0 419.9 jit_solution(14106563077109643005)
XLA Ops:
  0.6 0.0 copy-start.2
  0.7 0.1 pad.18.clone
  0.8 0.7 tile.4
  1.5 0.1 broadcast_in_dim_tile.6
  1.6 0.7 tile.5
  2.2 0.1 broadcast_in_dim_tile.7
  2.3 0.8 multiply_add_fusion.1
  3.1 0.7 maximum_maximum_fusion.refs_1_
  3.8 0.7 multiply_add_fusion
  4.5 0.6 broadcast_in_dim.21.refs_11_
  5.1 0.9 copy.31
  6.0 0.9 copy.32
  6.8 0.8 add.70.refs_10_
  7.6 1.8 pad_maximum_fusion.refs_2_
  9.4 1.8 copy.33
  11.2 1.4 fusion
  12.6 0.0 copy-done.2
  12.6 0.3 copy.34
  12.8 0.0 copy-start.3
  12.9 0.4 copy.35
  13.2 1.0 pad_bitcast_fusion.2.refs_4_
  14.2 0.3 copy.36
  14.5 0.4 copy.37
  14.8 0.5 copy-done.4
  15.3 0.4 copy.38
  15.7 1.4 pad_bitcast_fusion
  17.0 153.3 %forward.1 = (f32[8,2048]{1,0:T(8,128)}, bf16[2048,768]{1,0:T(8,128)(2,1)}, bf16[2048,384]{1,0:T(8,128)(2,1)}, bf16[4,4,80,2048]{3,2,1,0:T(8,128)(2,1)}, f32[8,3...) custom-call(bf16[80,2048]{1,0:T(8,128)(2,1)} %refs_13_.1, ...), custom_call_target="tpu_custom_call" | custom-call | bytes 62914560 | tf_op jit(solution)/shard_map/forward/pallas_call | solution.py:702
  170.3 116.6 %feed.1 = (bf16[4,4,80,2048]{3,2,1,0:T(8,128)(2,1)}, f32[80,2048]{1,0:T(8,128)}, bf16[1,4,80,2048]{3,2,1,0:T(8,128)(2,1)}, f32[8,2048]{1,0:T(8,128)}, bf16[4,256...) custom-call(bf16[1280,2048]{1,0:T(8,128)(2,1)} %bitcast.47, bf16[1280,2048]{1,0:T(8,128)(2,1)} %bitcast.46, ...), custom_call_target="tpu_custom_call" | custom-call | bytes 62914560 | tf_op jit(solution)/shard_map/feed/pallas_call | solution.py:702
  286.9 116.9 %backward.1 = (bf16[80,2048]{1,0:T(8,128)(2,1)}, f32[80,2048]{1,0:T(8,128)}, f32[256,512]{1,0:T(8,128)}, f32[256,128]{1,0:T(8,128)}, f32[256,512]{1,0:T(8,128)}, /*index=5*/f32[8,128]{1,0:T(8,128)}) custom-call(bf16[1,4,80,2048]{3,2,1,0:T(8,128)(2,1)} %get-tuple-element.40.refs_0_, bf16[2048,640]{1,0:T(8,128)(2,1)} %get-tuple-element.41.refs_1_, ...), custom_call_target="tpu_custom_call" | custom-call | bytes 62914560 | tf_op jit(solution)/shard_map/backward/pallas_call | solution.py:702
  403.8 0.8 constant_dynamic-slice_fusion
  404.6 0.5 slice_bitcast_fusion.12
  405.2 1.1 fusion.5
  406.2 0.7 copy.41
  406.9 0.7 copy.40
  407.7 2.0 copy.42
  409.7 0.1 slice_bitcast_fusion
  409.8 0.6 concatenate.28
  410.4 0.1 convert_bitcast_fusion
  410.5 1.5 copy.43
  412.1 0.9 slice_bitcast_fusion.4
  413.0 1.5 concatenate.26
  414.5 1.2 concatenate.27
  415.7 0.6 concatenate.24
  416.3 1.2 concatenate.25
  417.5 0.7 copy.47
  418.2 0.0 copy-done.5
  418.2 0.8 copy.48
  419.1 0.8 copy.49
  (14 shorter events, 0.0 us)
Async XLA Ops:
  0.6 11.9 %copy-start.2 = (bf16[256,1408]{1,0:T(8,128)(2,1)S(1)}, bf16[256,1408]{1,0:T(8,128)(2,1)}, u32[]{:S(2)}) copy-start(bf16[256,1408]{1,0:T(8,128)(2,1)} %param.22) | copy-start | bytes 2162692
  12.8 1.3 copy-start.3
  14.2 1.1 copy-start.4
  403.8 5.9 %copy-start.1 = (bf16[4,256,384]{2,1,0:T(8,128)(2,1)S(1)}, bf16[4,256,384]{2,1,0:T(8,128)(2,1)}, u32[]{:S(2)}) copy-start(bf16[4,256,384]{2,1,0:T(8,128)(2,1)} %get-tuple-element.68) | copy-start | bytes 2359300
  410.5 1.6 copy-start
  415.7 1.8 copy-start.7
  416.3 1.9 copy-start.5
  416.3 2.8 copy-start.6
